TPU v7x, 128 devices: a whole 4x4x4 slice. The times are simulated.
128 devices in a mesh: src: 4 (over z_hi, core), rcv: 32 (over y, z_lo, x).
Axes of the slice: x: 4, y: 4, z: 4 (z_hi: 2, z_lo: 2; z = z_hi * 2 + z_lo), core: 2. Of those that a mesh axis runs over, the one named last changes fastest.
Arguments:
- traces: bfloat16 [4096, 16, 2000], P('rcv', 'src')
- src_index: int32 [256], P('src'), may hold values from 0 to 4095, as said below
- quality: int32 [4096, 16], P('rcv'), may hold values 0 or 1
Outputs:
- xcorr: float32 [256, 201, 4096], P('src', None, 'rcv')
Inputs may be any that keep to these rules, and one draw needn't show every extreme that they name: `src_index`: the source numbered j within each group of 64 sources lies in receiver block j mod 32, among channels (j mod 32) * 128 up to that plus 128 - 1.
All inputs are finite; a program needn't handle non-finite values. No bound on the sum of `quality` on one device may be relied on, other than what follows from the above.
Results may differ from a plain program's by a relative error of at most 0.0067.
Values may be sent and summed in bfloat16 or wider, within the bound.
No kernel may reach another device: no remote copies, remote signals or barrier semaphores. Data moves between devices by JAX's collectives and lax.ppermute only.
A program may use at most 576 MiB of HBM per device.

v0:
```python
import math

import jax
import jax.numpy as jnp
from jax import lax
from jax.sharding import PartitionSpec as P

LAGH = 100


def make_tables(length):
    half = length // 2
    bins = jnp.arange(1, half + 1, dtype=jnp.int32)
    times = jnp.arange(length, dtype=jnp.int32)
    phase = (times[:, None] * bins[None, :] % length).astype(jnp.float32) * (2.0 * math.pi / length)
    forward = jnp.concatenate([jnp.cos(phase), -jnp.sin(phase)], axis=1).astype(jnp.bfloat16)
    lagvals = jnp.arange(-LAGH, LAGH + 1, dtype=jnp.int32)
    phase_lag = (bins[:, None] * lagvals[None, :] % length).astype(jnp.float32) * (
        2.0 * math.pi / length
    )
    weights = jnp.where(bins == half, 1.0, 2.0).astype(jnp.float32)[:, None] / jnp.sqrt(
        jnp.float32(half)
    )
    inverse = jnp.concatenate(
        [weights * jnp.cos(phase_lag), -weights * jnp.sin(phase_lag)], axis=0
    ).astype(jnp.bfloat16)
    return (forward, inverse)


def whiten(samples, forward):
    length = samples.shape[2]
    half = length // 2
    spec = jnp.dot(samples.reshape(-1, length), forward, preferred_element_type=jnp.float32)
    real_part = spec[:, :half]
    imag_part = spec[:, half:]
    power = real_part * real_part + imag_part * imag_part
    level = 0.5 * jnp.sqrt(jnp.mean(power, axis=1, keepdims=True) + 1e-06)
    denom = jnp.maximum(jnp.sqrt(power), level)
    white = jnp.concatenate([real_part / denom, imag_part / denom], axis=1).astype(jnp.bfloat16)
    return white.reshape(samples.shape[0], samples.shape[1], length)


def on_device(traces, src_index, quality):
    rows, seg_local, length = traces.shape
    half = length // 2
    nsrc = src_index.shape[0]
    seg_all = quality.shape[1]
    forward, inverse = make_tables(length)
    white_local = whiten(traces, forward)
    white_all = lax.all_gather(white_local, "src", axis=1, tiled=True)
    qual = quality.astype(jnp.bfloat16)
    first_channel = lax.axis_index("rcv") * rows
    onehot = (
        src_index[:, None] == first_channel + jnp.arange(rows, dtype=jnp.int32)[None, :]
    ).astype(jnp.bfloat16)
    found = jnp.dot(onehot, white_all.reshape(rows, -1), preferred_element_type=jnp.float32)
    flags = jnp.dot(onehot, qual, preferred_element_type=jnp.float32)
    found, flags = (
        lax.psum(found.astype(jnp.bfloat16), "rcv").astype(jnp.float32),
        lax.psum(flags.astype(jnp.bfloat16), "rcv").astype(jnp.float32),
    )
    srcw = found.reshape(nsrc, seg_all, length).astype(jnp.bfloat16)
    msrc = flags.astype(jnp.bfloat16)
    count = jnp.dot(msrc, qual.T, preferred_element_type=jnp.float32)
    recv = white_all * qual[:, :, None]
    recv_re = recv[:, :, :half]
    recv_im = recv[:, :, half:]
    left_all = srcw * msrc[:, :, None]
    group = 8
    left_blocks = left_all.reshape(nsrc // group, group, seg_all, length)

    def one_block(left):
        left_re = left[:, :, :half]
        left_im = left[:, :, half:]
        pre = jnp.einsum("isk,jsk->ijk", left_re, recv_re, preferred_element_type=jnp.float32)
        pre = pre + jnp.einsum("isk,jsk->ijk", left_im, recv_im, preferred_element_type=jnp.float32)
        pim = jnp.einsum("isk,jsk->ijk", left_im, recv_re, preferred_element_type=jnp.float32)
        pim = pim - jnp.einsum("isk,jsk->ijk", left_re, recv_im, preferred_element_type=jnp.float32)
        cross = jnp.concatenate([pre, pim], axis=2).astype(jnp.bfloat16)
        return jnp.einsum("ijk,kt->itj", cross, inverse, preferred_element_type=jnp.float32)

    lagged = lax.map(one_block, left_blocks)
    lagged = lagged.reshape(nsrc, 2 * LAGH + 1, rows)
    return lagged / jnp.maximum(count, 1.0)[:, None, :]


def solution(mesh):
    return jax.shard_map(
        on_device,
        mesh=mesh,
        in_specs=(P("rcv", "src", None), P("src"), P("rcv", None)),
        out_specs=P("src", None, "rcv"),
        check_vma=False,
    )
```

profile of v0, /device:TPU:1, one launch (start us, length us, event | category | flops | bytes accessed | tf_op | source)
XLA Modules:
  0.0 1214.9 jit_solution(14916867752042446205)
XLA Ops:
  6.5 35.3 %cosine_convert_fusion = (bf16[2000,1000]{1,0:T(8,128)(2,1)}, bf16[2000,1000]{1,0:T(8,128)(2,1)}) fusion(s32[1000]{0:T(1024)S(1)} %iota_add_fusion), kind=kLoop, calls=%fused_computation.36 | loop fusion | flops 24000000 | bytes 8004000 | tf_op jit(solution)/shard_map/convert.10
  41.9 3.4 copy.17
  47.6 10.1 fusion.37
  62.0 2.8 pad_maximum_fusion.1
  64.8 3.0 copy.20
  67.9 65.1 %all-gather.2.cloned.1.call-done = bf16[128,16,2000]{0,2,1:T(8,128)(2,1)} async-done(((bf16[128,4,2000]{0,2,1:T(8,128)(2,1)}), bf16[128,16,2000]{0,2,1:T(8,128)(2,1)}) %all-gather.2.cloned.1.call-update) | async-done | bytes 8192016 | tf_op jit(solution)/shard_map/all_gather | solution.py:50
  133.0 8.3 convolution_convert_fusion
  141.2 9.6 convert_element_type.35
  150.9 31.0 %copy.21 = bf16[8,8,16,2000]{2,1,3,0:T(8,128)(2,1)} copy(bf16[8,8,16,2000]{3,2,1,0:T(8,128)(2,1)} %convert_element_type.35) | data formatting | bytes 8192000 | tf_op jit(solution)/shard_map/convert_element_type | solution.py:62
  182.8 76.6 %psum.15 = bf16[64,16]{0,1:T(8,128)(2,1)S(1)} all-reduce(bf16[64,16]{0,1:T(8,128)(2,1)S(1)} %convolution_convert_fusion.1), channel_id=1, replica_groups=mesh['src'=4,'rcv'=32] {'rcv'}, use_global_device_ids=true, to_apply=%region_2.3 | all-reduce | flops 1024 | bytes 4096 | tf_op jit(solution)/shard_map/psum | solution.py:60
  260.3 3.7 multiply_convert_fusion.1
  265.2 7.3 broadcast_multiply_fusion.1
  272.5 3.8 fusion.54
  276.3 2.5 copy.23
  281.3 611.0 %all-reduce.2.cloned.1.call-done = bf16[8,8,16,2000]{2,1,3,0:T(8,128)(2,1)} async-done(((bf16[8,8,16,2000]{2,1,3,0:T(8,128)(2,1)}), bf16[8,8,16,2000]{2,1,3,0:T(8,128)(2,1)}) %all-reduce.2.cloned.1.call-update) | async-done | bytes 4096016 | tf_op jit(solution)/shard_map/psum | solution.py:59
  892.3 22.5 %broadcast_multiply_fusion = bf16[8,8,16,2000]{2,1,3,0:T(8,128)(2,1)} fusion(bf16[8,8,16,2000]{2,1,3,0:T(8,128)(2,1)} %all-reduce.2.cloned.1.call-done, bf16[8,8,16]{2,1,0:T(8,128)(2,1)S(1)} %bitcast.91), kind=kLoop, calls=%fused_computation.27 | loop fusion | flops 2048000 | bytes 8194048 | tf_op jit(solution)/shard_map/mul | solution.py:68
  914.8 285.8 %while.10 = (s32[]{:T(128)}, f32[8,8,201,128]{3,1,0,2:T(8,128)}, bf16[8,8,16,2000]{2,1,3,0:T(8,128)(2,1)}, bf16[128,16,1000]{0,1,2:T(8,128)(2,1)}, bf16[128,16,1...) while((s32[]{:T(128)}, f32[8,8,201,128]{3,1,0,2:T(8,128)}, ...), condition=%wide.region_4.5_spmd, body=%wide.region_3.4_spmd.sunk | while | flops 960512000 | bytes 119130632 | solution.py:82
  915.0 2.5 fusion.110
  919.6 2.5 fusion.112
  923.0 2.5 fusion.113
  929.2 2.5 fusion.116
  934.2 14.2 %pad_maximum_fusion.4 = bf16[8,128,2000]{1,0,2:T(8,128)(2,1)S(1)} fusion(bf16[8,128,1000]{1,0,2:T(8,128)(2,1)S(1)} %copy-done, bf16[8,128,1000]{1,0,2:T(8,128)(2,1)S(1)} %fusion.117), kind=kLoop, calls=%fused_computation.clone.1 | loop fusion | flops 2048000 | bytes 8192000 | tf_op jit(solution)/shard_map/while/body/eval_jaxpr/concatenate | solution.py:79
  955.3 2.5 fusion.112
  958.7 2.5 fusion.113
  964.9 2.5 fusion.116
  969.9 14.2 %pad_maximum_fusion.4 = bf16[8,128,2000]{1,0,2:T(8,128)(2,1)S(1)} fusion(bf16[8,128,1000]{1,0,2:T(8,128)(2,1)S(1)} %copy-done, bf16[8,128,1000]{1,0,2:T(8,128)(2,1)S(1)} %fusion.117), kind=kLoop, calls=%fused_computation.clone.1 | loop fusion | flops 2048000 | bytes 8192000 | tf_op jit(solution)/shard_map/while/body/eval_jaxpr/concatenate | solution.py:79
  991.0 2.5 fusion.112
  994.4 2.5 fusion.113
  1000.6 2.5 fusion.116
  1005.5 14.2 %pad_maximum_fusion.4 = bf16[8,128,2000]{1,0,2:T(8,128)(2,1)S(1)} fusion(bf16[8,128,1000]{1,0,2:T(8,128)(2,1)S(1)} %copy-done, bf16[8,128,1000]{1,0,2:T(8,128)(2,1)S(1)} %fusion.117), kind=kLoop, calls=%fused_computation.clone.1 | loop fusion | flops 2048000 | bytes 8192000 | tf_op jit(solution)/shard_map/while/body/eval_jaxpr/concatenate | solution.py:79
  1026.7 2.5 fusion.112
  1030.1 2.5 fusion.113
  1036.3 2.5 fusion.116
  1041.3 14.2 %pad_maximum_fusion.4 = bf16[8,128,2000]{1,0,2:T(8,128)(2,1)S(1)} fusion(bf16[8,128,1000]{1,0,2:T(8,128)(2,1)S(1)} %copy-done, bf16[8,128,1000]{1,0,2:T(8,128)(2,1)S(1)} %fusion.117), kind=kLoop, calls=%fused_computation.clone.1 | loop fusion | flops 2048000 | bytes 8192000 | tf_op jit(solution)/shard_map/while/body/eval_jaxpr/concatenate | solution.py:79
  1062.4 2.5 fusion.112
  1065.8 2.5 fusion.113
  1072.0 2.5 fusion.116
  1077.0 14.2 %pad_maximum_fusion.4 = bf16[8,128,2000]{1,0,2:T(8,128)(2,1)S(1)} fusion(bf16[8,128,1000]{1,0,2:T(8,128)(2,1)S(1)} %copy-done, bf16[8,128,1000]{1,0,2:T(8,128)(2,1)S(1)} %fusion.117), kind=kLoop, calls=%fused_computation.clone.1 | loop fusion | flops 2048000 | bytes 8192000 | tf_op jit(solution)/shard_map/while/body/eval_jaxpr/concatenate | solution.py:79
  1098.1 2.5 fusion.112
  1101.5 2.5 fusion.113
  1107.7 2.5 fusion.116
  1112.7 14.2 %pad_maximum_fusion.4 = bf16[8,128,2000]{1,0,2:T(8,128)(2,1)S(1)} fusion(bf16[8,128,1000]{1,0,2:T(8,128)(2,1)S(1)} %copy-done, bf16[8,128,1000]{1,0,2:T(8,128)(2,1)S(1)} %fusion.117), kind=kLoop, calls=%fused_computation.clone.1 | loop fusion | flops 2048000 | bytes 8192000 | tf_op jit(solution)/shard_map/while/body/eval_jaxpr/concatenate | solution.py:79
  1137.2 2.5 fusion.113
  1143.4 2.5 fusion.116
  1148.4 14.2 %pad_maximum_fusion.4 = bf16[8,128,2000]{1,0,2:T(8,128)(2,1)S(1)} fusion(bf16[8,128,1000]{1,0,2:T(8,128)(2,1)S(1)} %copy-done, bf16[8,128,1000]{1,0,2:T(8,128)(2,1)S(1)} %fusion.117), kind=kLoop, calls=%fused_computation.clone.1 | loop fusion | flops 2048000 | bytes 8192000 | tf_op jit(solution)/shard_map/while/body/eval_jaxpr/concatenate | solution.py:79
  1172.9 2.5 fusion.113
  1184.0 14.2 %pad_maximum_fusion.4 = bf16[8,128,2000]{1,0,2:T(8,128)(2,1)S(1)} fusion(bf16[8,128,1000]{1,0,2:T(8,128)(2,1)S(1)} %copy-done, bf16[8,128,1000]{1,0,2:T(8,128)(2,1)S(1)} %fusion.117), kind=kLoop, calls=%fused_computation.clone.1 | loop fusion | flops 2048000 | bytes 8192000 | tf_op jit(solution)/shard_map/while/body/eval_jaxpr/concatenate | solution.py:79
  1200.6 7.2 bitcast_divide_fusion
  (167 shorter events, 127.4 us)
Async XLA Ops:
  6.5 126.4 %all-gather.2.cloned.1.call-start = ((), (), s32[]{:S(2)}) async-start(), calls=%async_computation | async-start | bytes 10240000 | tf_op jit(solution)/shard_map/all_gather | solution.py:50
  64.8 68.2 %copy-start.7 = (s32[64]{0:T(128)S(1)}, s32[64]{0:T(128)}, u32[]{:S(2)}) copy-start(s32[64]{0:T(128)} %param.6) | copy-start | bytes 772
  67.8 824.5 %all-reduce.2.cloned.1.call-start = ((), (), s32[]{:S(2)}) async-start(), calls=%async_computation.1 | async-start | bytes 65536000 | tf_op jit(solution)/shard_map/psum | solution.py:59
  181.9 0.7 copy-start.6
  914.8 285.8 %copy-start.5 = (f32[64,128]{1,0:T(8,128)S(1)}, f32[64,128]{1,0:T(8,128)}, u32[]{:S(2)}) copy-start(f32[64,128]{1,0:T(8,128)} %convolution_maximum_fusion) | copy-start | bytes 98308
  915.0 3.4 copy-start.1
  919.6 3.4 copy-start.3
  929.2 3.4 copy-start.2
  932.6 1.6 copy-start
  934.2 14.3 %copy-start.4 = (bf16[2000,201]{0,1:T(8,128)(2,1)S(1)}, bf16[2000,201]{0,1:T(8,128)(2,1)}, u32[]{:S(2)}) copy-start(bf16[2000,201]{0,1:T(8,128)(2,1)} %get-tuple-element.122) | copy-start | bytes 2412004 | tf_op jit(solution)/shard_map/while
  950.7 3.4 copy-start.1
  955.3 3.4 copy-start.3
  964.9 3.4 copy-start.2
  968.3 1.6 copy-start
  969.9 14.3 %copy-start.4 = (bf16[2000,201]{0,1:T(8,128)(2,1)S(1)}, bf16[2000,201]{0,1:T(8,128)(2,1)}, u32[]{:S(2)}) copy-start(bf16[2000,201]{0,1:T(8,128)(2,1)} %get-tuple-element.122) | copy-start | bytes 2412004 | tf_op jit(solution)/shard_map/while
  986.4 3.4 copy-start.1
  991.0 3.4 copy-start.3
  1000.6 3.4 copy-start.2
  1004.0 1.6 copy-start
  1005.5 14.3 %copy-start.4 = (bf16[2000,201]{0,1:T(8,128)(2,1)S(1)}, bf16[2000,201]{0,1:T(8,128)(2,1)}, u32[]{:S(2)}) copy-start(bf16[2000,201]{0,1:T(8,128)(2,1)} %get-tuple-element.122) | copy-start | bytes 2412004 | tf_op jit(solution)/shard_map/while
  1022.1 3.4 copy-start.1
  1026.7 3.4 copy-start.3
  1036.3 3.4 copy-start.2
  1039.7 1.6 copy-start
  1041.3 14.3 %copy-start.4 = (bf16[2000,201]{0,1:T(8,128)(2,1)S(1)}, bf16[2000,201]{0,1:T(8,128)(2,1)}, u32[]{:S(2)}) copy-start(bf16[2000,201]{0,1:T(8,128)(2,1)} %get-tuple-element.122) | copy-start | bytes 2412004 | tf_op jit(solution)/shard_map/while
  1057.8 3.4 copy-start.1
  1062.4 3.4 copy-start.3
  1072.0 3.4 copy-start.2
  1075.4 1.6 copy-start
  1077.0 14.3 %copy-start.4 = (bf16[2000,201]{0,1:T(8,128)(2,1)S(1)}, bf16[2000,201]{0,1:T(8,128)(2,1)}, u32[]{:S(2)}) copy-start(bf16[2000,201]{0,1:T(8,128)(2,1)} %get-tuple-element.122) | copy-start | bytes 2412004 | tf_op jit(solution)/shard_map/while
  1093.5 3.4 copy-start.1
  1098.1 3.4 copy-start.3
  1107.7 3.4 copy-start.2
  1111.1 1.6 copy-start
  1112.7 14.3 %copy-start.4 = (bf16[2000,201]{0,1:T(8,128)(2,1)S(1)}, bf16[2000,201]{0,1:T(8,128)(2,1)}, u32[]{:S(2)}) copy-start(bf16[2000,201]{0,1:T(8,128)(2,1)} %get-tuple-element.122) | copy-start | bytes 2412004 | tf_op jit(solution)/shard_map/while
  1129.2 3.4 copy-start.1
  1133.8 3.4 copy-start.3
  1143.4 3.4 copy-start.2
  1146.8 1.6 copy-start
  1148.4 14.3 %copy-start.4 = (bf16[2000,201]{0,1:T(8,128)(2,1)S(1)}, bf16[2000,201]{0,1:T(8,128)(2,1)}, u32[]{:S(2)}) copy-start(bf16[2000,201]{0,1:T(8,128)(2,1)} %get-tuple-element.122) | copy-start | bytes 2412004 | tf_op jit(solution)/shard_map/while
  1164.9 3.4 copy-start.1
  1169.5 3.4 copy-start.3
  1179.1 3.4 copy-start.2
  1182.5 1.6 copy-start
  1184.0 14.3 %copy-start.4 = (bf16[2000,201]{0,1:T(8,128)(2,1)S(1)}, bf16[2000,201]{0,1:T(8,128)(2,1)}, u32[]{:S(2)}) copy-start(bf16[2000,201]{0,1:T(8,128)(2,1)} %get-tuple-element.122) | copy-start | bytes 2412004 | tf_op jit(solution)/shard_map/while
Sparse Core Ops, SparseCore 0:
  67.9 64.9 all-gather.1
  182.0 710.2 all-reduce.1
where the time goes:
time: 1220 us; the launch traced here: 1210 us
  waiting for transfers between devices  676 us (55%)
  other arithmetic  195 us (16%)
  local copies, waits for them, and re-layouts  174 us (14%)
  matrix products  77.6 us (6%)
  blocking collectives  76.6 us (6%)
  between operations  13.9 us (1%)
    psum x1, waiting for transfers between devices, on_device(): lax.psum(found.astype(jnp.bfloat16), 'rcv').astype(jnp.float32)  611 us
    concatenate x8, other arithmetic, one_block(): cross = jnp.concatenate([pre, pim], axis=2).astype(jnp.bfloat16)  114 us
    psum x1, blocking collectives, on_device(): lax.psum(flags.astype(jnp.bfloat16), 'rcv').astype(jnp.float32)  76.6 us
    all_gather x1, waiting for transfers between devices, on_device(): white_all = lax.all_gather(white_local, 'src', axis=1, tiled=True)  65.1 us
    convert_element_type x2, local copies, waits for them, and re-layouts, on_device(): srcw = found.reshape(nsrc, seg_all, length).astype(jnp.bfloat16)  40.6 us
    another operation x3, other arithmetic  40 us
  transfers between devices with their start and end apart: 2, of which 2 were waited for; matrix products, arithmetic and copies ran while one was open for 2% of the time, Pallas kernels for 0%

commit v1 on v0

v1 whole, which is shorter than its diff:
```python
import functools
import math

import jax
import jax.numpy as jnp
import ml_dtypes
import numpy as np
from jax import lax
from jax.experimental import pallas as pl
from jax.experimental.pallas import tpu as pltpu
from jax.sharding import Mesh, PartitionSpec as P

LAGH = 100
NLAG = 2 * LAGH + 1
TAU = 208
GRP = 8
KPAD = 1024
NGRP = KPAD // GRP
SDEV = 4
ROWS = 64
MB = 1 << 20


def start_tables(length):
    bins = np.arange(1, GRP + 1, dtype=np.float64)
    times = np.arange(length, dtype=np.float64)
    phase = 2.0 * math.pi / length * ((bins[:, None] * times[None, :]) % length)
    step = 2.0 * math.pi / length * ((GRP * times) % length)
    step = np.broadcast_to(step[None, :], phase.shape)
    return np.stack([np.cos(phase), -np.sin(phase), np.cos(step), np.sin(step)]).astype(np.float32)


def lag_table(half):
    bins = np.arange(1, half + 1, dtype=np.int64)
    lags = np.arange(-LAGH, LAGH + 1, dtype=np.int64)
    phase = 2.0 * math.pi / (2 * half) * ((lags[:, None] * bins[None, :]) % (2 * half))
    weight = np.where(bins == half, 1.0, 2.0)[None, :] / math.sqrt(half)
    out = np.zeros((TAU, 2, KPAD), np.float32)
    out[:NLAG, 0, :half] = weight * np.cos(phase)
    out[:NLAG, 1, :half] = -weight * np.sin(phase)
    return out.astype(ml_dtypes.bfloat16)


DBLK = 25


def spectra_kernel(half, x_ref, start_ref, qual_ref, y_ref, state, table, spec, power):
    ngrp = half // GRP
    state[0] = start_ref[0]
    state[1] = start_ref[1]
    power[...] = jnp.zeros_like(power)
    x01 = [x_ref[g] for g in range(4)]
    samples = jnp.concatenate(x01, axis=1)

    def gen(n, _):
        cos, sin = state[0], state[1]
        table[pl.ds(pl.multiple_of(n * 16, 16), 16), :] = jnp.concatenate([cos, sin], axis=0).astype(jnp.bfloat16)
        rc, rs = start_ref[2], start_ref[3]
        state[0] = cos * rc + sin * rs
        state[1] = sin * rc - cos * rs
        return 0

    def block(b, _):
        lax.fori_loop(0, DBLK, gen, 0)
        prod = jnp.dot(table[...], samples, preferred_element_type=jnp.float32)
        spec[pl.ds(pl.multiple_of(b * (DBLK * 16), DBLK * 16), DBLK * 16), :] = prod
        sq = prod * prod
        power[...] += jnp.sum(sq.reshape(DBLK * 2, 8, 512), axis=0)
        return 0

    lax.fori_loop(0, ngrp // DBLK, block, 0)
    mean = jnp.sum(power[...], axis=0, keepdims=True) * (1.0 / half)
    level2 = 0.25 * (mean + 1e-06)

    def white(n, _):
        base = pl.multiple_of(n * 16, 16)
        real = spec[pl.ds(base, 8), :]
        imag = spec[pl.ds(base + 8, 8), :]
        inv = lax.rsqrt(jnp.maximum(real * real + imag * imag, level2)) * qual_ref[...]
        parts = []
        for value in (real * inv, imag * inv):
            for g in range(4):
                parts.append(value[:, g * 128 : (g + 1) * 128])
        y_ref[pl.ds(pl.multiple_of(n * ROWS, ROWS), ROWS), :] = jnp.concatenate(parts, axis=0).astype(jnp.bfloat16)
        return 0

    lax.fori_loop(0, ngrp, white, 0)
    y_ref[pl.ds(ngrp * ROWS, (NGRP - ngrp) * ROWS), :] = jnp.zeros(((NGRP - ngrp) * ROWS, 128), jnp.bfloat16)


def spectra(samples, qual):
    length = samples.shape[1]
    half = length // 2
    start = jnp.asarray(start_tables(length))
    return pl.pallas_call(
        functools.partial(spectra_kernel, half),
        out_shape=jax.ShapeDtypeStruct((NGRP * ROWS, 128), jnp.bfloat16),
        scratch_shapes=[
            pltpu.VMEM((2, 8, length), jnp.float32),
            pltpu.VMEM((DBLK * 16, length), jnp.bfloat16),
            pltpu.VMEM((2 * half, 512), jnp.float32),
            pltpu.VMEM((8, 512), jnp.float32),
        ],
        compiler_params=pltpu.CompilerParams(vmem_limit_bytes=48 * MB),
        name="spectra",
    )(samples, start, qual)


CHUNKS = 4
CGRP = NGRP // CHUNKS
CK = KPAD // CHUNKS


def correlate_kernel(y_ref, x_ref, lag_ref, msrc_ref, qual_ref, out_ref, xrow, cross, acc):
    step = pl.program_id(0)
    rowid = lax.broadcasted_iota(jnp.int32, (16, 256), 0) % GRP
    lane = lax.broadcasted_iota(jnp.int32, (16, 256), 1) % GRP
    keep = rowid == lane
    zero = jnp.zeros((16, 256), jnp.bfloat16)

    def pair(n, _):
        halves = []
        for s in range(SDEV):
            halves.append(x_ref[:, s, pl.ds(pl.multiple_of(n * 128, 128), 128)].astype(jnp.float32))
        low = lax.broadcasted_iota(jnp.int32, (64, 128), 1) < 64
        prods = []
        for a in range(2):
            cols = []
            for q in range(2):
                left, right = halves[2 * q], halves[2 * q + 1]
                if a == 0:
                    cols.append(jnp.where(low, left, pltpu.roll(right, 64, 1)))
                else:
                    cols.append(jnp.where(low, pltpu.roll(left, 64, 1), right))
            xrow[a] = jnp.concatenate(cols, axis=1)
            tiles = []
            for i in range(0, 64, 2):
                two = jnp.concatenate(
                    [xrow[a, pl.ds(i, 8, stride=0), :], xrow[a, pl.ds(i + 1, 8, stride=0), :]], axis=0
                ).astype(jnp.bfloat16)
                tiles.append(jnp.where(keep, two, zero))
            lhs = jnp.concatenate(tiles, axis=0)
            base = pl.multiple_of((2 * n + a) * ROWS, ROWS)
            reim, imre = [], []
            for s in range(SDEV):
                yr = y_ref[s, pl.ds(base, 32), :]
                yi = y_ref[s, pl.ds(base + 32, 32), :]
                reim += [yr, yi]
                imre += [-yi, yr]
            right = jnp.concatenate(
                [jnp.concatenate(reim, axis=0), jnp.concatenate(imre, axis=0)], axis=1
            )
            prods.append(jnp.dot(lhs, right, preferred_element_type=jnp.float32))
        off = pl.multiple_of(n * 16, 16)
        for i in range(64):
            both = jnp.concatenate([prods[0][8 * i : 8 * i + 8], prods[1][8 * i : 8 * i + 8]], axis=0).astype(
                jnp.bfloat16
            )
            cross[i, pl.ds(off, 16), :] = both[:, :128]
            cross[i, pl.ds(pl.multiple_of(CK + off, 16), 16), :] = both[:, 128:]
        return 0

    lax.fori_loop(0, CGRP // 2, pair, 0)

    @pl.when(step == 0)
    def _():
        acc[...] = jnp.zeros_like(acc)

    table = lag_ref[0]

    def lags(n, _):
        right = jnp.concatenate([cross[2 * n], cross[2 * n + 1]], axis=1)
        prod = jnp.dot(table, right, preferred_element_type=jnp.float32)
        acc[2 * n] += prod[:, :128]
        acc[2 * n + 1] += prod[:, 128:]
        return 0

    lax.fori_loop(0, 32, lags, 0)

    @pl.when(step == CHUNKS - 1)
    def _():
        count = jnp.dot(msrc_ref[...], qual_ref[...], preferred_element_type=jnp.float32)
        xrow[0, :, :128] = 1.0 / jnp.maximum(count, 1.0)

        def source(p):
            return (p % 2) * 32 + (p // 16) * 8 + (p // 2) % 2 * 4 + (p // 4) % 4

        def finish(t, _):
            for p in range(64):
                scale = xrow[0, pl.ds(p, 8, stride=0), :128]
                lagged = acc[p, pl.ds(pl.multiple_of(t * 8, 8), 8), :]
                out_ref[pl.ds(t * 512 + source(p), 8, stride=64), :] = lagged * scale
            return 0

        lax.fori_loop(0, NLAG // 8, finish, 0)
        for p in range(64):
            out_ref[pl.ds((NLAG - 1) * 64 + source(p), 1), :] = (
                acc[p, NLAG - 1 : NLAG, :] * xrow[0, p : p + 1, :128]
            )


def correlate(y_all, x_all, msrc, qual_t):
    table = lag_table(1000)
    table = table.reshape(TAU, 2, CHUNKS, CK).transpose(2, 0, 1, 3).reshape(CHUNKS, TAU, 2 * CK)
    return pl.pallas_call(
        correlate_kernel,
        grid=(CHUNKS,),
        out_shape=jax.ShapeDtypeStruct((NLAG * 64, 128), jnp.float32),
        in_specs=[
            pl.BlockSpec((SDEV, CGRP * ROWS, 128), lambda c: (0, c, 0)),
            pl.BlockSpec((64, SDEV, CGRP * ROWS), lambda c: (0, 0, c)),
            pl.BlockSpec((1, TAU, 2 * CK), lambda c: (c, 0, 0)),
            pl.BlockSpec((64, 16), lambda c: (0, 0)),
            pl.BlockSpec((16, 128), lambda c: (0, 0)),
        ],
        out_specs=pl.BlockSpec((NLAG * 64, 128), lambda c: (0, 0)),
        scratch_shapes=[
            pltpu.VMEM((2, 64, 256), jnp.float32),
            pltpu.VMEM((64, 2 * CK, 128), jnp.bfloat16),
            pltpu.VMEM((64, TAU, 128), jnp.float32),
        ],
        compiler_params=pltpu.CompilerParams(vmem_limit_bytes=60 * MB),
        name="correlate",
    )(y_all, x_all, jnp.asarray(table), msrc, qual_t)


def on_device(traces, src_index, quality):
    rows = traces.shape[0]
    samples = jnp.transpose(traces, (1, 2, 0))
    qual_t = jnp.transpose(quality, (1, 0))
    me = lax.axis_index(("zhi", "core"))
    first = lax.axis_index(("y", "zlo", "x")) * rows
    r = lax.axis_index(("y", "zlo", "x"))
    qual_f = qual_t.astype(jnp.float32)
    qual_own = lax.dynamic_slice_in_dim(qual_f, me * 4, 4, axis=0).reshape(1, 512)
    y = spectra(samples, qual_own)
    index_all = lax.all_gather(src_index, ("zhi", "core"), axis=0, tiled=False)
    mine = index_all.reshape(4, 2, 32)
    mine = lax.dynamic_slice_in_dim(mine, r, 1, axis=2).reshape(8)
    onehot = (mine[:, None] == first + jnp.arange(rows, dtype=jnp.int32)[None, :]).astype(jnp.bfloat16)
    sel = lax.dot_general(onehot, y, (((1,), (1,)), ((), ())), preferred_element_type=jnp.float32)
    sel = sel.astype(jnp.bfloat16).reshape(4, 2, NGRP * ROWS)
    got = lax.all_to_all(sel, ("zhi", "core"), 0, 0, tiled=False)
    own = lax.dynamic_slice_in_dim(onehot, me * 2, 2, axis=0)
    msel = jnp.dot(own, qual_f.astype(jnp.bfloat16).T, preferred_element_type=jnp.float32).astype(jnp.bfloat16)
    payload = jnp.concatenate(
        [jnp.transpose(got, (1, 0, 2)).reshape(2, -1), jnp.pad(msel, ((0, 0), (0, 112)))], axis=1
    )
    payload = lax.all_gather(payload, "zlo", axis=0, tiled=True)
    payload = lax.all_gather(payload, ("y", "x"), axis=0, tiled=True)
    x_all = payload[:, : 4 * NGRP * ROWS].reshape(64, 4, NGRP * ROWS)
    msrc = payload[:, 4 * NGRP * ROWS : 4 * NGRP * ROWS + 16]
    y_all = lax.all_gather(y, ("zhi", "core"), axis=0, tiled=False)
    out = correlate(y_all, x_all, msrc, qual_f.astype(jnp.bfloat16))
    return jnp.transpose(out.reshape(NLAG, 64, 128), (1, 0, 2))


def solution(mesh):
    fine = Mesh(mesh.devices.reshape(2, 2, 4, 2, 4), ("zhi", "core", "y", "zlo", "x"))
    rcv = ("y", "zlo", "x")
    src = ("zhi", "core")
    return jax.shard_map(
        on_device,
        mesh=fine,
        in_specs=(P(rcv, src, None), P(src), P(rcv, None)),
        out_specs=P(src, None, rcv),
        check_vma=False,
    )
```

time: 1220 us -> 240 us (0.20)
  waiting for transfers between devices: 676 us -> 101 us
  other arithmetic: 195 us -> 1.5 us
  local copies, waits for them, and re-layouts: 174 us -> 28.1 us
  Pallas kernels: 0 us -> 75.9 us
  matrix products: 77.6 us -> 2.38 us
  blocking collectives: 76.6 us -> 11.9 us
    psum x1 -> x0, waiting for transfers between devices: 611 us -> none  [on_device(): lax.psum(found.astype(jnp.bfloat16), 'rcv').astype(jnp.float32)]
    concatenate x10 -> x0, other arithmetic: 118 us -> none  [the longest x8 114 us: one_block(): cross = jnp.concatenate([pre, pim], axis=2).astype(jnp.bfloat16)]
    dot_general x32 -> x0, local copies, waits for them, and re-layouts: 78.7 us -> none  [the longest x8 20 us: one_block(): jnp.einsum('isk,jsk->ijk', left_re, recv_im, preferred_element_type=jnp.f...]
    psum x1 -> x0, blocking collectives: 76.6 us -> none  [on_device(): lax.psum(flags.astype(jnp.bfloat16), 'rcv').astype(jnp.float32)]
    pallas_call x0 -> x2, Pallas kernels: none -> 75.9 us  [the longest x1 63.9 us: correlate(): pl.pallas_call(correlate_kernel, grid=(CHUNKS,), out_shape=jax.ShapeDtype...]
    dot_general x44 -> x2, matrix products: 77.6 us -> 2.38 us  [the longest x1 2.26 us: on_device(): lax.dot_general(onehot, y, (((1,), (1,)), ((), ())), preferred_element_ty...]
    convert_element_type x2 -> x0, local copies, waits for them, and re-layouts: 40.6 us -> none  [on_device(): srcw = found.reshape(nsrc, seg_all, length).astype(jnp.bfloat16)]
    another operation x3 -> x0, other arithmetic: 40 us -> none
  transfers between devices with their start and end apart: 2 -> 3, of which waited for: 2 -> 3; matrix products, arithmetic and copies ran while one was open for 2% -> 9% of each run, Pallas kernels for 0% -> 0%
where the time goes in v1:
time: 240 us
  waiting for transfers between devices  101 us (42%)
  Pallas kernels  75.9 us (32%)
  local copies, waits for them, and re-layouts  28.1 us (12%)
  between operations  14.1 us (6%)
  blocking collectives  11.9 us (5%)
  starting transfers between devices  5.03 us (2%)
    pallas_call x1, Pallas kernels, correlate(): pl.pallas_call(correlate_kernel, grid=(CHUNKS,), out_shape=jax.ShapeDtype...  63.9 us
    all_gather x1, waiting for transfers between devices, on_device(): payload = lax.all_gather(payload, ('y', 'x'), axis=0, tiled=True)  51.8 us
    all_gather x1, waiting for transfers between devices, on_device(): y_all = lax.all_gather(y, ('zhi', 'core'), axis=0, tiled=False)  43.2 us
    unnamed x11, local copies, waits for them, and re-layouts  12.8 us
    pallas_call x1, Pallas kernels, spectra(): pl.pallas_call(functools.partial(spectra_kernel, half), out_shape=jax.Sha...  12 us
    reshape x1, local copies, waits for them, and re-layouts, on_device(): x_all = payload[:, :4 * NGRP * ROWS].reshape(64, 4, NGRP * ROWS)  8.13 us
    unnamed x1, blocking collectives  7.44 us
    all_to_all x1, starting transfers between devices, on_device(): got = lax.all_to_all(sel, ('zhi', 'core'), 0, 0, tiled=False)  4.98 us
  transfers between devices with their start and end apart: 3, of which 3 were waited for; matrix products, arithmetic and copies ran while one was open for 9% of the time, Pallas kernels for 0%

profile of v1, /device:TPU:1, one launch (start us, length us, event | category | flops | bytes accessed | tf_op | source)
XLA Modules:
  0.0 239.5 jit_solution(12635263592615105458)
XLA Ops:
  6.5 0.0 copy-start.2
  6.5 1.2 dynamic-slice.4
  8.4 0.9 dynamic-update-slice
  9.3 0.1 reshape.25
  9.4 7.4 %all-reduce.2 = s32[4,2,32]{2,1,0:T(2,128)S(1)} all-reduce(s32[4,2,32]{2,1,0:T(2,128)S(1)} %reshape.25), channel_id=3, replica_groups=mesh['zhi'=2,'core'=2,'y'=4,'zlo'=2,'x'=4] {'zhi','core'}, use_global_device_ids=true, to_apply=%add.1 | all-reduce | flops 256 | bytes 2048
  16.8 0.2 dynamic-slice_reduce_fusion
  17.0 0.1 eq.15
  17.1 1.3 convert_bitcast_fusion
  18.4 0.0 copy-start
  18.4 1.6 copy-done
  20.0 0.0 copy-start.1
  20.0 0.9 copy-done.1
  21.0 12.0 %spectra.1 = bf16[8192,128]{1,0:T(8,128)(2,1)} custom-call(bf16[4,2000,128]{2,1,0:T(8,128)(2,1)S(1)} %bitcast.17, f32[4,8,2000]{2,1,0:T(8,128)S(1)} %copy-done.1, f32[1,512]{1,0:T(1,128)S(1)} %bitcast.18), custom_call_target="tpu_custom_call" | custom-call | tf_op jit(solution)/shard_map/spectra/pallas_call | solution.py:95
  33.0 2.3 convolution_convert_fusion
  35.3 0.8 reshape.26
  36.0 5.0 %all-to-all-start = ((bf16[4,2,8192]{2,1,0:T(2,128)(2,1)}), bf16[4,2,8192]{2,1,0:T(2,128)(2,1)S(1)}, u32[]{:S(2)}, u32[]{:S(2)}) async-start(bf16[4,2,8192]{2,1,0:T(2,128)(2,1)} %reshape.26), calls=%async_computation | async-start | bytes 262144 | tf_op jit(solution)/shard_map/all_to_all | solution.py:243
  41.0 0.0 all-gather.9.cloned.1.call-start
  41.0 0.1 broadcast_compare_fusion
  41.1 0.0 copy-done.2
  41.1 0.1 convolution_convert_fusion.1
  41.2 4.9 %all-to-all-done = bf16[4,2,8192]{2,1,0:T(2,128)(2,1)S(1)} async-done(((bf16[4,2,8192]{2,1,0:T(2,128)(2,1)}), bf16[4,2,8192]{2,1,0:T(2,128)(2,1)S(1)}, u32[]{:S(2)}, u32[]{:S(2)}) %all-to-all-start) | async-done | bytes 131104 | tf_op jit(solution)/shard_map/all_to_all | solution.py:243
  46.1 0.1 fusion.1
  46.2 4.5 %all-gather.2 = bf16[2,2,32896]{2,1,0:T(2,128)(2,1)S(1)} all-gather(bf16[1,2,32896]{2,1,0:T(2,128)(2,1)S(1)} %fusion.1), channel_id=1, replica_groups=mesh['zhi'=2,'core'=2,'y'=4,'zlo'=2,'x'=4] {'zlo'}, dimensions={0}, use_global_device_ids=true | all-gather | bytes 394752 | tf_op jit(solution)/shard_map/all_gather | solution.py:249
  50.7 1.2 reshape.38
  51.9 0.0 all-gather.9.cloned.1.call-update
  51.9 0.0 all-gather.7.cloned.1.call-start
  52.0 0.7 all-gather.7.cloned.1.call-update
  52.7 51.8 %all-gather.9.cloned.1.call-done = bf16[16,4,32896]{2,1,0:T(4,128)(2,1)} async-done(((bf16[1,4,32896]{2,1,0:T(4,128)(2,1)}), bf16[16,4,32896]{2,1,0:T(4,128)(2,1)}) %all-gather.9.cloned.1.call-update) | async-done | bytes 4210704 | tf_op jit(solution)/shard_map/all_gather | solution.py:250
  104.5 7.0 %reshape.39 = bf16[64,32896]{1,0:T(8,128)(2,1)} reshape(bf16[16,4,32896]{2,1,0:T(4,128)(2,1)} %all-gather.9.cloned.1.call-done) | data formatting | bytes 8421376
  111.5 1.3 slice.9.msrc_ref
  112.8 4.7 %slice.8 = bf16[64,32768]{1,0:T(8,128)(2,1)} slice(bf16[64,32896]{1,0:T(8,128)(2,1)} %reshape.39), slice={[0:64], [0:32768]} | slice | bytes 8388608 | tf_op jit(solution)/shard_map/slice | solution.py:251
  117.5 8.1 %reshape.28.x_ref = bf16[64,4,8192]{2,1,0:T(4,128)(2,1)} reshape(bf16[64,32768]{1,0:T(8,128)(2,1)} %slice.8) | data formatting | bytes 8388608 | tf_op jit(solution)/shard_map/reshape | solution.py:251
  125.6 43.2 %all-gather.7.cloned.1.call-done = bf16[32768,128]{1,0:T(8,128)(2,1)} async-done(((bf16[8192,128]{1,0:T(8,128)(2,1)}), bf16[32768,128]{1,0:T(8,128)(2,1)}) %all-gather.7.cloned.1.call-update) | async-done | bytes 8388624 | tf_op jit(solution)/shard_map/all_gather | solution.py:253
  168.8 63.9 %correlate.1 = f32[12864,128]{1,0:T(8,128)} custom-call(bf16[4,8192,128]{2,1,0:T(8,128)(2,1)} %bitcast.19, bf16[64,4,8192]{2,1,0:T(4,128)(2,1)} %reshape.28.x_ref, bf16[4,208,512]{2,1,0:T(8,128)(2,1)} %constant.41.clone.lag_ref, bf16[64,16]{1,0:T(8,128)(2,1)} %slice.9.msrc_ref, bf16[16,128]{1,0:T(8,128)(2,1)} %get-tuple-element.5.qual_ref), custom_call_target="tpu_custom_call" | custom-call | tf_op jit(solution)/shard_map/correlate/pallas_call | solution.py:205
  (3 shorter events, 0.0 us)
Async XLA Ops:
  6.5 34.6 %copy-start.2 = (s32[128,16]{0,1:T(8,128)S(1)}, s32[128,16]{0,1:T(8,128)}, u32[]{:S(2)}) copy-start(s32[128,16]{0,1:T(8,128)} %param.7) | copy-start | bytes 24580
  18.4 1.6 copy-start
  20.0 0.9 copy-start.1
  36.0 10.1 %all-to-all-start = ((bf16[4,2,8192]{2,1,0:T(2,128)(2,1)}), bf16[4,2,8192]{2,1,0:T(2,128)(2,1)S(1)}, u32[]{:S(2)}, u32[]{:S(2)}) async-start(bf16[4,2,8192]{2,1,0:T(2,128)(2,1)} %reshape.26), calls=%async_computation | async-start | bytes 262144 | tf_op jit(solution)/shard_map/all_to_all | solution.py:243
  41.0 63.5 %all-gather.9.cloned.1.call-start = ((), (), s32[]{:S(2)}) async-start(), calls=%async_computation.2 | async-start | bytes 4473856 | tf_op jit(solution)/shard_map/all_gather | solution.py:250
  51.9 116.9 %all-gather.7.cloned.1.call-start = ((), (), s32[]{:S(2)}) async-start(), calls=%async_computation.1 | async-start | bytes 10485760 | tf_op jit(solution)/shard_map/all_gather | solution.py:253
Sparse Core Ops, SparseCore 0:
  52.0 52.4 all-gather.8
  106.2 62.6 all-gather.6

commit v2 on v1

v2 whole, which is shorter than its diff:
```python
import functools
import math

import jax
import jax.numpy as jnp
import ml_dtypes
import numpy as np
from jax import lax
from jax.experimental import pallas as pl
from jax.experimental.pallas import tpu as pltpu
from jax.sharding import Mesh, PartitionSpec as P

LAGH = 100
NLAG = 2 * LAGH + 1
TAU = 208
GRP = 8
KPAD = 1024
NGRP = KPAD // GRP
SDEV = 4
ROWS = 64
MB = 1 << 20


def start_tables(length):
    bins = np.arange(1, GRP + 1, dtype=np.float64)
    times = np.arange(length, dtype=np.float64)
    phase = 2.0 * math.pi / length * ((bins[:, None] * times[None, :]) % length)
    step = 2.0 * math.pi / length * ((GRP * times) % length)
    step = np.broadcast_to(step[None, :], phase.shape)
    return np.stack([np.cos(phase), -np.sin(phase), np.cos(step), np.sin(step)]).astype(np.float32)


def lag_table(half):
    bins = np.arange(1, half + 1, dtype=np.int64)
    lags = np.arange(-LAGH, LAGH + 1, dtype=np.int64)
    phase = 2.0 * math.pi / (2 * half) * ((lags[:, None] * bins[None, :]) % (2 * half))
    weight = np.where(bins == half, 1.0, 2.0)[None, :] / math.sqrt(half)
    out = np.zeros((TAU, 2, KPAD), np.float32)
    out[:NLAG, 0, :half] = weight * np.cos(phase)
    out[:NLAG, 1, :half] = -weight * np.sin(phase)
    return out.astype(ml_dtypes.bfloat16)


DBLK = 25


def spectra_kernel(half, x_ref, start_ref, qual_ref, flag_ref, hot_ref, y0_ref, y1_ref, sel_ref, y_ref, state, table, spec, power):
    ngrp = half // GRP
    state[0] = start_ref[0]
    state[1] = start_ref[1]
    power[...] = jnp.zeros_like(power)
    x01 = [x_ref[g] for g in range(4)]
    samples = jnp.concatenate(x01, axis=1)

    def gen(n, _):
        cos, sin = state[0], state[1]
        table[pl.ds(pl.multiple_of(n * 16, 16), 16), :] = jnp.concatenate([cos, sin], axis=0).astype(jnp.bfloat16)
        rc, rs = start_ref[2], start_ref[3]
        state[0] = cos * rc + sin * rs
        state[1] = sin * rc - cos * rs
        return 0

    def block(b, _):
        lax.fori_loop(0, DBLK, gen, 0)
        prod = jnp.dot(table[...], samples, preferred_element_type=jnp.float32)
        spec[pl.ds(pl.multiple_of(b * (DBLK * 16), DBLK * 16), DBLK * 16), :] = prod
        sq = prod * prod
        power[...] += jnp.sum(sq.reshape(DBLK * 2, 8, 512), axis=0)
        return 0

    lax.fori_loop(0, ngrp // DBLK, block, 0)
    mean = jnp.sum(power[...], axis=0, keepdims=True) * (1.0 / half)
    level2 = 0.25 * (mean + 1e-06)

    def white(n, _):
        base = pl.multiple_of(n * 16, 16)
        real = spec[pl.ds(base, 8), :]
        imag = spec[pl.ds(base + 8, 8), :]
        inv = lax.rsqrt(jnp.maximum(real * real + imag * imag, level2)) * qual_ref[...]
        parts = []
        for value in (real * inv, imag * inv):
            for g in range(4):
                parts.append(value[:, g * 128 : (g + 1) * 128])
        y_ref[pl.ds(pl.multiple_of(n * ROWS, ROWS), ROWS), :] = jnp.concatenate(parts, axis=0).astype(jnp.bfloat16)
        return 0

    lax.fori_loop(0, ngrp, white, 0)
    y_ref[pl.ds(ngrp * ROWS, (NGRP - ngrp) * ROWS), :] = jnp.zeros(((NGRP - ngrp) * ROWS, 128), jnp.bfloat16)
    y_ref[pl.ds((NGRP - 1) * ROWS, 16), :] = flag_ref[...].astype(jnp.bfloat16)
    y0_ref[...] = y_ref[: CHUNKS[0] * 8, :]
    y1_ref[...] = y_ref[CHUNKS[0] * 8 :, :]
    picked = lax.dot_general(
        hot_ref[...], y_ref[...], (((1,), (1,)), ((), ())), preferred_element_type=jnp.float32
    )
    sel_ref[...] = picked.astype(jnp.bfloat16)


def spectra(samples, qual, flags, onehot):
    length = samples.shape[1]
    half = length // 2
    start = jnp.asarray(start_tables(length))
    return pl.pallas_call(
        functools.partial(spectra_kernel, half),
        out_shape=[
            jax.ShapeDtypeStruct((CHUNKS[0] * 8, 128), jnp.bfloat16),
            jax.ShapeDtypeStruct((CHUNKS[1] * 8, 128), jnp.bfloat16),
            jax.ShapeDtypeStruct((8, NGRP * ROWS), jnp.bfloat16),
        ],
        scratch_shapes=[
            pltpu.VMEM((NGRP * ROWS, 128), jnp.bfloat16),
            pltpu.VMEM((2, 8, length), jnp.float32),
            pltpu.VMEM((DBLK * 16, length), jnp.bfloat16),
            pltpu.VMEM((2 * half, 512), jnp.float32),
            pltpu.VMEM((8, 512), jnp.float32),
        ],
        compiler_params=pltpu.CompilerParams(vmem_limit_bytes=48 * MB),
        name="spectra",
    )(samples, start, qual, flags, onehot)


UNROLL = 4
CHUNKS = (640, 384)


def correlate_kernel(first, last, kc, *refs):
    where_ref, seg_ref, ya, yb, yc, yd, xa, xb, xc, xd, lag_ref, qual_ref = refs[:12]
    if first:
        out_ref, ybuf, xbuf, xrow, cross, sems = refs[12:]
        acc_ref = None
    else:
        acc_hbm, out_ref, ybuf, xbuf, xrow, cross, sems, acc_ref, scale, stage, osem = refs[12:]
    copies = []
    for j, ref in enumerate((ya, yb, yc, yd)):
        copies.append(pltpu.make_async_copy(ref, ybuf.at[seg_ref[j]], sems.at[j]))
    for j, ref in enumerate((xa, xb, xc, xd)):
        copies.append(pltpu.make_async_copy(ref, xbuf.at[j], sems.at[4 + j]))
    for copy in copies:
        copy.start()
    if not first:
        prefetch = pltpu.make_async_copy(acc_hbm, acc_ref, sems.at[8])
        prefetch.start()
    for copy in copies:
        copy.wait()

    rowid = lax.broadcasted_iota(jnp.int32, (16, 256), 0) % GRP
    lane = lax.broadcasted_iota(jnp.int32, (16, 256), 1) % GRP
    keep = rowid == lane
    zero = jnp.zeros((16, 256), jnp.bfloat16)
    stay = (lax.broadcasted_iota(jnp.int32, (8, 128), 0) < 4) == (lax.broadcasted_iota(jnp.int32, (8, 128), 1) < 64)

    def pair(n, slot):
        for far in range(4):
            for near in range(4):
                tile = xbuf[far, near * 16 : near * 16 + 16, pl.ds(pl.multiple_of(n * 128, 128), 128)].astype(jnp.float32)
                for half in range(2):
                    part = tile[half * 8 : half * 8 + 8]
                    moved = pltpu.roll(pltpu.roll(part, 4, 0), 64, 1)
                    row = (far * 4 + near) * 8
                    xrow[slot, row : row + 8, half * 128 : half * 128 + 128] = jnp.where(stay, part, moved)
        prods = []
        for a in range(2):
            tiles = []
            for p in range(0, 64, 2):
                row = (p // 4) * 8 + a * 4 + p % 4
                two = jnp.concatenate(
                    [xrow[slot, pl.ds(row, 8, stride=0), :], xrow[slot, pl.ds(row + 1, 8, stride=0), :]], axis=0
                ).astype(jnp.bfloat16)
                tiles.append(jnp.where(keep, two, zero))
            lhs = jnp.concatenate(tiles, axis=0)
            base = pl.multiple_of((2 * n + a) * ROWS, ROWS)
            reim, imre = [], []
            for s in range(SDEV):
                yr = ybuf[s, pl.ds(base, 32), :]
                yi = ybuf[s, pl.ds(base + 32, 32), :]
                reim += [yr, yi]
                imre += [-yi, yr]
            right = jnp.concatenate([jnp.concatenate(reim, axis=0), jnp.concatenate(imre, axis=0)], axis=1)
            prods.append(jnp.dot(lhs, right, preferred_element_type=jnp.float32))
        off = pl.multiple_of(n * 16, 16)
        for p in range(64):
            both = jnp.concatenate([prods[0][8 * p : 8 * p + 8], prods[1][8 * p : 8 * p + 8]], axis=0)
            both = both.astype(jnp.bfloat16)
            cross[p, pl.ds(off, 16), :] = both[:, :128]
            cross[p, pl.ds(pl.multiple_of(kc + off, 16), 16), :] = both[:, 128:]

    def pairs(m, _):
        for v in range(UNROLL):
            pair(m * UNROLL + v, v)
        return 0

    lax.fori_loop(0, kc // 16 // UNROLL, pairs, 0)
    table = lag_ref[...]
    if last:
        flags = []
        for far in range(4):
            for near in range(4):
                flags.append(xbuf[far, near * 16 : near * 16 + 4, kc * 8 - 128 :])
        flags = jnp.concatenate([f.astype(jnp.float32) for f in flags], axis=0)[:, 64:80].astype(jnp.bfloat16)
        count = jnp.dot(flags, qual_ref[...], preferred_element_type=jnp.float32)
        scale[...] = 1.0 / jnp.maximum(count, 1.0)
        prefetch.wait()

    def flush(n, slot):
        return pltpu.make_async_copy(stage.at[slot], out_ref.at[:, pl.ds(pl.multiple_of(n * 8, 8), 8), :], osem.at[slot])

    def lags(n, _):
        spots = [where_ref[n * 8 + j] for j in range(8)]
        parts = []
        for q in range(4):
            right = jnp.concatenate([cross[spots[2 * q]], cross[spots[2 * q + 1]]], axis=1)
            prod = jnp.dot(table, right, preferred_element_type=jnp.float32)
            parts += [prod[:, :128], prod[:, 128:]]
        if last:
            slot = n % 2
            parts = [(part + acc_ref[p]) * scale[pl.ds(p, 1), :] for part, p in zip(parts, spots)]

            @pl.when(n >= 2)
            def _():
                flush(n - 2, slot).wait()

            stage[slot] = pltpu.einshape("itj->tij", jnp.stack(parts, axis=0))[:NLAG]
            flush(n, slot).start()
        else:
            for part, p in zip(parts, spots):
                out_ref[p] = part
        return 0

    lax.fori_loop(0, 8, lags, 0)
    if last:
        flush(6, 0).wait()
        flush(7, 1).wait()


def correlate(first, last, kc, where, seg, ys, xs, table, qual_t, acc=None):
    smem = pl.BlockSpec(memory_space=pltpu.SMEM)
    hbm = pl.BlockSpec(memory_space=pl.ANY)
    vmem = pl.BlockSpec(memory_space=pltpu.VMEM)
    args = (where, seg, *ys, *xs, table, qual_t)
    in_specs = [smem, smem] + [hbm] * 8 + [vmem, vmem]
    scratch = [
        pltpu.VMEM((4, kc * 8, 128), jnp.bfloat16),
        pltpu.VMEM((4, 64, kc * 8), jnp.bfloat16),
        pltpu.VMEM((UNROLL, 128, 256), jnp.float32),
        pltpu.VMEM((64, 2 * kc, 128), jnp.bfloat16),
        pltpu.SemaphoreType.DMA((9,)),
    ]
    if first:
        out_shape, out_specs = (64, TAU, 128), vmem
    else:
        out_shape, out_specs = (NLAG, 64, 128), hbm
        args += (acc,)
        in_specs += [hbm]
        scratch += [
            pltpu.VMEM((64, TAU, 128), jnp.float32),
            pltpu.VMEM((64, 128), jnp.float32),
            pltpu.VMEM((2, NLAG, 8, 128), jnp.float32),
            pltpu.SemaphoreType.DMA((2,)),
        ]
    return pl.pallas_call(
        functools.partial(correlate_kernel, first, last, kc),
        out_shape=jax.ShapeDtypeStruct(out_shape, jnp.float32),
        in_specs=in_specs,
        out_specs=out_specs,
        scratch_shapes=scratch,
        compiler_params=pltpu.CompilerParams(vmem_limit_bytes=60 * MB),
        name="correlate_first" if first else "correlate_last",
    )(*args)


AXES = ("zhi", "core", "y", "zlo", "x")
SIZES = (2, 2, 4, 2, 4)


def permutation(move):
    out = []
    for flat in range(128):
        at = list(np.unravel_index(flat, SIZES))
        to = move(*[int(v) for v in at])
        out.append((flat, int(np.ravel_multi_index([v % n for v, n in zip(to, SIZES)], SIZES))))
    return out


def send(value, move):
    return lax.ppermute(value, AXES, permutation(move))


def sibling(zhi, core, y, zlo, x):
    return zhi, core + 1, y, zlo, x


def across(zhi, core, y, zlo, x):
    return zhi + 1, core, y, zlo, x


def ring(phase, d):
    def move(zhi, core, y, zlo, x):
        if core == phase:
            return zhi, core, y, zlo, x + d
        return zhi, core, y + d, zlo, x

    return move


def on_device(traces, src_index, quality):
    rows = traces.shape[0]
    samples = jnp.transpose(traces, (1, 2, 0))
    qual_f = jnp.transpose(quality, (1, 0)).astype(jnp.float32)
    zhi, core, yy, zlo, xx = [lax.axis_index(a) for a in AXES]
    me = zhi * 2 + core
    r = yy * 8 + zlo * 4 + xx
    qual_own = lax.dynamic_slice_in_dim(qual_f, me * 4, 4, axis=0).reshape(1, 512)
    index_all = lax.all_gather(src_index, ("zhi", "core"), axis=0, tiled=False)
    mine = lax.dynamic_slice_in_dim(index_all.reshape(4, 2, 32), r, 1, axis=2).reshape(8) - r * rows
    onehot = (mine[:, None] == jnp.arange(rows, dtype=jnp.int32)[None, :]).astype(jnp.bfloat16)
    table = lag_table(1000)
    tables, start = [], 0
    for kc in CHUNKS:
        tables.append(jnp.asarray(np.ascontiguousarray(table[:, :, start : start + kc]).reshape(TAU, 2 * kc)))
        start += kc

    y0, y1, sel = spectra(samples, qual_own, qual_f, onehot)
    ys0 = [y0]
    ys1 = [y1]
    far0 = send(y0, across)
    far1 = send(y1, across)
    near0, near1 = send(y0, sibling), send(y1, sibling)

    sel = sel.reshape(4, 1, 2, -1)
    slots = jnp.broadcast_to(sel, (4, 2, 2, sel.shape[-1])).reshape(8, 2, -1)
    got = lax.all_to_all(slots, ("zhi", "core", "zlo"), 0, 0, tiled=False)
    got = got.reshape(16, -1)
    xs = []
    start = 0
    for kc in CHUNKS:
        own = got[:, start * 8 : (start + kc) * 8]
        start += kc
        line = jnp.concatenate([own] + [send(own, ring(0, d)) for d in (1, 2, 3)], axis=0)
        xs.append([line] + [send(line, ring(1, d)) for d in (1, 2, 3)])

    i = jnp.arange(64, dtype=jnp.int32)
    dx, dy = (xx - i % 4) % 4, (yy - (i // 8) % 4) % 4
    far_step, near_step = jnp.where(core == 0, dy, dx), jnp.where(core == 0, dx, dy)
    where = far_step * 16 + near_step * 4 + (i // 4) % 2 * 2 + i // 32
    seg = jnp.bitwise_xor(me, jnp.arange(4, dtype=jnp.int32))
    qual_b = qual_f.astype(jnp.bfloat16)
    acc = correlate(
        True, False, CHUNKS[0], where, seg, (y0, near0, far0, send(far0, sibling)), xs[0], tables[0], qual_b
    )
    out = correlate(
        False, True, CHUNKS[1], where, seg, (y1, near1, far1, send(far1, sibling)), xs[1], tables[1], qual_b, acc
    )
    return jnp.transpose(out, (1, 0, 2))


def solution(mesh):
    fine = Mesh(mesh.devices.reshape(2, 2, 4, 2, 4), ("zhi", "core", "y", "zlo", "x"))
    rcv = ("y", "zlo", "x")
    src = ("zhi", "core")
    return jax.shard_map(
        on_device,
        mesh=fine,
        in_specs=(P(rcv, src, None), P(src), P(rcv, None)),
        out_specs=P(src, None, rcv),
        check_vma=False,
    )
```

time: 240 us -> 149 us (0.62)
  waiting for transfers between devices: 101 us -> 25.2 us
  Pallas kernels: 75.9 us -> 47 us
  blocking collectives: 11.9 us -> 40.3 us
  local copies, waits for them, and re-layouts: 28.1 us -> 8.84 us
  starting transfers between devices: 5.03 us -> 21.5 us
  between operations: 14.1 us -> 0.86 us
    all_gather x2 -> x0, waiting for transfers between devices: 95 us -> none  [the longest x1 51.8 us: on_device(): payload = lax.all_gather(payload, ('y', 'x'), axis=0, tiled=True)]
    all_to_all x0 -> x1, blocking collectives: none -> 32.9 us  [on_device(): got = lax.all_to_all(slots, ('zhi', 'core', 'zlo'), 0, 0, tiled=False)]
    pallas_call x2 -> x3, Pallas kernels: 75.9 us -> 47 us  [the longest x2 35.6 us: correlate(): pl.pallas_call(functools.partial(correlate_kernel, first, last, kc), out_...]
    ppermute x0 -> x18, waiting for transfers between devices: none -> 25.2 us  [send(): return lax.ppermute(value, AXES, permutation(move))]
    ppermute x0 -> x18, starting transfers between devices: none -> 21.5 us  [send(): return lax.ppermute(value, AXES, permutation(move))]
    reshape x3 -> x2, local copies, waits for them, and re-layouts: 8.99 us -> 0.18 us  [the longest x1 0.1 us: on_device(): got = got.reshape(16, -1)]
    slice x2, local copies, waits for them, and re-layouts: 6 us -> 0.02 us  [on_device(): own = got[:, start * 8:(start + kc) * 8]]
    all_to_all x1 -> x0, starting transfers between devices: 4.98 us -> none  [on_device(): got = lax.all_to_all(sel, ('zhi', 'core'), 0, 0, tiled=False)]
  transfers between devices with their start and end apart: 3 -> 18, of which waited for: 3 -> 6; matrix products, arithmetic and copies ran while one was open for 9% -> 1% of each run, Pallas kernels for 0% -> 14%
where the time goes in v2:
time: 149 us; the launch traced here: 146 us
  Pallas kernels  47 us (32%)
  blocking collectives  40.3 us (27%)
  waiting for transfers between devices  25.2 us (17%)
  starting transfers between devices  21.5 us (14%)
  local copies, waits for them, and re-layouts  8.84 us (6%)
  other arithmetic  2.76 us (2%)
    pallas_call x2, Pallas kernels, correlate(): pl.pallas_call(functools.partial(correlate_kernel, first, last, kc), out_...  35.6 us
    all_to_all x1, blocking collectives, on_device(): got = lax.all_to_all(slots, ('zhi', 'core', 'zlo'), 0, 0, tiled=False)  32.9 us
    ppermute x18, waiting for transfers between devices, send(): return lax.ppermute(value, AXES, permutation(move))  25.2 us
    ppermute x18, starting transfers between devices, send(): return lax.ppermute(value, AXES, permutation(move))  21.5 us
    pallas_call x1, Pallas kernels, spectra(): pl.pallas_call(functools.partial(spectra_kernel, half), out_shape=[jax.Sh...  11.4 us
    unnamed x31, local copies, waits for them, and re-layouts  8.31 us
    unnamed x1, blocking collectives  7.44 us
  transfers between devices with their start and end apart: 18, of which 6 were waited for; matrix products, arithmetic and copies ran while one was open for 1% of the time, Pallas kernels for 14%

profile of v2, /device:TPU:1, one launch (start us, length us, event | category | flops | bytes accessed | tf_op | source)
XLA Modules:
  0.0 146.4 jit_solution(18350349254346556655)
XLA Ops:
  0.0 1.2 dynamic-slice.4
  1.9 0.9 dynamic-update-slice
  2.8 0.1 reshape.23
  2.8 7.4 %all-reduce.1 = s32[4,2,32]{2,1,0:T(2,128)S(1)} all-reduce(s32[4,2,32]{2,1,0:T(2,128)S(1)} %reshape.23), channel_id=2, replica_groups=mesh['zhi'=2,'core'=2,'y'=4,'zlo'=2,'x'=4] {'zhi','core'}, use_global_device_ids=true, to_apply=%add | all-reduce | flops 256 | bytes 2048
  10.3 0.2 subtract_reduce_fusion
  10.5 0.1 sub.48
  10.6 0.1 fusion.hot_ref
  10.7 1.3 bitcast_convert_fusion
  12.0 1.6 %copy-done = bf16[128,4,2000]{0,2,1:T(8,128)(2,1)S(1)} copy-done((bf16[128,4,2000]{0,2,1:T(8,128)(2,1)S(1)}, bf16[128,4,2000]{0,2,1:T(8,128)(2,1)}, u32[]{:S(2)}) %copy-start) | copy-done | bytes 2048024
  13.5 0.9 copy-done.3
  14.5 11.4 %spectra.1 = (bf16[5120,128]{1,0:T(8,128)(2,1)S(1)}, bf16[3072,128]{1,0:T(8,128)(2,1)S(1)}, bf16[8,8192]{1,0:T(8,128)(2,1)S(1)}) custom-call(bf16[4,2000,128]{2,1,0:T(8,128)(2,1)S(1)} %bitcast.10, f32[4,8,2000]{2,1,0:T(8,128)S(1)} %copy-done.3, f32[1,512]{1,0:T(1,128)S(1)} %bitcast.11, f32[16,128]{1,0:T(8,128)S(1)} %get-tuple-element.12.flag_ref, ...), custom_call_target="tpu_custom_call" | custom-call | tf_op jit(solution)/shard_map/spectra/pallas_call | solution.py:102
  25.9 1.7 %collective-permute-start.10 = (bf16[5120,128]{1,0:T(8,128)(2,1)S(1)}, bf16[5120,128]{1,0:T(8,128)(2,1)}, u32[]{:S(2)}, u32[]{:S(2)}) collective-permute-start(bf16[5120,128]{1,0:T(8,128)(2,1)S(1)} %get-tuple-element.10.refs_2_), channel_id=1, source_target_pairs={{0,64},{1,65},{2,66},{3,67},{4,68},{5,69},{6,70},{7,71},{8,72},{9,... | collective-permute-start | bytes 3932168 | tf_op jit(solution)/shard_map/ppermute | solution.py:284
  27.6 0.1 broadcast_in_dim.4
  27.7 0.1 broadcast_in_dim.10
  27.8 32.9 %all_to_all.5 = bf16[8,2,8192]{2,1,0:T(2,128)(2,1)S(1)} all-to-all(bf16[8,2,8192]{2,1,0:T(2,128)(2,1)S(1)} %bitcast.12), channel_id=1, replica_groups=mesh['zhi'=2,'core'=2,'y'=4,'zlo'=2,'x'=4] {'zhi','core','zlo'}, dimensions={0} | all-to-all | bytes 524288 | tf_op jit(solution)/shard_map/all_to_all | solution.py:330
  60.7 0.1 reshape.25
  60.8 1.4 collective-permute-start.12
  62.2 2.6 %collective-permute-start.13 = (bf16[16,5120]{1,0:T(8,128)(2,1)S(1)}, bf16[16,5120]{1,0:T(8,128)(2,1)S(1)}, u32[]{:S(2)}, u32[]{:S(2)}) collective-permute-start(bf16[16,5120]{1,0:T(8,128)(2,1)S(1)} %slice.9), channel_id=1, source_target_pairs={{0,2},{1,3},{2,0},{3,1},{4,6},{5,7},{6,4},{7,5},{8,10},{9,11},{10,... | collective-permute-start | bytes 491528 | tf_op jit(solution)/shard_map/ppermute | solution.py:284
  64.8 1.1 collective-permute-start.14
  65.9 0.5 collective-permute-start.3
  66.4 4.3 %collective-permute-done.3 = bf16[16,3072]{1,0:T(8,128)(2,1)S(1)} collective-permute-done((bf16[16,3072]{1,0:T(8,128)(2,1)S(1)}, bf16[16,3072]{1,0:T(8,128)(2,1)S(1)}, u32[]{:S(2)}, u32[]{:S(2)}) %collective-permute-start.3) | collective-permute-done | bytes 98336 | tf_op jit(solution)/shard_map/ppermute | solution.py:284
  70.6 2.6 %collective-permute-start.9 = (bf16[5120,128]{1,0:T(8,128)(2,1)S(1)}, bf16[5120,128]{1,0:T(8,128)(2,1)S(1)}, u32[]{:S(2)}, u32[]{:S(2)}) collective-permute-start(bf16[5120,128]{1,0:T(8,128)(2,1)S(1)} %get-tuple-element.10.refs_2_), channel_id=1, source_target_pairs={{0,32},{1,33},{2,34},{3,35},{4,36},{5,37},{6,38},{7,39},{8,40},{9,... | collective-permute-start | bytes 3932168 | tf_op jit(solution)/shard_map/ppermute | solution.py:284
  73.2 0.0 collective-permute-done.12
  73.2 1.6 %collective-permute-start.1 = (bf16[3072,128]{1,0:T(8,128)(2,1)S(1)}, bf16[3072,128]{1,0:T(8,128)(2,1)}, u32[]{:S(2)}, u32[]{:S(2)}) collective-permute-start(bf16[3072,128]{1,0:T(8,128)(2,1)S(1)} %get-tuple-element.8.refs_2_), channel_id=1, source_target_pairs={{0,64},{1,65},{2,66},{3,67},{4,68},{5,69},{6,70},{7,71},{8,72},{9,... | collective-permute-start | bytes 2359304 | tf_op jit(solution)/shard_map/ppermute | solution.py:284
  74.9 0.0 collective-permute-done.13
  74.9 2.9 %collective-permute-start.4 = (bf16[16,3072]{1,0:T(8,128)(2,1)S(1)}, bf16[16,3072]{1,0:T(8,128)(2,1)S(1)}, u32[]{:S(2)}, u32[]{:S(2)}) collective-permute-start(bf16[16,3072]{1,0:T(8,128)(2,1)S(1)} %slice.8), channel_id=1, source_target_pairs={{0,2},{1,3},{2,0},{3,1},{4,6},{5,7},{6,4},{7,5},{8,10},{9,11},{10,... | collective-permute-start | bytes 294920 | tf_op jit(solution)/shard_map/ppermute | solution.py:284
  77.8 0.0 collective-permute-done.14
  77.8 0.8 collective-permute-start.5
  78.6 0.0 collective-permute-done.10.refs_4_
  78.6 1.6 %collective-permute-done.4 = bf16[16,3072]{1,0:T(8,128)(2,1)S(1)} collective-permute-done((bf16[16,3072]{1,0:T(8,128)(2,1)S(1)}, bf16[16,3072]{1,0:T(8,128)(2,1)S(1)}, u32[]{:S(2)}, u32[]{:S(2)}) %collective-permute-start.4) | collective-permute-done | bytes 98336 | tf_op jit(solution)/shard_map/ppermute | solution.py:284
  80.2 1.4 collective-permute-done.5
  81.7 0.3 collective-permute-start.16
  81.9 12.1 %collective-permute-done.1.refs_4_ = bf16[3072,128]{1,0:T(8,128)(2,1)} collective-permute-done((bf16[3072,128]{1,0:T(8,128)(2,1)S(1)}, bf16[3072,128]{1,0:T(8,128)(2,1)}, u32[]{:S(2)}, u32[]{:S(2)}) %collective-permute-start.1) | collective-permute-done | bytes 786464 | tf_op jit(solution)/shard_map/ppermute | solution.py:284
  94.0 4.2 %collective-permute-done.15.refs_7_ = bf16[64,5120]{1,0:T(8,128)(2,1)S(1)} collective-permute-done((bf16[64,5120]{1,0:T(8,128)(2,1)S(1)}, bf16[64,5120]{1,0:T(8,128)(2,1)S(1)}, u32[]{:S(2)}, u32[]{:S(2)}) %collective-permute-start.15) | collective-permute-done | bytes 655392 | tf_op jit(solution)/shard_map/ppermute | solution.py:284
  98.2 0.8 copy-done.8
  99.1 0.8 copy-done.9
  99.9 2.3 %collective-permute-start.2 = (bf16[3072,128]{1,0:T(8,128)(2,1)}, bf16[3072,128]{1,0:T(8,128)(2,1)}, u32[]{:S(2)}, u32[]{:S(2)}) collective-permute-start(bf16[3072,128]{1,0:T(8,128)(2,1)} %collective-permute-done.1.refs_4_), channel_id=1, source_target_pairs={{0,32},{1,33},{2,34},{3,35},{4,36},{5,37},{6,38},{7,39},{8,40},{9,... | collective-permute-start | bytes 2359304 | tf_op jit(solution)/shard_map/ppermute | solution.py:284
  102.2 1.6 %collective-permute-done.17.refs_9_ = bf16[64,5120]{1,0:T(8,128)(2,1)S(1)} collective-permute-done((bf16[64,5120]{1,0:T(8,128)(2,1)S(1)}, bf16[64,5120]{1,0:T(8,128)(2,1)S(1)}, u32[]{:S(2)}, u32[]{:S(2)}) %collective-permute-start.17) | collective-permute-done | bytes 655392 | tf_op jit(solution)/shard_map/ppermute | solution.py:284
  103.8 2.1 %collective-permute-start.7 = (bf16[64,3072]{1,0:T(8,128)(2,1)S(1)}, bf16[64,3072]{1,0:T(8,128)(2,1)S(1)}, u32[]{:S(2)}, u32[]{:S(2)}) collective-permute-start(bf16[64,3072]{1,0:T(8,128)(2,1)S(1)} %pad_maximum_fusion.1.refs_6_), channel_id=1, source_target_pairs={{0,16},{1,17},{2,18},{3,19},{4,20},{5,21},{6,22},{7,23},{8,24},{9,... | collective-permute-start | bytes 1179656 | tf_op jit(solution)/shard_map/ppermute | solution.py:284
  105.9 1.0 copy-done.7
  106.9 1.7 %collective-permute-start.8 = (bf16[64,3072]{1,0:T(8,128)(2,1)S(1)}, bf16[64,3072]{1,0:T(8,128)(2,1)S(1)}, u32[]{:S(2)}, u32[]{:S(2)}) collective-permute-start(bf16[64,3072]{1,0:T(8,128)(2,1)S(1)} %pad_maximum_fusion.1.refs_6_), channel_id=1, source_target_pairs={{0,24},{1,25},{2,26},{3,27},{4,28},{5,29},{6,30},{7,31},{8,0},{9,1... | collective-permute-start | bytes 1179656 | tf_op jit(solution)/shard_map/ppermute | solution.py:284
  108.7 0.6 iota_xor_fusion.refs_1_
  109.2 0.5 fusion.1.refs_0_
  109.8 21.1 %correlate_first.1.refs_12_ = f32[64,208,128]{2,1,0:T(8,128)} custom-call(s32[64]{0:T(128)} %fusion.1.refs_0_, s32[4]{0:T(128)} %iota_xor_fusion.refs_1_, bf16[5120,128]{1,0:T(8,128)(2,1)} %copy-done.1, bf16[5120,128]{1,0:T(8,128)(2,1)} %copy-done.6, bf16[5120,128]{1,0:T(8,128)(2,1)} %collective-permute-done.10.refs_4_, bf16[5120,128]{1,0:T(8,128)(2,1)} %copy-done.7, ...), custom_call_target="tpu_custom_call" | custom-call | tf_op jit(solution)/shard_map/correlate_first/pallas_call | solution.py:259
  131.0 0.7 copy-done.11
  131.7 0.1 copy-done.12
  131.8 0.1 copy-done.13
  131.9 14.4 %correlate_last.1 = f32[201,64,128]{2,1,0:T(8,128)} custom-call(s32[64]{0:T(128)} %fusion.1.refs_0_, s32[4]{0:T(128)} %iota_xor_fusion.refs_1_, bf16[3072,128]{1,0:T(8,128)(2,1)} %copy-done.2, bf16[3072,128]{1,0:T(8,128)(2,1)} %collective-permute-done.refs_3_, bf16[3072,128]{1,0:T(8,128)(2,1)} %collective-permute-done.1.refs_4_, ...), custom_call_target="tpu_custom_call" | custom-call | tf_op jit(solution)/shard_map/correlate_last/pallas_call | solution.py:259
  (39 shorter events, 0.2 us)
Async XLA Ops:
  12.0 1.6 %copy-start = (bf16[128,4,2000]{0,2,1:T(8,128)(2,1)S(1)}, bf16[128,4,2000]{0,2,1:T(8,128)(2,1)}, u32[]{:S(2)}) copy-start(bf16[128,4,2000]{0,2,1:T(8,128)(2,1)} %param.6) | copy-start | bytes 6144004
  13.5 0.9 copy-start.3
  25.9 52.7 %copy-start.1 = (bf16[5120,128]{1,0:T(8,128)(2,1)}, bf16[5120,128]{1,0:T(8,128)(2,1)S(1)}, u32[]{:S(2)}) copy-start(bf16[5120,128]{1,0:T(8,128)(2,1)S(1)} %get-tuple-element.10.refs_2_) | copy-start | bytes 3932164
  25.9 72.3 %copy-start.2 = (bf16[3072,128]{1,0:T(8,128)(2,1)}, bf16[3072,128]{1,0:T(8,128)(2,1)S(1)}, u32[]{:S(2)}) copy-start(bf16[3072,128]{1,0:T(8,128)(2,1)S(1)} %get-tuple-element.8.refs_2_) | copy-start | bytes 2359300
  25.9 52.7 %collective-permute-start.10 = (bf16[5120,128]{1,0:T(8,128)(2,1)S(1)}, bf16[5120,128]{1,0:T(8,128)(2,1)}, u32[]{:S(2)}, u32[]{:S(2)}) collective-permute-start(bf16[5120,128]{1,0:T(8,128)(2,1)S(1)} %get-tuple-element.10.refs_2_), channel_id=1, source_target_pairs={{0,64},{1,65},{2,66},{3,67},{4,68},{5,69},{6,70},{7,71},{8,72},{9,... | collective-permute-start | bytes 3932168 | tf_op jit(solution)/shard_map/ppermute | solution.py:284
  60.8 12.4 %collective-permute-start.12 = (bf16[16,5120]{1,0:T(8,128)(2,1)S(1)}, bf16[16,5120]{1,0:T(8,128)(2,1)S(1)}, u32[]{:S(2)}, u32[]{:S(2)}) collective-permute-start(bf16[16,5120]{1,0:T(8,128)(2,1)S(1)} %slice.9), channel_id=1, source_target_pairs={{0,1},{1,2},{2,3},{3,0},{4,5},{5,6},{6,7},{7,4},{8,9},{9,10},{10,1... | collective-permute-start | bytes 491528 | tf_op jit(solution)/shard_map/ppermute | solution.py:284
  62.2 12.7 %collective-permute-start.13 = (bf16[16,5120]{1,0:T(8,128)(2,1)S(1)}, bf16[16,5120]{1,0:T(8,128)(2,1)S(1)}, u32[]{:S(2)}, u32[]{:S(2)}) collective-permute-start(bf16[16,5120]{1,0:T(8,128)(2,1)S(1)} %slice.9), channel_id=1, source_target_pairs={{0,2},{1,3},{2,0},{3,1},{4,6},{5,7},{6,4},{7,5},{8,10},{9,11},{10,... | collective-permute-start | bytes 491528 | tf_op jit(solution)/shard_map/ppermute | solution.py:284
  64.8 13.0 %collective-permute-start.14 = (bf16[16,5120]{1,0:T(8,128)(2,1)S(1)}, bf16[16,5120]{1,0:T(8,128)(2,1)S(1)}, u32[]{:S(2)}, u32[]{:S(2)}) collective-permute-start(bf16[16,5120]{1,0:T(8,128)(2,1)S(1)} %slice.9), channel_id=1, source_target_pairs={{0,3},{1,0},{2,1},{3,2},{4,7},{5,4},{6,5},{7,6},{8,11},{9,8},{10,9... | collective-permute-start | bytes 491528 | tf_op jit(solution)/shard_map/ppermute | solution.py:284
  65.9 4.7 %collective-permute-start.3 = (bf16[16,3072]{1,0:T(8,128)(2,1)S(1)}, bf16[16,3072]{1,0:T(8,128)(2,1)S(1)}, u32[]{:S(2)}, u32[]{:S(2)}) collective-permute-start(bf16[16,3072]{1,0:T(8,128)(2,1)S(1)} %slice.8), channel_id=1, source_target_pairs={{0,1},{1,2},{2,3},{3,0},{4,5},{5,6},{6,7},{7,4},{8,9},{9,10},{10,1... | collective-permute-start | bytes 294920 | tf_op jit(solution)/shard_map/ppermute | solution.py:284
  70.6 33.1 %collective-permute-start.9 = (bf16[5120,128]{1,0:T(8,128)(2,1)S(1)}, bf16[5120,128]{1,0:T(8,128)(2,1)S(1)}, u32[]{:S(2)}, u32[]{:S(2)}) collective-permute-start(bf16[5120,128]{1,0:T(8,128)(2,1)S(1)} %get-tuple-element.10.refs_2_), channel_id=1, source_target_pairs={{0,32},{1,33},{2,34},{3,35},{4,36},{5,37},{6,38},{7,39},{8,40},{9,... | collective-permute-start | bytes 3932168 | tf_op jit(solution)/shard_map/ppermute | solution.py:284
  73.2 20.8 %collective-permute-start.1 = (bf16[3072,128]{1,0:T(8,128)(2,1)S(1)}, bf16[3072,128]{1,0:T(8,128)(2,1)}, u32[]{:S(2)}, u32[]{:S(2)}) collective-permute-start(bf16[3072,128]{1,0:T(8,128)(2,1)S(1)} %get-tuple-element.8.refs_2_), channel_id=1, source_target_pairs={{0,64},{1,65},{2,66},{3,67},{4,68},{5,69},{6,70},{7,71},{8,72},{9,... | collective-permute-start | bytes 2359304 | tf_op jit(solution)/shard_map/ppermute | solution.py:284
  74.9 5.4 %collective-permute-start.4 = (bf16[16,3072]{1,0:T(8,128)(2,1)S(1)}, bf16[16,3072]{1,0:T(8,128)(2,1)S(1)}, u32[]{:S(2)}, u32[]{:S(2)}) collective-permute-start(bf16[16,3072]{1,0:T(8,128)(2,1)S(1)} %slice.8), channel_id=1, source_target_pairs={{0,2},{1,3},{2,0},{3,1},{4,6},{5,7},{6,4},{7,5},{8,10},{9,11},{10,... | collective-permute-start | bytes 294920 | tf_op jit(solution)/shard_map/ppermute | solution.py:284
  77.8 3.9 %collective-permute-start.5 = (bf16[16,3072]{1,0:T(8,128)(2,1)S(1)}, bf16[16,3072]{1,0:T(8,128)(2,1)S(1)}, u32[]{:S(2)}, u32[]{:S(2)}) collective-permute-start(bf16[16,3072]{1,0:T(8,128)(2,1)S(1)} %slice.8), channel_id=1, source_target_pairs={{0,3},{1,0},{2,1},{3,2},{4,7},{5,4},{6,5},{7,6},{8,11},{9,8},{10,9... | collective-permute-start | bytes 294920 | tf_op jit(solution)/shard_map/ppermute | solution.py:284
  78.6 27.3 %collective-permute-start.11 = (bf16[5120,128]{1,0:T(8,128)(2,1)}, bf16[5120,128]{1,0:T(8,128)(2,1)S(1)}, u32[]{:S(2)}, u32[]{:S(2)}) collective-permute-start(bf16[5120,128]{1,0:T(8,128)(2,1)} %collective-permute-done.10.refs_4_), channel_id=1, source_target_pairs={{0,32},{1,33},{2,34},{3,35},{4,36},{5,37},{6,38},{7,39},{8,40},{9,... | collective-permute-start | bytes 3932168 | tf_op jit(solution)/shard_map/ppermute | solution.py:284
  78.6 31.1 %copy-start.4 = (bf16[64,5120]{1,0:T(8,128)(2,1)}, bf16[64,5120]{1,0:T(8,128)(2,1)S(1)}, u32[]{:S(2)}) copy-start(bf16[64,5120]{1,0:T(8,128)(2,1)S(1)} %pad_maximum_fusion.refs_6_) | copy-start | bytes 1966084
  80.2 18.0 %collective-permute-start.15 = (bf16[64,5120]{1,0:T(8,128)(2,1)S(1)}, bf16[64,5120]{1,0:T(8,128)(2,1)S(1)}, u32[]{:S(2)}, u32[]{:S(2)}) collective-permute-start(bf16[64,5120]{1,0:T(8,128)(2,1)S(1)} %pad_maximum_fusion.refs_6_), channel_id=1, source_target_pairs={{0,8},{1,9},{2,10},{3,11},{4,12},{5,13},{6,14},{7,15},{8,16},{9,17... | collective-permute-start | bytes 1966088 | tf_op jit(solution)/shard_map/ppermute | solution.py:284
  81.7 16.6 %collective-permute-start.16 = (bf16[64,5120]{1,0:T(8,128)(2,1)S(1)}, bf16[64,5120]{1,0:T(8,128)(2,1)S(1)}, u32[]{:S(2)}, u32[]{:S(2)}) collective-permute-start(bf16[64,5120]{1,0:T(8,128)(2,1)S(1)} %pad_maximum_fusion.refs_6_), channel_id=1, source_target_pairs={{0,16},{1,17},{2,18},{3,19},{4,20},{5,21},{6,22},{7,23},{8,24},{9,... | collective-permute-start | bytes 1966088 | tf_op jit(solution)/shard_map/ppermute | solution.py:284
  94.0 9.7 %collective-permute-start.17 = (bf16[64,5120]{1,0:T(8,128)(2,1)S(1)}, bf16[64,5120]{1,0:T(8,128)(2,1)S(1)}, u32[]{:S(2)}, u32[]{:S(2)}) collective-permute-start(bf16[64,5120]{1,0:T(8,128)(2,1)S(1)} %pad_maximum_fusion.refs_6_), channel_id=1, source_target_pairs={{0,24},{1,25},{2,26},{3,27},{4,28},{5,29},{6,30},{7,31},{8,0},{9,1... | collective-permute-start | bytes 1966088 | tf_op jit(solution)/shard_map/ppermute | solution.py:284
  98.2 0.8 copy-start.8
  98.2 32.8 %collective-permute-start = (bf16[3072,128]{1,0:T(8,128)(2,1)S(1)}, bf16[3072,128]{1,0:T(8,128)(2,1)}, u32[]{:S(2)}, u32[]{:S(2)}) collective-permute-start(bf16[3072,128]{1,0:T(8,128)(2,1)S(1)} %get-tuple-element.8.refs_2_), channel_id=1, source_target_pairs={{0,32},{1,33},{2,34},{3,35},{4,36},{5,37},{6,38},{7,39},{8,40},{9,... | collective-permute-start | bytes 2359304 | tf_op jit(solution)/shard_map/ppermute | solution.py:284
  99.1 0.8 copy-start.9
  99.9 31.1 %collective-permute-start.2 = (bf16[3072,128]{1,0:T(8,128)(2,1)}, bf16[3072,128]{1,0:T(8,128)(2,1)}, u32[]{:S(2)}, u32[]{:S(2)}) collective-permute-start(bf16[3072,128]{1,0:T(8,128)(2,1)} %collective-permute-done.1.refs_4_), channel_id=1, source_target_pairs={{0,32},{1,33},{2,34},{3,35},{4,36},{5,37},{6,38},{7,39},{8,40},{9,... | collective-permute-start | bytes 2359304 | tf_op jit(solution)/shard_map/ppermute | solution.py:284
  102.2 28.7 %copy-start.5 = (bf16[64,3072]{1,0:T(8,128)(2,1)}, bf16[64,3072]{1,0:T(8,128)(2,1)S(1)}, u32[]{:S(2)}) copy-start(bf16[64,3072]{1,0:T(8,128)(2,1)S(1)} %pad_maximum_fusion.1.refs_6_) | copy-start | bytes 1179652
  103.8 2.1 %copy-start.10 = (bf16[64,5120]{1,0:T(8,128)(2,1)}, bf16[64,5120]{1,0:T(8,128)(2,1)S(1)}, u32[]{:S(2)}) copy-start(bf16[64,5120]{1,0:T(8,128)(2,1)S(1)} %collective-permute-done.17.refs_9_) | copy-start | bytes 1966084
  103.8 27.2 %collective-permute-start.6 = (bf16[64,3072]{1,0:T(8,128)(2,1)S(1)}, bf16[64,3072]{1,0:T(8,128)(2,1)S(1)}, u32[]{:S(2)}, u32[]{:S(2)}) collective-permute-start(bf16[64,3072]{1,0:T(8,128)(2,1)S(1)} %pad_maximum_fusion.1.refs_6_), channel_id=1, source_target_pairs={{0,8},{1,9},{2,10},{3,11},{4,12},{5,13},{6,14},{7,15},{8,16},{9,17... | collective-permute-start | bytes 1179656 | tf_op jit(solution)/shard_map/ppermute | solution.py:284
  103.8 2.1 %copy-start.6 = (bf16[5120,128]{1,0:T(8,128)(2,1)}, bf16[5120,128]{1,0:T(8,128)(2,1)S(1)}, u32[]{:S(2)}) copy-start(bf16[5120,128]{1,0:T(8,128)(2,1)S(1)} %collective-permute-done.9.refs_3_) | copy-start | bytes 3932164
  103.8 27.2 %collective-permute-start.7 = (bf16[64,3072]{1,0:T(8,128)(2,1)S(1)}, bf16[64,3072]{1,0:T(8,128)(2,1)S(1)}, u32[]{:S(2)}, u32[]{:S(2)}) collective-permute-start(bf16[64,3072]{1,0:T(8,128)(2,1)S(1)} %pad_maximum_fusion.1.refs_6_), channel_id=1, source_target_pairs={{0,16},{1,17},{2,18},{3,19},{4,20},{5,21},{6,22},{7,23},{8,24},{9,... | collective-permute-start | bytes 1179656 | tf_op jit(solution)/shard_map/ppermute | solution.py:284
  105.9 1.1 copy-start.7
  106.9 24.0 %collective-permute-start.8 = (bf16[64,3072]{1,0:T(8,128)(2,1)S(1)}, bf16[64,3072]{1,0:T(8,128)(2,1)S(1)}, u32[]{:S(2)}, u32[]{:S(2)}) collective-permute-start(bf16[64,3072]{1,0:T(8,128)(2,1)S(1)} %pad_maximum_fusion.1.refs_6_), channel_id=1, source_target_pairs={{0,24},{1,25},{2,26},{3,27},{4,28},{5,29},{6,30},{7,31},{8,0},{9,1... | collective-permute-start | bytes 1179656 | tf_op jit(solution)/shard_map/ppermute | solution.py:284
  130.9 0.8 copy-start.11
  130.9 0.9 copy-start.12
  131.0 1.0 copy-start.13

commit v3 on v2

--- a/solution.py
+++ b/solution.py
@@ -41,106 +41,171 @@
     return out.astype(ml_dtypes.bfloat16)
 
 
+def cost(us):
+    return pl.CostEstimate(flops=int(us * 1.1e9), transcendentals=0, bytes_accessed=1 << 20)
+
+
 DBLK = 25
-
-
-def spectra_kernel(half, x_ref, start_ref, qual_ref, flag_ref, hot_ref, y0_ref, y1_ref, sel_ref, y_ref, state, table, spec, power):
+CHUNKS = (576, 448)
+
+
+def spectra_kernel(half, me_ref, x_hbm, start_ref, qual_ref, y0_ref, y1_ref, y_ref, x_ref, state, table, spec, power, sem):
     ngrp = half // GRP
+    length = 2 * half
+    blocks = ngrp // DBLK
+    load = pltpu.make_async_copy(x_hbm, x_ref, sem)
+    load.start()
+
+    def gen(slot):
+        for lo in range(0, length, 128):
+            cols = slice(lo, min(lo + 128, length))
+            cos, sin = state[0, :, cols], state[1, :, cols]
+            rc, rs = start_ref[2, :, cols], start_ref[3, :, cols]
+            for n in range(DBLK):
+                table[slot, n * 16 : n * 16 + 16, cols] = jnp.concatenate([cos, sin], axis=0).astype(jnp.bfloat16)
+                cos, sin = cos * rc + sin * rs, sin * rc - cos * rs
+            state[0, :, cols] = cos
+            state[1, :, cols] = sin
+
     state[0] = start_ref[0]
     state[1] = start_ref[1]
     power[...] = jnp.zeros_like(power)
-    x01 = [x_ref[g] for g in range(4)]
-    samples = jnp.concatenate(x01, axis=1)
-
-    def gen(n, _):
-        cos, sin = state[0], state[1]
-        table[pl.ds(pl.multiple_of(n * 16, 16), 16), :] = jnp.concatenate([cos, sin], axis=0).astype(jnp.bfloat16)
-        rc, rs = start_ref[2], start_ref[3]
-        state[0] = cos * rc + sin * rs
-        state[1] = sin * rc - cos * rs
+    gen(0)
+    load.wait()
+    samples = jnp.concatenate([x_ref[g] for g in range(4)], axis=1)
+
+    def block(b, _):
+        slot = b % 2
+        prod = jnp.dot(table[slot], samples, preferred_element_type=jnp.float32)
+        gen(1 - slot)
+        spec[pl.ds(pl.multiple_of(b * (DBLK * 16), DBLK * 16), DBLK * 16), :] = prod
+        power[...] += jnp.sum((prod * prod).reshape(DBLK * 2, 8, 512), axis=0)
         return 0
 
-    def block(b, _):
-        lax.fori_loop(0, DBLK, gen, 0)
-        prod = jnp.dot(table[...], samples, preferred_element_type=jnp.float32)
-        spec[pl.ds(pl.multiple_of(b * (DBLK * 16), DBLK * 16), DBLK * 16), :] = prod
-        sq = prod * prod
-        power[...] += jnp.sum(sq.reshape(DBLK * 2, 8, 512), axis=0)
-        return 0
-
-    lax.fori_loop(0, ngrp // DBLK, block, 0)
+    lax.fori_loop(0, blocks, block, 0)
     mean = jnp.sum(power[...], axis=0, keepdims=True) * (1.0 / half)
     level2 = 0.25 * (mean + 1e-06)
-
-    def white(n, _):
+    own = [qual_ref[pl.ds(me_ref[0] * 4 + g, 1), :].astype(jnp.float32) for g in range(4)]
+
+    def whiten(n, part_ref, m):
         base = pl.multiple_of(n * 16, 16)
-        real = spec[pl.ds(base, 8), :]
-        imag = spec[pl.ds(base + 8, 8), :]
-        inv = lax.rsqrt(jnp.maximum(real * real + imag * imag, level2)) * qual_ref[...]
-        parts = []
-        for value in (real * inv, imag * inv):
-            for g in range(4):
-                parts.append(value[:, g * 128 : (g + 1) * 128])
-        y_ref[pl.ds(pl.multiple_of(n * ROWS, ROWS), ROWS), :] = jnp.concatenate(parts, axis=0).astype(jnp.bfloat16)
-        return 0
-
-    lax.fori_loop(0, ngrp, white, 0)
-    y_ref[pl.ds(ngrp * ROWS, (NGRP - ngrp) * ROWS), :] = jnp.zeros(((NGRP - ngrp) * ROWS, 128), jnp.bfloat16)
-    y_ref[pl.ds((NGRP - 1) * ROWS, 16), :] = flag_ref[...].astype(jnp.bfloat16)
-    y0_ref[...] = y_ref[: CHUNKS[0] * 8, :]
-    y1_ref[...] = y_ref[CHUNKS[0] * 8 :, :]
-    picked = lax.dot_general(
-        hot_ref[...], y_ref[...], (((1,), (1,)), ((), ())), preferred_element_type=jnp.float32
-    )
-    sel_ref[...] = picked.astype(jnp.bfloat16)
-
-
-def spectra(samples, qual, flags, onehot):
+        reals, imags = [], []
+        for g in range(4):
+            cols = slice(g * 128, (g + 1) * 128)
+            real = spec[pl.ds(base, 8), cols]
+            imag = spec[pl.ds(base + 8, 8), cols]
+            inv = lax.rsqrt(jnp.maximum(real * real + imag * imag, level2[:, cols])) * own[g]
+            reals.append(real * inv)
+            imags.append(imag * inv)
+        value = jnp.concatenate(reals + imags, axis=0).astype(jnp.bfloat16)
+        part_ref[pl.ds(pl.multiple_of(m * ROWS, ROWS), ROWS), :] = value
+        y_ref[pl.ds(pl.multiple_of(n * ROWS, ROWS), ROWS), :] = value
+
+    first = CHUNKS[0] // GRP
+
+    def sweep(lo, hi, part_ref):
+        def some(m, _):
+            for v in range(4):
+                whiten(lo + m * 4 + v, part_ref, m * 4 + v)
+            return 0
+
+        lax.fori_loop(0, (hi - lo) // 4, some, 0)
+        for n in range(hi - (hi - lo) % 4, hi):
+            whiten(n, part_ref, n - lo)
+
+    sweep(0, first, y0_ref)
+    sweep(first, ngrp, y1_ref)
+    tail = (ngrp - first) * ROWS
+    for ref in (y1_ref, y_ref):
+        rows = ref.shape[0]
+        ref[rows - CHUNKS[1] * 8 + tail :, :] = jnp.zeros((CHUNKS[1] * 8 - tail, 128), jnp.bfloat16)
+        ref[rows - ROWS : rows - ROWS + 16, :] = qual_ref[...].astype(jnp.float32).astype(jnp.bfloat16)
+
+
+def spectra(samples, qual_t, me):
     length = samples.shape[1]
     half = length // 2
     start = jnp.asarray(start_tables(length))
+    vmem = pl.BlockSpec(memory_space=pltpu.VMEM)
     return pl.pallas_call(
         functools.partial(spectra_kernel, half),
         out_shape=[
             jax.ShapeDtypeStruct((CHUNKS[0] * 8, 128), jnp.bfloat16),
             jax.ShapeDtypeStruct((CHUNKS[1] * 8, 128), jnp.bfloat16),
-            jax.ShapeDtypeStruct((8, NGRP * ROWS), jnp.bfloat16),
+            jax.ShapeDtypeStruct((NGRP * ROWS, 128), jnp.bfloat16),
         ],
+        in_specs=[pl.BlockSpec(memory_space=pltpu.SMEM), pl.BlockSpec(memory_space=pl.ANY), vmem, vmem],
+        out_specs=[vmem, vmem, vmem],
         scratch_shapes=[
-            pltpu.VMEM((NGRP * ROWS, 128), jnp.bfloat16),
+            pltpu.VMEM((4, length, 128), jnp.bfloat16),
             pltpu.VMEM((2, 8, length), jnp.float32),
-            pltpu.VMEM((DBLK * 16, length), jnp.bfloat16),
+            pltpu.VMEM((2, DBLK * 16, length), jnp.bfloat16),
             pltpu.VMEM((2 * half, 512), jnp.float32),
             pltpu.VMEM((8, 512), jnp.float32),
+            pltpu.SemaphoreType.DMA,
         ],
         compiler_params=pltpu.CompilerParams(vmem_limit_bytes=48 * MB),
+        cost_estimate=cost(10),
         name="spectra",
-    )(samples, start, qual, flags, onehot)
+    )(me, samples, start, qual_t)
+
+
+def select_kernel(me_ref, ia, ib, ic, id_, y_ref, out_ref):
+    me, r = me_ref[0], me_ref[1]
+    row = lax.broadcasted_iota(jnp.int32, (16, 128), 0)
+    lane = lax.broadcasted_iota(jnp.int32, (16, 128), 1)
+    hot = jnp.zeros((16, 128), jnp.float32)
+    for rel, ref in enumerate((ia, ib, ic, id_)):
+        group = jnp.bitwise_xor(me, rel)
+        for h in range(2):
+            here = (row // 4 == group) & (row % 2 == h) & (lane == ref[r + 32 * h] - r * 128)
+            hot = jnp.where(here, 1.0, hot)
+    hot = hot.astype(jnp.bfloat16)
+    picked = lax.dot_general(hot, y_ref[...], (((1,), (1,)), ((), ())), preferred_element_type=jnp.float32)
+    out_ref[...] = picked.astype(jnp.bfloat16)
+
+
+def select(where, lists, y):
+    smem = pl.BlockSpec(memory_space=pltpu.SMEM)
+    vmem = pl.BlockSpec(memory_space=pltpu.VMEM)
+    return pl.pallas_call(
+        select_kernel,
+        out_shape=jax.ShapeDtypeStruct((16, NGRP * ROWS), jnp.bfloat16),
+        in_specs=[smem] * 5 + [vmem],
+        out_specs=vmem,
+        compiler_params=pltpu.CompilerParams(vmem_limit_bytes=16 * MB),
+        cost_estimate=cost(2),
+        name="select",
+    )(where, *lists, y)
 
 
 UNROLL = 4
-CHUNKS = (640, 384)
-
-
-def correlate_kernel(first, last, kc, *refs):
+HEAD = 128
+
+
+def correlate_kernel(first, last, kc, offset, *refs):
     where_ref, seg_ref, ya, yb, yc, yd, xa, xb, xc, xd, lag_ref, qual_ref = refs[:12]
     if first:
         out_ref, ybuf, xbuf, xrow, cross, sems = refs[12:]
         acc_ref = None
     else:
         acc_hbm, out_ref, ybuf, xbuf, xrow, cross, sems, acc_ref, scale, stage, osem = refs[12:]
+    parts = ((0, HEAD), (HEAD, kc - HEAD))
     copies = []
-    for j, ref in enumerate((ya, yb, yc, yd)):
-        copies.append(pltpu.make_async_copy(ref, ybuf.at[seg_ref[j]], sems.at[j]))
-    for j, ref in enumerate((xa, xb, xc, xd)):
-        copies.append(pltpu.make_async_copy(ref, xbuf.at[j], sems.at[4 + j]))
-    for copy in copies:
-        copy.start()
+    for k, (lo, size) in enumerate(parts):
+        span = pl.ds(lo * 8, size * 8)
+        some = []
+        for j, ref in enumerate((ya, yb, yc, yd)):
+            rows = span if j >= 2 else pl.ds((offset + lo) * 8, size * 8)
+            some.append(pltpu.make_async_copy(ref.at[rows], ybuf.at[seg_ref[j], span], sems.at[k * 8 + j]))
+        for j, ref in enumerate((xa, xb, xc, xd)):
+            some.append(pltpu.make_async_copy(ref.at[:, span], xbuf.at[j, :, span], sems.at[k * 8 + 4 + j]))
+        copies.append(some)
+        for copy in some:
+            copy.start()
     if not first:
-        prefetch = pltpu.make_async_copy(acc_hbm, acc_ref, sems.at[8])
+        prefetch = pltpu.make_async_copy(acc_hbm, acc_ref, sems.at[16])
         prefetch.start()
-    for copy in copies:
-        copy.wait()
 
     rowid = lax.broadcasted_iota(jnp.int32, (16, 256), 0) % GRP
     lane = lax.broadcasted_iota(jnp.int32, (16, 256), 1) % GRP
@@ -188,7 +253,10 @@
             pair(m * UNROLL + v, v)
         return 0
 
-    lax.fori_loop(0, kc // 16 // UNROLL, pairs, 0)
+    for (lo, size), some in zip(parts, copies):
+        for copy in some:
+            copy.wait()
+        lax.fori_loop(lo // 16 // UNROLL, (lo + size) // 16 // UNROLL, pairs, 0)
     table = lag_ref[...]
     if last:
         flags = []
@@ -196,7 +264,8 @@
             for near in range(4):
                 flags.append(xbuf[far, near * 16 : near * 16 + 4, kc * 8 - 128 :])
         flags = jnp.concatenate([f.astype(jnp.float32) for f in flags], axis=0)[:, 64:80].astype(jnp.bfloat16)
-        count = jnp.dot(flags, qual_ref[...], preferred_element_type=jnp.float32)
+        quality = qual_ref[...].astype(jnp.float32).astype(jnp.bfloat16)
+        count = jnp.dot(flags, quality, preferred_element_type=jnp.float32)
         scale[...] = 1.0 / jnp.maximum(count, 1.0)
         prefetch.wait()
 
@@ -231,7 +300,7 @@
         flush(7, 1).wait()
 
 
-def correlate(first, last, kc, where, seg, ys, xs, table, qual_t, acc=None):
+def correlate(first, last, kc, offset, where, seg, ys, xs, table, qual_t, acc=None):
     smem = pl.BlockSpec(memory_space=pltpu.SMEM)
     hbm = pl.BlockSpec(memory_space=pl.ANY)
     vmem = pl.BlockSpec(memory_space=pltpu.VMEM)
@@ -242,7 +311,7 @@
         pltpu.VMEM((4, 64, kc * 8), jnp.bfloat16),
         pltpu.VMEM((UNROLL, 128, 256), jnp.float32),
         pltpu.VMEM((64, 2 * kc, 128), jnp.bfloat16),
-        pltpu.SemaphoreType.DMA((9,)),
+        pltpu.SemaphoreType.DMA((17,)),
     ]
     if first:
         out_shape, out_specs = (64, TAU, 128), vmem
@@ -257,12 +326,13 @@
             pltpu.SemaphoreType.DMA((2,)),
         ]
     return pl.pallas_call(
-        functools.partial(correlate_kernel, first, last, kc),
+        functools.partial(correlate_kernel, first, last, kc, offset),
         out_shape=jax.ShapeDtypeStruct(out_shape, jnp.float32),
         in_specs=in_specs,
         out_specs=out_specs,
         scratch_shapes=scratch,
         compiler_params=pltpu.CompilerParams(vmem_limit_bytes=60 * MB),
+        cost_estimate=cost(kc / 40),
         name="correlate_first" if first else "correlate_last",
     )(*args)
 
@@ -301,53 +371,53 @@
     return move
 
 
+def both(zhi, core, y, zlo, x):
+    return zhi + 1, core + 1, y, zlo, x
+
+
 def on_device(traces, src_index, quality):
-    rows = traces.shape[0]
     samples = jnp.transpose(traces, (1, 2, 0))
-    qual_f = jnp.transpose(quality, (1, 0)).astype(jnp.float32)
+    qual_t = jnp.transpose(quality, (1, 0))
     zhi, core, yy, zlo, xx = [lax.axis_index(a) for a in AXES]
     me = zhi * 2 + core
-    r = yy * 8 + zlo * 4 + xx
-    qual_own = lax.dynamic_slice_in_dim(qual_f, me * 4, 4, axis=0).reshape(1, 512)
-    index_all = lax.all_gather(src_index, ("zhi", "core"), axis=0, tiled=False)
-    mine = lax.dynamic_slice_in_dim(index_all.reshape(4, 2, 32), r, 1, axis=2).reshape(8) - r * rows
-    onehot = (mine[:, None] == jnp.arange(rows, dtype=jnp.int32)[None, :]).astype(jnp.bfloat16)
+    spot = jnp.stack([me, yy * 8 + zlo * 4 + xx])
+    i = jnp.arange(64, dtype=jnp.int32)
+    dx, dy = (xx - i % 4) % 4, (yy - (i // 8) % 4) % 4
+    dx, dy = dx % 2 * 2 + dx // 2, dy % 2 * 2 + dy // 2
+    far_step, near_step = jnp.where(core == 0, dy, dx), jnp.where(core == 0, dx, dy)
+    where = far_step * 16 + near_step * 4 + (i // 4) % 2 * 2 + i // 32
+    seg = jnp.bitwise_xor(me, jnp.arange(4, dtype=jnp.int32))
     table = lag_table(1000)
     tables, start = [], 0
     for kc in CHUNKS:
         tables.append(jnp.asarray(np.ascontiguousarray(table[:, :, start : start + kc]).reshape(TAU, 2 * kc)))
         start += kc
 
-    y0, y1, sel = spectra(samples, qual_own, qual_f, onehot)
-    ys0 = [y0]
-    ys1 = [y1]
+    lists = [src_index] + [send(src_index, move) for move in (sibling, across, both)]
+    y0, y1, y = spectra(samples, qual_t, spot)
+
+    slots = select(spot, lists, y).reshape(8, 2, -1)
+    got = lax.all_to_all(slots, ("zhi", "core", "zlo"), 0, 0, tiled=False)
+    y0, y1, y, got = lax.optimization_barrier((y0, y1, y, got))
+    got = got.reshape(16, -1)
     far0 = send(y0, across)
     far1 = send(y1, across)
-    near0, near1 = send(y0, sibling), send(y1, sibling)
-
-    sel = sel.reshape(4, 1, 2, -1)
-    slots = jnp.broadcast_to(sel, (4, 2, 2, sel.shape[-1])).reshape(8, 2, -1)
-    got = lax.all_to_all(slots, ("zhi", "core", "zlo"), 0, 0, tiled=False)
-    got = got.reshape(16, -1)
-    xs = []
-    start = 0
+    pieces = [got] + [send(got, ring(0, d)) for d in (2, 1, 3)]
+    *pieces, y = lax.optimization_barrier((*pieces, y))
+    near = send(y, sibling)
+    lines, start = [], 0
     for kc in CHUNKS:
-        own = got[:, start * 8 : (start + kc) * 8]
+        lines.append(jnp.concatenate([piece[:, start * 8 : (start + kc) * 8] for piece in pieces], axis=0))
         start += kc
-        line = jnp.concatenate([own] + [send(own, ring(0, d)) for d in (1, 2, 3)], axis=0)
-        xs.append([line] + [send(line, ring(1, d)) for d in (1, 2, 3)])
-
-    i = jnp.arange(64, dtype=jnp.int32)
-    dx, dy = (xx - i % 4) % 4, (yy - (i // 8) % 4) % 4
-    far_step, near_step = jnp.where(core == 0, dy, dx), jnp.where(core == 0, dx, dy)
-    where = far_step * 16 + near_step * 4 + (i // 4) % 2 * 2 + i // 32
-    seg = jnp.bitwise_xor(me, jnp.arange(4, dtype=jnp.int32))
-    qual_b = qual_f.astype(jnp.bfloat16)
+    xs0 = [lines[0]] + [send(lines[0], ring(1, d)) for d in (2, 1, 3)]
+    *xs0, line1, far0 = lax.optimization_barrier((*xs0, lines[1], far0))
+    xs1 = [line1] + [send(line1, ring(1, d)) for d in (2, 1, 3)]
     acc = correlate(
-        True, False, CHUNKS[0], where, seg, (y0, near0, far0, send(far0, sibling)), xs[0], tables[0], qual_b
+        True, False, CHUNKS[0], 0, where, seg, (y, near, far0, send(far0, sibling)), xs0, tables[0], qual_t
     )
+    far1, acc, *xs1 = lax.optimization_barrier((far1, acc, *xs1))
     out = correlate(
-        False, True, CHUNKS[1], where, seg, (y1, near1, far1, send(far1, sibling)), xs[1], tables[1], qual_b, acc
+        False, True, CHUNKS[1], CHUNKS[0], where, seg, (y, near, far1, send(far1, sibling)), xs1, tables[1], qual_t, acc
     )
     return jnp.transpose(out, (1, 0, 2))
 

time: 149 us -> 116 us (0.78); the launches traced: 146 us -> 116 us
  blocking collectives: 40.3 us -> 11.5 us
  Pallas kernels: 47 us -> 44.7 us
    all_to_all x1, blocking collectives: 32.9 us -> 11.5 us  [on_device(): got = lax.all_to_all(slots, ('zhi', 'core', 'zlo'), 0, 0, tiled=False)]
    unnamed x1 -> x0, blocking collectives: 7.44 us -> none
    pallas_call x1, Pallas kernels: 11.4 us -> 9.69 us  [spectra(): pl.pallas_call(functools.partial(spectra_kernel, half), out_shape=[jax.Sh...]
    ppermute x18 -> x17, starting transfers between devices: 21.5 us -> 22.2 us  [send(): return lax.ppermute(value, AXES, permutation(move))]
    pallas_call x2 -> x3, Pallas kernels: 35.6 us -> 35 us  [the longest x2 33.8 us: correlate(): pl.pallas_call(functools.partial(correlate_kernel, first, last, kc, offse...]
    ppermute x18 -> x17, waiting for transfers between devices: 25.2 us -> 25.6 us  [send(): return lax.ppermute(value, AXES, permutation(move))]
    unnamed x31 -> x28, local copies, waits for them, and re-layouts: 8.31 us -> 8.48 us
  transfers between devices with their start and end apart: 18 -> 17, of which waited for: 6 -> 6; matrix products, arithmetic and copies ran while one was open for 1% -> 2% of each run, Pallas kernels for 14% -> 24%
where the time goes in v3:
time: 116 us
  Pallas kernels  44.7 us (39%)
  waiting for transfers between devices  25.6 us (22%)
  starting transfers between devices  22.2 us (19%)
  blocking collectives  11.5 us (10%)
  local copies, waits for them, and re-layouts  9.82 us (8%)
  other arithmetic  2.05 us (2%)
    pallas_call x2, Pallas kernels, correlate(): pl.pallas_call(functools.partial(correlate_kernel, first, last, kc, offse...  33.8 us
    ppermute x17, waiting for transfers between devices, send(): return lax.ppermute(value, AXES, permutation(move))  25.6 us
    ppermute x17, starting transfers between devices, send(): return lax.ppermute(value, AXES, permutation(move))  22.2 us
    all_to_all x1, blocking collectives, on_device(): got = lax.all_to_all(slots, ('zhi', 'core', 'zlo'), 0, 0, tiled=False)  11.5 us
    pallas_call x1, Pallas kernels, spectra(): pl.pallas_call(functools.partial(spectra_kernel, half), out_shape=[jax.Sh...  9.69 us
    unnamed x28, local copies, waits for them, and re-layouts  8.48 us
  transfers between devices with their start and end apart: 17, of which 6 were waited for; matrix products, arithmetic and copies ran while one was open for 2% of the time, Pallas kernels for 24%

profile of v3, /device:TPU:1, one launch (start us, length us, event | category | flops | bytes accessed | tf_op | source)
XLA Modules:
  0.0 116.1 jit_solution(11088334391670534732)
XLA Ops:
  0.0 4.4 %collective-permute-start.1 = (s32[64]{0:T(128)}, s32[64]{0:T(128)S(1)}, u32[]{:S(2)}, u32[]{:S(2)}) collective-permute-start(s32[64]{0:T(128)} %ia.1), channel_id=1, source_target_pairs={{0,64},{1,65},{2,66},{3,67},{4,68},{5,69},{6,70},{7,71},{8,72},{9,... | collective-permute-start | bytes 776 | tf_op jit(solution)/shard_map/ppermute | solution.py:354
  4.4 1.0 collective-permute-start
  5.4 0.0 collective-permute-start.2
  5.4 0.1 pad_add_fusion.me_ref
  5.5 1.6 %copy-done.2 = bf16[128,4,2000]{0,2,1:T(8,128)(2,1)S(1)} copy-done((bf16[128,4,2000]{0,2,1:T(8,128)(2,1)S(1)}, bf16[128,4,2000]{0,2,1:T(8,128)(2,1)}, u32[]{:S(2)}) %copy-start.2) | copy-done | bytes 2048024
  7.0 0.7 copy-done.4
  7.7 0.9 copy-done.6
  8.7 9.7 %spectra.1 = (bf16[4608,128]{1,0:T(8,128)(2,1)S(1)}, bf16[3584,128]{1,0:T(8,128)(2,1)S(1)}, bf16[8192,128]{1,0:T(8,128)(2,1)}) custom-call(s32[2]{0:T(128)S(1)} %pad_add_fusion.me_ref, bf16[4,2000,128]{2,1,0:T(8,128)(2,1)S(1)} %bitcast.5, f32[4,8,2000]{2,1,0:T(8,128)S(1)} %copy-done.6, s32[16,128]{1,0:T(8,128)S(1)} %bitcast.8), custom_call_target="tpu_custom_call" | custom-call | flops 11000000512 | bytes 1048576 | tf_op jit(solution)/shard_map/spectra/pallas_call | solution.py:130
  18.4 1.0 copy-done.3
  19.4 0.0 collective-permute-done.ib
  19.4 0.0 collective-permute-done.2.id_
  19.4 1.6 %copy-done = bf16[8192,128]{1,0:T(8,128)(2,1)S(1)} copy-done((bf16[8192,128]{1,0:T(8,128)(2,1)S(1)}, bf16[8192,128]{1,0:T(8,128)(2,1)}, u32[]{:S(2)}) %copy-start) | copy-done | bytes 2097176
  21.0 1.2 %select.35 = bf16[16,8192]{1,0:T(8,128)(2,1)S(1)} custom-call(s32[2]{0:T(128)S(1)} %pad_add_fusion.me_ref, s32[64]{0:T(128)S(1)} %copy-done.5, s32[64]{0:T(128)S(1)} %collective-permute-done.ib, s32[64]{0:T(128)S(1)} %collective-permute-done.1.ic, s32[64]{0:T(128)S(1)} %collective-permute-done.2.id_, bf16[8192,128]{1,0:T(8,128)(2,1)S(1)} %copy-done), custom_call_target="tpu_custom_call" | custom-call | flops 2200000000 | bytes 1048576 | tf_op jit(solution)/shard_map/select/pallas_call | solution.py:171
  22.2 0.2 reshape.6
  22.4 11.5 %all_to_all.5 = bf16[8,2,8192]{2,1,0:T(2,128)(2,1)} all-to-all(bf16[8,2,8192]{2,1,0:T(2,128)(2,1)S(1)} %reshape.6), channel_id=1, replica_groups=mesh['zhi'=2,'core'=2,'y'=4,'zlo'=2,'x'=4] {'zhi','core','zlo'}, dimensions={0} | all-to-all | bytes 524288 | tf_op jit(solution)/shard_map/all_to_all | solution.py:400
  33.9 1.0 reshape.7
  35.0 2.8 %collective-permute-start.5 = (bf16[16,8192]{1,0:T(8,128)(2,1)S(1)}, bf16[16,8192]{1,0:T(8,128)(2,1)S(1)}, u32[]{:S(2)}, u32[]{:S(2)}) collective-permute-start(bf16[16,8192]{1,0:T(8,128)(2,1)S(1)} %reshape.7), channel_id=1, source_target_pairs={{0,3},{1,0},{2,1},{3,2},{4,7},{5,4},{6,5},{7,6},{8,11},{9,8},{10,9... | collective-permute-start | bytes 786440 | tf_op jit(solution)/shard_map/ppermute | solution.py:354
  37.8 0.0 collective-permute-start.4
  37.8 1.6 %collective-permute-start.3 = (bf16[16,8192]{1,0:T(8,128)(2,1)S(1)}, bf16[16,8192]{1,0:T(8,128)(2,1)S(1)}, u32[]{:S(2)}, u32[]{:S(2)}) collective-permute-start(bf16[16,8192]{1,0:T(8,128)(2,1)S(1)} %reshape.7), channel_id=1, source_target_pairs={{0,2},{1,3},{2,0},{3,1},{4,6},{5,7},{6,4},{7,5},{8,10},{9,11},{10,... | collective-permute-start | bytes 786440 | tf_op jit(solution)/shard_map/ppermute | solution.py:354
  39.4 1.0 collective-permute-start.11
  40.4 0.7 collective-permute-done.5
  41.1 6.3 %collective-permute-done.4 = bf16[16,8192]{1,0:T(8,128)(2,1)S(1)} collective-permute-done((bf16[16,8192]{1,0:T(8,128)(2,1)S(1)}, bf16[16,8192]{1,0:T(8,128)(2,1)S(1)}, u32[]{:S(2)}, u32[]{:S(2)}) %collective-permute-start.4) | collective-permute-done | bytes 262176 | tf_op jit(solution)/shard_map/ppermute | solution.py:354
  47.4 0.0 collective-permute-done.3
  47.5 2.0 %collective-permute-start.6 = (bf16[8192,128]{1,0:T(8,128)(2,1)S(1)}, bf16[8192,128]{1,0:T(8,128)(2,1)}, u32[]{:S(2)}, u32[]{:S(2)}) collective-permute-start(bf16[8192,128]{1,0:T(8,128)(2,1)S(1)} %copy-done.1), channel_id=1, source_target_pairs={{0,32},{1,33},{2,34},{3,35},{4,36},{5,37},{6,38},{7,39},{8,40},{9,... | collective-permute-start | bytes 6291464 | tf_op jit(solution)/shard_map/ppermute | solution.py:354
  49.6 0.6 collective-permute-start.10
  50.2 0.9 collective-permute-start.9
  51.1 0.8 collective-permute-start.8
  52.0 0.8 pad_maximum_fusion.1.refs_6_
  52.8 6.0 %collective-permute-done.10.refs_9_ = bf16[64,4608]{1,0:T(8,128)(2,1)S(1)} collective-permute-done((bf16[64,4608]{1,0:T(8,128)(2,1)S(1)}, bf16[64,4608]{1,0:T(8,128)(2,1)S(1)}, u32[]{:S(2)}, u32[]{:S(2)}) %collective-permute-start.10) | collective-permute-done | bytes 589856 | tf_op jit(solution)/shard_map/ppermute | solution.py:354
  58.8 8.1 %collective-permute-done.9.refs_8_ = bf16[64,4608]{1,0:T(8,128)(2,1)S(1)} collective-permute-done((bf16[64,4608]{1,0:T(8,128)(2,1)S(1)}, bf16[64,4608]{1,0:T(8,128)(2,1)S(1)}, u32[]{:S(2)}, u32[]{:S(2)}) %collective-permute-start.9) | collective-permute-done | bytes 589856 | tf_op jit(solution)/shard_map/ppermute | solution.py:354
  66.9 0.8 copy-done.11
  67.7 0.2 copy-done.12
  67.9 3.2 %collective-permute-start.12 = (bf16[4608,128]{1,0:T(8,128)(2,1)}, bf16[4608,128]{1,0:T(8,128)(2,1)S(1)}, u32[]{:S(2)}, u32[]{:S(2)}) collective-permute-start(bf16[4608,128]{1,0:T(8,128)(2,1)} %collective-permute-done.11.refs_4_), channel_id=1, source_target_pairs={{0,32},{1,33},{2,34},{3,35},{4,36},{5,37},{6,38},{7,39},{8,40},{9,... | collective-permute-start | bytes 3538952 | tf_op jit(solution)/shard_map/ppermute | solution.py:354
  71.1 0.6 iota_xor_fusion.refs_1_
  71.7 0.6 fusion.refs_0_
  72.2 0.1 collective-permute-start.7
  72.4 1.4 %collective-permute-start.15 = (bf16[64,3584]{1,0:T(8,128)(2,1)}, bf16[64,3584]{1,0:T(8,128)(2,1)S(1)}, u32[]{:S(2)}, u32[]{:S(2)}) collective-permute-start(bf16[64,3584]{1,0:T(8,128)(2,1)} %pad_maximum_fusion.1.refs_6_), channel_id=1, source_target_pairs={{0,24},{1,25},{2,26},{3,27},{4,28},{5,29},{6,30},{7,31},{8,0},{9,1... | collective-permute-start | bytes 1376264 | tf_op jit(solution)/shard_map/ppermute | solution.py:354
  73.7 0.1 collective-permute-start.14
  73.9 1.4 %collective-permute-start.13 = (bf16[64,3584]{1,0:T(8,128)(2,1)}, bf16[64,3584]{1,0:T(8,128)(2,1)}, u32[]{:S(2)}, u32[]{:S(2)}) collective-permute-start(bf16[64,3584]{1,0:T(8,128)(2,1)} %pad_maximum_fusion.1.refs_6_), channel_id=1, source_target_pairs={{0,16},{1,17},{2,18},{3,19},{4,20},{5,21},{6,22},{7,23},{8,24},{9,... | collective-permute-start | bytes 1376264 | tf_op jit(solution)/shard_map/ppermute | solution.py:354
  75.2 0.0 collective-permute-done.6.refs_3_
  75.3 18.5 %correlate_first.1.refs_12_ = f32[64,208,128]{2,1,0:T(8,128)} custom-call(s32[64]{0:T(128)} %fusion.refs_0_, s32[4]{0:T(128)} %iota_xor_fusion.refs_1_, bf16[8192,128]{1,0:T(8,128)(2,1)} %get-tuple-element.34.y_ref.refs_2_, bf16[8192,128]{1,0:T(8,128)(2,1)} %collective-permute-done.6.refs_3_, bf16[4608,128]{1,0:T(8,128)(2,1)} %collective-permute-done.11.refs_4_, ...), custom_call_target="tpu_custom_call" | custom-call | flops 15840000000 | bytes 1048576 | tf_op jit(solution)/shard_map/correlate_first/pallas_call | solution.py:328
  93.8 2.2 %collective-permute-done.7.refs_4_ = bf16[3584,128]{1,0:T(8,128)(2,1)} collective-permute-done((bf16[3584,128]{1,0:T(8,128)(2,1)}, bf16[3584,128]{1,0:T(8,128)(2,1)}, u32[]{:S(2)}, u32[]{:S(2)}) %collective-permute-start.7) | collective-permute-done | bytes 917536 | tf_op jit(solution)/shard_map/ppermute | solution.py:354
  96.0 0.0 collective-permute-done.15.refs_9_
  96.1 0.8 copy-done.13
  96.8 0.8 collective-permute-start.16
  97.6 2.3 %collective-permute-done.16.refs_5_ = bf16[3584,128]{1,0:T(8,128)(2,1)S(1)} collective-permute-done((bf16[3584,128]{1,0:T(8,128)(2,1)}, bf16[3584,128]{1,0:T(8,128)(2,1)S(1)}, u32[]{:S(2)}, u32[]{:S(2)}) %collective-permute-start.16) | collective-permute-done | bytes 917536 | tf_op jit(solution)/shard_map/ppermute | solution.py:354
  99.9 0.9 copy-done.9
  100.8 15.3 %correlate_last.1 = f32[201,64,128]{2,1,0:T(8,128)} custom-call(s32[64]{0:T(128)} %fusion.refs_0_, s32[4]{0:T(128)} %iota_xor_fusion.refs_1_, bf16[8192,128]{1,0:T(8,128)(2,1)} %get-tuple-element.34.y_ref.refs_2_, bf16[8192,128]{1,0:T(8,128)(2,1)} %collective-permute-done.6.refs_3_, bf16[3584,128]{1,0:T(8,128)(2,1)} %collective-permute-done.7.refs_4_, ...), custom_call_target="tpu_custom_call" | custom-call | flops 12320000000 | bytes 1048576 | tf_op jit(solution)/shard_map/correlate_last/pallas_call | solution.py:328
  (34 shorter events, 0.2 us)
Async XLA Ops:
  0.0 19.4 %collective-permute-start.1 = (s32[64]{0:T(128)}, s32[64]{0:T(128)S(1)}, u32[]{:S(2)}, u32[]{:S(2)}) collective-permute-start(s32[64]{0:T(128)} %ia.1), channel_id=1, source_target_pairs={{0,64},{1,65},{2,66},{3,67},{4,68},{5,69},{6,70},{7,71},{8,72},{9,... | collective-permute-start | bytes 776 | tf_op jit(solution)/shard_map/ppermute | solution.py:354
  4.4 15.0 %collective-permute-start = (s32[64]{0:T(128)}, s32[64]{0:T(128)S(1)}, u32[]{:S(2)}, u32[]{:S(2)}) collective-permute-start(s32[64]{0:T(128)} %ia.1), channel_id=1, source_target_pairs={{0,32},{1,33},{2,34},{3,35},{4,36},{5,37},{6,38},{7,39},{8,40},{9,... | collective-permute-start | bytes 776 | tf_op jit(solution)/shard_map/ppermute | solution.py:354
  5.4 14.0 %collective-permute-start.2 = (s32[64]{0:T(128)}, s32[64]{0:T(128)S(1)}, u32[]{:S(2)}, u32[]{:S(2)}) collective-permute-start(s32[64]{0:T(128)} %ia.1), channel_id=1, source_target_pairs={{0,96},{1,97},{2,98},{3,99},{4,100},{5,101},{6,102},{7,103},{8,104... | collective-permute-start | bytes 776 | tf_op jit(solution)/shard_map/ppermute | solution.py:354
  5.5 1.6 %copy-start.2 = (bf16[128,4,2000]{0,2,1:T(8,128)(2,1)S(1)}, bf16[128,4,2000]{0,2,1:T(8,128)(2,1)}, u32[]{:S(2)}) copy-start(bf16[128,4,2000]{0,2,1:T(8,128)(2,1)} %param.6) | copy-start | bytes 6144004
  7.0 0.7 copy-start.4
  7.7 0.9 copy-start.6
  8.7 10.7 %copy-start.5 = (s32[64]{0:T(128)S(1)}, s32[64]{0:T(128)}, u32[]{:S(2)}) copy-start(s32[64]{0:T(128)} %ia.1) | copy-start | bytes 772
  18.4 1.0 copy-start.3
  19.4 1.6 %copy-start = (bf16[8192,128]{1,0:T(8,128)(2,1)S(1)}, bf16[8192,128]{1,0:T(8,128)(2,1)}, u32[]{:S(2)}) copy-start(bf16[8192,128]{1,0:T(8,128)(2,1)} %get-tuple-element.34.y_ref.refs_2_) | copy-start | bytes 6291460
  22.4 25.1 %copy-start.1 = (bf16[8192,128]{1,0:T(8,128)(2,1)S(1)}, bf16[8192,128]{1,0:T(8,128)(2,1)}, u32[]{:S(2)}) copy-start(bf16[8192,128]{1,0:T(8,128)(2,1)} %get-tuple-element.34.y_ref.refs_2_) | copy-start | bytes 6291460
  35.0 6.1 %collective-permute-start.5 = (bf16[16,8192]{1,0:T(8,128)(2,1)S(1)}, bf16[16,8192]{1,0:T(8,128)(2,1)S(1)}, u32[]{:S(2)}, u32[]{:S(2)}) collective-permute-start(bf16[16,8192]{1,0:T(8,128)(2,1)S(1)} %reshape.7), channel_id=1, source_target_pairs={{0,3},{1,0},{2,1},{3,2},{4,7},{5,4},{6,5},{7,6},{8,11},{9,8},{10,9... | collective-permute-start | bytes 786440 | tf_op jit(solution)/shard_map/ppermute | solution.py:354
  37.8 9.6 %collective-permute-start.4 = (bf16[16,8192]{1,0:T(8,128)(2,1)S(1)}, bf16[16,8192]{1,0:T(8,128)(2,1)S(1)}, u32[]{:S(2)}, u32[]{:S(2)}) collective-permute-start(bf16[16,8192]{1,0:T(8,128)(2,1)S(1)} %reshape.7), channel_id=1, source_target_pairs={{0,1},{1,2},{2,3},{3,0},{4,5},{5,6},{6,7},{7,4},{8,9},{9,10},{10,1... | collective-permute-start | bytes 786440 | tf_op jit(solution)/shard_map/ppermute | solution.py:354
  37.8 9.6 %collective-permute-start.3 = (bf16[16,8192]{1,0:T(8,128)(2,1)S(1)}, bf16[16,8192]{1,0:T(8,128)(2,1)S(1)}, u32[]{:S(2)}, u32[]{:S(2)}) collective-permute-start(bf16[16,8192]{1,0:T(8,128)(2,1)S(1)} %reshape.7), channel_id=1, source_target_pairs={{0,2},{1,3},{2,0},{3,1},{4,6},{5,7},{6,4},{7,5},{8,10},{9,11},{10,... | collective-permute-start | bytes 786440 | tf_op jit(solution)/shard_map/ppermute | solution.py:354
  39.4 27.5 %collective-permute-start.11 = (bf16[4608,128]{1,0:T(8,128)(2,1)S(1)}, bf16[4608,128]{1,0:T(8,128)(2,1)}, u32[]{:S(2)}, u32[]{:S(2)}) collective-permute-start(bf16[4608,128]{1,0:T(8,128)(2,1)S(1)} %get-tuple-element.40), channel_id=1, source_target_pairs={{0,64},{1,65},{2,66},{3,67},{4,68},{5,69},{6,70},{7,71},{8,72},{9,... | collective-permute-start | bytes 3538952 | tf_op jit(solution)/shard_map/ppermute | solution.py:354
  47.5 27.8 %collective-permute-start.6 = (bf16[8192,128]{1,0:T(8,128)(2,1)S(1)}, bf16[8192,128]{1,0:T(8,128)(2,1)}, u32[]{:S(2)}, u32[]{:S(2)}) collective-permute-start(bf16[8192,128]{1,0:T(8,128)(2,1)S(1)} %copy-done.1), channel_id=1, source_target_pairs={{0,32},{1,33},{2,34},{3,35},{4,36},{5,37},{6,38},{7,39},{8,40},{9,... | collective-permute-start | bytes 6291464 | tf_op jit(solution)/shard_map/ppermute | solution.py:354
  49.6 17.3 %copy-start.7 = (bf16[64,4608]{1,0:T(8,128)(2,1)}, bf16[64,4608]{1,0:T(8,128)(2,1)S(1)}, u32[]{:S(2)}) copy-start(bf16[64,4608]{1,0:T(8,128)(2,1)S(1)} %pad_maximum_fusion.refs_6_) | copy-start | bytes 1769476
  49.6 9.2 %collective-permute-start.10 = (bf16[64,4608]{1,0:T(8,128)(2,1)S(1)}, bf16[64,4608]{1,0:T(8,128)(2,1)S(1)}, u32[]{:S(2)}, u32[]{:S(2)}) collective-permute-start(bf16[64,4608]{1,0:T(8,128)(2,1)S(1)} %pad_maximum_fusion.refs_6_), channel_id=1, source_target_pairs={{0,24},{1,25},{2,26},{3,27},{4,28},{5,29},{6,30},{7,31},{8,0},{9,1... | collective-permute-start | bytes 1769480 | tf_op jit(solution)/shard_map/ppermute | solution.py:354
  50.2 16.7 %collective-permute-start.9 = (bf16[64,4608]{1,0:T(8,128)(2,1)S(1)}, bf16[64,4608]{1,0:T(8,128)(2,1)S(1)}, u32[]{:S(2)}, u32[]{:S(2)}) collective-permute-start(bf16[64,4608]{1,0:T(8,128)(2,1)S(1)} %pad_maximum_fusion.refs_6_), channel_id=1, source_target_pairs={{0,8},{1,9},{2,10},{3,11},{4,12},{5,13},{6,14},{7,15},{8,16},{9,17... | collective-permute-start | bytes 1769480 | tf_op jit(solution)/shard_map/ppermute | solution.py:354
  51.1 15.8 %collective-permute-start.8 = (bf16[64,4608]{1,0:T(8,128)(2,1)S(1)}, bf16[64,4608]{1,0:T(8,128)(2,1)S(1)}, u32[]{:S(2)}, u32[]{:S(2)}) collective-permute-start(bf16[64,4608]{1,0:T(8,128)(2,1)S(1)} %pad_maximum_fusion.refs_6_), channel_id=1, source_target_pairs={{0,16},{1,17},{2,18},{3,19},{4,20},{5,21},{6,22},{7,23},{8,24},{9,... | collective-permute-start | bytes 1769480 | tf_op jit(solution)/shard_map/ppermute | solution.py:354
  58.8 8.1 %copy-start.10 = (bf16[64,4608]{1,0:T(8,128)(2,1)}, bf16[64,4608]{1,0:T(8,128)(2,1)S(1)}, u32[]{:S(2)}) copy-start(bf16[64,4608]{1,0:T(8,128)(2,1)S(1)} %collective-permute-done.10.refs_9_) | copy-start | bytes 1769476
  66.9 0.8 copy-start.11
  66.9 1.0 copy-start.12
  67.9 6.0 %collective-permute-start.12 = (bf16[4608,128]{1,0:T(8,128)(2,1)}, bf16[4608,128]{1,0:T(8,128)(2,1)S(1)}, u32[]{:S(2)}, u32[]{:S(2)}) collective-permute-start(bf16[4608,128]{1,0:T(8,128)(2,1)} %collective-permute-done.11.refs_4_), channel_id=1, source_target_pairs={{0,32},{1,33},{2,34},{3,35},{4,36},{5,37},{6,38},{7,39},{8,40},{9,... | collective-permute-start | bytes 3538952 | tf_op jit(solution)/shard_map/ppermute | solution.py:354
  72.2 23.8 %collective-permute-start.7 = (bf16[3584,128]{1,0:T(8,128)(2,1)}, bf16[3584,128]{1,0:T(8,128)(2,1)}, u32[]{:S(2)}, u32[]{:S(2)}) collective-permute-start(bf16[3584,128]{1,0:T(8,128)(2,1)} %copy-done.3), channel_id=1, source_target_pairs={{0,64},{1,65},{2,66},{3,67},{4,68},{5,69},{6,70},{7,71},{8,72},{9,... | collective-permute-start | bytes 2752520 | tf_op jit(solution)/shard_map/ppermute | solution.py:354
  72.4 23.7 %collective-permute-start.15 = (bf16[64,3584]{1,0:T(8,128)(2,1)}, bf16[64,3584]{1,0:T(8,128)(2,1)S(1)}, u32[]{:S(2)}, u32[]{:S(2)}) collective-permute-start(bf16[64,3584]{1,0:T(8,128)(2,1)} %pad_maximum_fusion.1.refs_6_), channel_id=1, source_target_pairs={{0,24},{1,25},{2,26},{3,27},{4,28},{5,29},{6,30},{7,31},{8,0},{9,1... | collective-permute-start | bytes 1376264 | tf_op jit(solution)/shard_map/ppermute | solution.py:354
  73.7 22.3 %collective-permute-start.14 = (bf16[64,3584]{1,0:T(8,128)(2,1)}, bf16[64,3584]{1,0:T(8,128)(2,1)}, u32[]{:S(2)}, u32[]{:S(2)}) collective-permute-start(bf16[64,3584]{1,0:T(8,128)(2,1)} %pad_maximum_fusion.1.refs_6_), channel_id=1, source_target_pairs={{0,8},{1,9},{2,10},{3,11},{4,12},{5,13},{6,14},{7,15},{8,16},{9,17... | collective-permute-start | bytes 1376264 | tf_op jit(solution)/shard_map/ppermute | solution.py:354
  73.8 1.4 %copy-start.8 = (bf16[4608,128]{1,0:T(8,128)(2,1)}, bf16[4608,128]{1,0:T(8,128)(2,1)S(1)}, u32[]{:S(2)}) copy-start(bf16[4608,128]{1,0:T(8,128)(2,1)S(1)} %collective-permute-done.12.refs_5_) | copy-start | bytes 3538948
  73.9 23.0 %collective-permute-start.13 = (bf16[64,3584]{1,0:T(8,128)(2,1)}, bf16[64,3584]{1,0:T(8,128)(2,1)}, u32[]{:S(2)}, u32[]{:S(2)}) collective-permute-start(bf16[64,3584]{1,0:T(8,128)(2,1)} %pad_maximum_fusion.1.refs_6_), channel_id=1, source_target_pairs={{0,16},{1,17},{2,18},{3,19},{4,20},{5,21},{6,22},{7,23},{8,24},{9,... | collective-permute-start | bytes 1376264 | tf_op jit(solution)/shard_map/ppermute | solution.py:354
  96.0 0.8 copy-start.13
  96.8 3.1 %collective-permute-start.16 = (bf16[3584,128]{1,0:T(8,128)(2,1)}, bf16[3584,128]{1,0:T(8,128)(2,1)S(1)}, u32[]{:S(2)}, u32[]{:S(2)}) collective-permute-start(bf16[3584,128]{1,0:T(8,128)(2,1)} %collective-permute-done.7.refs_4_), channel_id=1, source_target_pairs={{0,32},{1,33},{2,34},{3,35},{4,36},{5,37},{6,38},{7,39},{8,40},{9,... | collective-permute-start | bytes 2752520 | tf_op jit(solution)/shard_map/ppermute | solution.py:354
  99.9 0.9 copy-start.9

commit v4 on v3

--- a/solution.py
+++ b/solution.py
@@ -42,19 +42,26 @@
 
 
 def cost(us):
-    return pl.CostEstimate(flops=int(us * 1.1e9), transcendentals=0, bytes_accessed=1 << 20)
+    return pl.CostEstimate(flops=int(us * 1.1e9), transcendentals=0, bytes_accessed=1024)
 
 
 DBLK = 25
-CHUNKS = (576, 448)
-
-
-def spectra_kernel(half, me_ref, x_hbm, start_ref, qual_ref, y0_ref, y1_ref, y_ref, x_ref, state, table, spec, power, sem):
+CHUNKS = (640, 384)
+
+
+def spectra_kernel(
+    half, me_ref, ia, ib, ic, id_, x_hbm, start_hbm, qual_ref, y0_hbm, y1_hbm, y_hbm, sel_ref,
+    x_ref, start_ref, y_ref, state, table, spec, power, sems,
+):
     ngrp = half // GRP
     length = 2 * half
     blocks = ngrp // DBLK
-    load = pltpu.make_async_copy(x_hbm, x_ref, sem)
+    me, r = me_ref[0], me_ref[1]
+    load_start = pltpu.make_async_copy(start_hbm, start_ref, sems.at[0])
+    load_start.start()
+    load = pltpu.make_async_copy(x_hbm, x_ref, sems.at[1])
     load.start()
+    load_start.wait()
 
     def gen(slot):
         for lo in range(0, length, 128):
@@ -85,9 +92,9 @@
     lax.fori_loop(0, blocks, block, 0)
     mean = jnp.sum(power[...], axis=0, keepdims=True) * (1.0 / half)
     level2 = 0.25 * (mean + 1e-06)
-    own = [qual_ref[pl.ds(me_ref[0] * 4 + g, 1), :].astype(jnp.float32) for g in range(4)]
-
-    def whiten(n, part_ref, m):
+    own = [qual_ref[pl.ds(me * 4 + g, 1), :].astype(jnp.float32) for g in range(4)]
+
+    def whiten(n):
         base = pl.multiple_of(n * 16, 16)
         reals, imags = [], []
         for g in range(4):
@@ -98,85 +105,132 @@
             reals.append(real * inv)
             imags.append(imag * inv)
         value = jnp.concatenate(reals + imags, axis=0).astype(jnp.bfloat16)
-        part_ref[pl.ds(pl.multiple_of(m * ROWS, ROWS), ROWS), :] = value
         y_ref[pl.ds(pl.multiple_of(n * ROWS, ROWS), ROWS), :] = value
 
     first = CHUNKS[0] // GRP
 
-    def sweep(lo, hi, part_ref):
+    def sweep(lo, hi):
         def some(m, _):
-            for v in range(4):
-                whiten(lo + m * 4 + v, part_ref, m * 4 + v)
+            for v in range(5):
+                whiten(lo + m * 5 + v)
             return 0
 
-        lax.fori_loop(0, (hi - lo) // 4, some, 0)
-        for n in range(hi - (hi - lo) % 4, hi):
-            whiten(n, part_ref, n - lo)
-
-    sweep(0, first, y0_ref)
-    sweep(first, ngrp, y1_ref)
-    tail = (ngrp - first) * ROWS
-    for ref in (y1_ref, y_ref):
-        rows = ref.shape[0]
-        ref[rows - CHUNKS[1] * 8 + tail :, :] = jnp.zeros((CHUNKS[1] * 8 - tail, 128), jnp.bfloat16)
-        ref[rows - ROWS : rows - ROWS + 16, :] = qual_ref[...].astype(jnp.float32).astype(jnp.bfloat16)
-
-
-def spectra(samples, qual_t, me):
+        lax.fori_loop(0, (hi - lo) // 5, some, 0)
+
+    row = lax.broadcasted_iota(jnp.int32, (8, 128), 0)
+    lane = lax.broadcasted_iota(jnp.int32, (8, 128), 1)
+    hot = jnp.zeros((8, 128), jnp.float32)
+    for rel, ref in enumerate((ia, ib, ic, id_)):
+        for h in range(2):
+            here = (row == rel * 2 + h) & (lane == ref[r + 32 * h] - r * 128)
+            hot = jnp.where(here, 1.0, hot)
+    hot = hot.astype(jnp.bfloat16)
+
+    def finish(lo, hi, part_hbm, k):
+        span = pl.ds(lo * ROWS, (hi - lo) * ROWS)
+        copies = [
+            pltpu.make_async_copy(y_ref.at[span], part_hbm, sems.at[2 * k]),
+            pltpu.make_async_copy(y_ref.at[span], y_hbm.at[span], sems.at[2 * k + 1]),
+        ]
+        for copy in copies:
+            copy.start()
+        value = y_ref[lo * ROWS : hi * ROWS, :]
+        picked = lax.dot_general(hot, value, (((1,), (1,)), ((), ())), preferred_element_type=jnp.float32)
+        picked = picked.astype(jnp.bfloat16)
+        for rel in range(4):
+            sel_ref[rel, :, lo * ROWS : hi * ROWS] = picked[rel * 2 : rel * 2 + 2]
+        return copies
+
+    first = CHUNKS[0] // GRP
+    sweep(0, first)
+    copies = finish(0, first, y0_hbm, 1)
+    sweep(first, ngrp)
+    y_ref[ngrp * ROWS :, :] = jnp.zeros(((NGRP - ngrp) * ROWS, 128), jnp.bfloat16)
+    last = (NGRP - 1) * ROWS
+    y_ref[last : last + 16, :] = qual_ref[...].astype(jnp.float32).astype(jnp.bfloat16)
+    copies += finish(first, NGRP, y1_hbm, 2)
+    for copy in copies:
+        copy.wait()
+
+
+def spectra(samples, qual_t, me, lists):
     length = samples.shape[1]
     half = length // 2
     start = jnp.asarray(start_tables(length))
     vmem = pl.BlockSpec(memory_space=pltpu.VMEM)
+    smem = pl.BlockSpec(memory_space=pltpu.SMEM)
+    hbm = pl.BlockSpec(memory_space=pltpu.HBM)
     return pl.pallas_call(
         functools.partial(spectra_kernel, half),
         out_shape=[
             jax.ShapeDtypeStruct((CHUNKS[0] * 8, 128), jnp.bfloat16),
             jax.ShapeDtypeStruct((CHUNKS[1] * 8, 128), jnp.bfloat16),
             jax.ShapeDtypeStruct((NGRP * ROWS, 128), jnp.bfloat16),
+            jax.ShapeDtypeStruct((4, 2, NGRP * ROWS), jnp.bfloat16),
         ],
-        in_specs=[pl.BlockSpec(memory_space=pltpu.SMEM), pl.BlockSpec(memory_space=pl.ANY), vmem, vmem],
-        out_specs=[vmem, vmem, vmem],
+        in_specs=[smem] * 5 + [hbm, hbm, vmem],
+        out_specs=[hbm, hbm, hbm, vmem],
         scratch_shapes=[
             pltpu.VMEM((4, length, 128), jnp.bfloat16),
+            pltpu.VMEM((4, 8, length), jnp.float32),
+            pltpu.VMEM((NGRP * ROWS, 128), jnp.bfloat16),
             pltpu.VMEM((2, 8, length), jnp.float32),
             pltpu.VMEM((2, DBLK * 16, length), jnp.bfloat16),
             pltpu.VMEM((2 * half, 512), jnp.float32),
             pltpu.VMEM((8, 512), jnp.float32),
-            pltpu.SemaphoreType.DMA,
+            pltpu.SemaphoreType.DMA((6,)),
         ],
         compiler_params=pltpu.CompilerParams(vmem_limit_bytes=48 * MB),
-        cost_estimate=cost(10),
+        cost_estimate=cost(0.001),
         name="spectra",
-    )(me, samples, start, qual_t)
-
-
-def select_kernel(me_ref, ia, ib, ic, id_, y_ref, out_ref):
-    me, r = me_ref[0], me_ref[1]
-    row = lax.broadcasted_iota(jnp.int32, (16, 128), 0)
-    lane = lax.broadcasted_iota(jnp.int32, (16, 128), 1)
-    hot = jnp.zeros((16, 128), jnp.float32)
-    for rel, ref in enumerate((ia, ib, ic, id_)):
-        group = jnp.bitwise_xor(me, rel)
-        for h in range(2):
-            here = (row // 4 == group) & (row % 2 == h) & (lane == ref[r + 32 * h] - r * 128)
-            hot = jnp.where(here, 1.0, hot)
-    hot = hot.astype(jnp.bfloat16)
-    picked = lax.dot_general(hot, y_ref[...], (((1,), (1,)), ((), ())), preferred_element_type=jnp.float32)
-    out_ref[...] = picked.astype(jnp.bfloat16)
-
-
-def select(where, lists, y):
-    smem = pl.BlockSpec(memory_space=pltpu.SMEM)
+    )(me, *lists, samples, start, qual_t)
+
+
+def join_kernel(plan, count, *refs):
+    for out, row, src, at in plan:
+        value = refs[src][...].reshape(-1, refs[src].shape[-1]) if at is None else refs[src][at]
+        refs[count + out][row : row + value.shape[0], :] = value
+
+
+def join(values, plan, shapes, name):
     vmem = pl.BlockSpec(memory_space=pltpu.VMEM)
     return pl.pallas_call(
-        select_kernel,
-        out_shape=jax.ShapeDtypeStruct((16, NGRP * ROWS), jnp.bfloat16),
-        in_specs=[smem] * 5 + [vmem],
-        out_specs=vmem,
+        functools.partial(join_kernel, plan, len(values)),
+        out_shape=[jax.ShapeDtypeStruct(shape, values[0].dtype) for shape in shapes],
+        in_specs=[vmem] * len(values),
+        out_specs=[vmem] * len(shapes),
         compiler_params=pltpu.CompilerParams(vmem_limit_bytes=16 * MB),
-        cost_estimate=cost(2),
-        name="select",
-    )(where, *lists, y)
+        cost_estimate=cost(0.001),
+        name=name,
+    )(*values)
+
+
+def split_kernel(pa, pb, pc, pd, line0, line1, sems):
+    copies, start = [], 0
+    for k, (line, kc) in enumerate(zip((line0, line1), CHUNKS)):
+        for j, piece in enumerate((pa, pb, pc, pd)):
+            copies.append(
+                pltpu.make_async_copy(
+                    piece.at[:, pl.ds(start * 8, kc * 8)], line.at[pl.ds(j * 16, 16), :], sems.at[k * 4 + j]
+                )
+            )
+            copies[-1].start()
+        start += kc
+    for copy in copies:
+        copy.wait()
+
+
+def split(pieces):
+    hbm = pl.BlockSpec(memory_space=pl.ANY)
+    return pl.pallas_call(
+        split_kernel,
+        out_shape=[jax.ShapeDtypeStruct((64, kc * 8), jnp.bfloat16) for kc in CHUNKS],
+        in_specs=[hbm] * 4,
+        out_specs=[hbm] * 2,
+        scratch_shapes=[pltpu.SemaphoreType.DMA((8,))],
+        cost_estimate=cost(0.001),
+        name="split",
+    )(*pieces)
 
 
 UNROLL = 4
@@ -184,20 +238,20 @@
 
 
 def correlate_kernel(first, last, kc, offset, *refs):
-    where_ref, seg_ref, ya, yb, yc, yd, xa, xb, xc, xd, lag_ref, qual_ref = refs[:12]
+    where_ref, ya, yb, yc, yd, xa, xb, xc, xd, lag_ref, qual_ref = refs[:11]
     if first:
-        out_ref, ybuf, xbuf, xrow, cross, sems = refs[12:]
+        out_ref, ybuf, xbuf, xrow, cross, sems = refs[11:]
         acc_ref = None
     else:
-        acc_hbm, out_ref, ybuf, xbuf, xrow, cross, sems, acc_ref, scale, stage, osem = refs[12:]
+        acc_hbm, out_ref, ybuf, xbuf, xrow, cross, sems, acc_ref, scale, stage, osem = refs[11:]
     parts = ((0, HEAD), (HEAD, kc - HEAD))
     copies = []
     for k, (lo, size) in enumerate(parts):
         span = pl.ds(lo * 8, size * 8)
         some = []
-        for j, ref in enumerate((ya, yb, yc, yd)):
-            rows = span if j >= 2 else pl.ds((offset + lo) * 8, size * 8)
-            some.append(pltpu.make_async_copy(ref.at[rows], ybuf.at[seg_ref[j], span], sems.at[k * 8 + j]))
+        for j, ref in enumerate((ya, yc, yb, yd)):
+            rows = span if j % 2 else pl.ds((offset + lo) * 8, size * 8)
+            some.append(pltpu.make_async_copy(ref.at[rows], ybuf.at[j, span], sems.at[k * 8 + j]))
         for j, ref in enumerate((xa, xb, xc, xd)):
             some.append(pltpu.make_async_copy(ref.at[:, span], xbuf.at[j, :, span], sems.at[k * 8 + 4 + j]))
         copies.append(some)
@@ -300,12 +354,12 @@
         flush(7, 1).wait()
 
 
-def correlate(first, last, kc, offset, where, seg, ys, xs, table, qual_t, acc=None):
+def correlate(first, last, kc, offset, where, ys, xs, table, qual_t, acc=None):
     smem = pl.BlockSpec(memory_space=pltpu.SMEM)
     hbm = pl.BlockSpec(memory_space=pl.ANY)
     vmem = pl.BlockSpec(memory_space=pltpu.VMEM)
-    args = (where, seg, *ys, *xs, table, qual_t)
-    in_specs = [smem, smem] + [hbm] * 8 + [vmem, vmem]
+    args = (where, *ys, *xs, table, qual_t)
+    in_specs = [smem] + [hbm] * 8 + [vmem, vmem]
     scratch = [
         pltpu.VMEM((4, kc * 8, 128), jnp.bfloat16),
         pltpu.VMEM((4, 64, kc * 8), jnp.bfloat16),
@@ -332,7 +386,7 @@
         out_specs=out_specs,
         scratch_shapes=scratch,
         compiler_params=pltpu.CompilerParams(vmem_limit_bytes=60 * MB),
-        cost_estimate=cost(kc / 40),
+        cost_estimate=cost(0.001),
         name="correlate_first" if first else "correlate_last",
     )(*args)
 
@@ -373,6 +427,14 @@
 
 def both(zhi, core, y, zlo, x):
     return zhi + 1, core + 1, y, zlo, x
+
+
+def beside(zhi, core, y, zlo, x):
+    return zhi, core, y, zlo + 1, x
+
+
+def aside(zhi, core, y, zlo, x):
+    return zhi + 1, core, y, zlo + 1, x
 
 
 def on_device(traces, src_index, quality):
@@ -385,8 +447,7 @@
     dx, dy = (xx - i % 4) % 4, (yy - (i // 8) % 4) % 4
     dx, dy = dx % 2 * 2 + dx // 2, dy % 2 * 2 + dy // 2
     far_step, near_step = jnp.where(core == 0, dy, dx), jnp.where(core == 0, dx, dy)
-    where = far_step * 16 + near_step * 4 + (i // 4) % 2 * 2 + i // 32
-    seg = jnp.bitwise_xor(me, jnp.arange(4, dtype=jnp.int32))
+    where = far_step * 16 + near_step * 4 + jnp.bitwise_xor((i // 4) % 2, zlo) * 2 + i // 32
     table = lag_table(1000)
     tables, start = [], 0
     for kc in CHUNKS:
@@ -394,30 +455,33 @@
         start += kc
 
     lists = [src_index] + [send(src_index, move) for move in (sibling, across, both)]
-    y0, y1, y = spectra(samples, qual_t, spot)
-
-    slots = select(spot, lists, y).reshape(8, 2, -1)
-    got = lax.all_to_all(slots, ("zhi", "core", "zlo"), 0, 0, tiled=False)
-    y0, y1, y, got = lax.optimization_barrier((y0, y1, y, got))
-    got = got.reshape(16, -1)
+    y0, y1, y, sel = spectra(samples, qual_t, spot, lists)
+
+    stay, away = sel[:2], sel[2:]
+    out = [send(stay, beside), send(away, across), send(away, aside)]
+    y0, y1, y, stay, *out = lax.optimization_barrier((y0, y1, y, stay, *out))
     far0 = send(y0, across)
+    held = [stay] + out
+    near = send(y, sibling)
+    lanes = y.shape[0]
+    both_cores = [(part, j * 2, j, part) for part in range(2) for j in range(4)]
+    mine, theirs = join(held, both_cores, [(8, lanes)] * 2, "join_column")
+    theirs = send(theirs, sibling)
+    (got,) = join((mine, theirs), [(0, 0, 0, None), (0, 8, 1, None)], [(16, lanes)], "join_cores")
+    pieces = [got] + [send(got, ring(0, d)) for d in (2, 1, 3)]
+    *pieces, near, y1 = lax.optimization_barrier((*pieces, near, y1))
     far1 = send(y1, across)
-    pieces = [got] + [send(got, ring(0, d)) for d in (2, 1, 3)]
-    *pieces, y = lax.optimization_barrier((*pieces, y))
-    near = send(y, sibling)
-    lines, start = [], 0
-    for kc in CHUNKS:
-        lines.append(jnp.concatenate([piece[:, start * 8 : (start + kc) * 8] for piece in pieces], axis=0))
-        start += kc
+    lines = split(pieces)
     xs0 = [lines[0]] + [send(lines[0], ring(1, d)) for d in (2, 1, 3)]
-    *xs0, line1, far0 = lax.optimization_barrier((*xs0, lines[1], far0))
+    *xs0, line1 = lax.optimization_barrier((*xs0, lines[1]))
+    far0 = lax.optimization_barrier((far0, lines[1]))[0]
     xs1 = [line1] + [send(line1, ring(1, d)) for d in (2, 1, 3)]
     acc = correlate(
-        True, False, CHUNKS[0], 0, where, seg, (y, near, far0, send(far0, sibling)), xs0, tables[0], qual_t
+        True, False, CHUNKS[0], 0, where, (y, near, far0, send(far0, sibling)), xs0, tables[0], qual_t
     )
     far1, acc, *xs1 = lax.optimization_barrier((far1, acc, *xs1))
     out = correlate(
-        False, True, CHUNKS[1], CHUNKS[0], where, seg, (y, near, far1, send(far1, sibling)), xs1, tables[1], qual_t, acc
+        False, True, CHUNKS[1], CHUNKS[0], where, (y, near, far1, send(far1, sibling)), xs1, tables[1], qual_t, acc
     )
     return jnp.transpose(out, (1, 0, 2))
 

time: 116 us -> 146 us (1.26)
  Pallas kernels: 44.7 us -> 76.3 us
  blocking collectives: 11.5 us -> 0 us
  waiting for transfers between devices: 25.6 us -> 34.9 us
  starting transfers between devices: 22.2 us -> 26.9 us
  local copies, waits for them, and re-layouts: 9.82 us -> 6.7 us
    pallas_call x1 -> x3, Pallas kernels: 1.21 us -> 33.1 us  [the longest x1 32.9 us: split(): pl.pallas_call(split_kernel, out_shape=[jax.ShapeDtypeStruct((64, kc * 8)...]
    all_to_all x1 -> x0, blocking collectives: 11.5 us -> none  [on_device(): got = lax.all_to_all(slots, ('zhi', 'core', 'zlo'), 0, 0, tiled=False)]
    ppermute x17 -> x21, waiting for transfers between devices: 25.6 us -> 34.9 us  [send(): return lax.ppermute(value, AXES, permutation(move))]
    ppermute x17 -> x21, starting transfers between devices: 22.2 us -> 26.9 us  [send(): return lax.ppermute(value, AXES, permutation(move))]
    unnamed x28 -> x24, local copies, waits for them, and re-layouts: 8.48 us -> 6.61 us
  transfers between devices with their start and end apart: 17 -> 21, of which waited for: 6 -> 10; matrix products, arithmetic and copies ran while one was open for 2% -> 0% of each run, Pallas kernels for 24% -> 36%
where the time goes in v4:
time: 146 us
  Pallas kernels  76.3 us (52%)
  waiting for transfers between devices  34.9 us (24%)
  starting transfers between devices  26.9 us (18%)
  local copies, waits for them, and re-layouts  6.7 us (5%)
    ppermute x21, waiting for transfers between devices, send(): return lax.ppermute(value, AXES, permutation(move))  34.9 us
    pallas_call x2, Pallas kernels, correlate(): pl.pallas_call(functools.partial(correlate_kernel, first, last, kc, offse...  33.1 us
    pallas_call x1, Pallas kernels, split(): pl.pallas_call(split_kernel, out_shape=[jax.ShapeDtypeStruct((64, kc * 8)...  32.9 us
    ppermute x21, starting transfers between devices, send(): return lax.ppermute(value, AXES, permutation(move))  26.9 us
    pallas_call x1, Pallas kernels, spectra(): pl.pallas_call(functools.partial(spectra_kernel, half), out_shape=[jax.Sh...  10 us
    unnamed x24, local copies, waits for them, and re-layouts  6.61 us
  transfers between devices with their start and end apart: 21, of which 10 were waited for; matrix products, arithmetic and copies ran while one was open for 0% of the time, Pallas kernels for 36%

profile of v4, /device:TPU:1, one launch (start us, length us, event | category | flops | bytes accessed | tf_op | source)
XLA Modules:
  0.0 145.6 jit_solution(17607271154164873226)
XLA Ops:
  0.0 4.4 %collective-permute-start.1 = (s32[64]{0:T(128)}, s32[64]{0:T(128)S(1)}, u32[]{:S(2)}, u32[]{:S(2)}) collective-permute-start(s32[64]{0:T(128)} %ia.1), channel_id=1, source_target_pairs={{0,64},{1,65},{2,66},{3,67},{4,68},{5,69},{6,70},{7,71},{8,72},{9,... | collective-permute-start | bytes 776 | tf_op jit(solution)/shard_map/ppermute | solution.py:408
  4.4 1.0 collective-permute-start
  5.4 0.1 pad_add_fusion.me_ref
  5.5 0.0 collective-permute-done.1.ic
  5.5 0.8 collective-permute-done.ib
  6.3 3.7 %collective-permute-done.2.id_ = s32[64]{0:T(128)S(1)} collective-permute-done((s32[64]{0:T(128)}, s32[64]{0:T(128)S(1)}, u32[]{:S(2)}, u32[]{:S(2)}) %collective-permute-start.2) | collective-permute-done | bytes 288 | tf_op jit(solution)/shard_map/ppermute | solution.py:408
  10.0 1.6 %copy-done = bf16[128,4,2000]{0,2,1:T(8,128)(2,1)S(1)} copy-done((bf16[128,4,2000]{0,2,1:T(8,128)(2,1)S(1)}, bf16[128,4,2000]{0,2,1:T(8,128)(2,1)}, u32[]{:S(2)}) %copy-start) | copy-done | bytes 2048024
  11.6 0.9 copy-done.2
  12.5 0.7 copy-done.3
  13.2 0.7 copy-done.4
  13.9 10.0 %spectra.1 = (bf16[5120,128]{1,0:T(8,128)(2,1)S(1)}, bf16[3072,128]{1,0:T(8,128)(2,1)S(1)}, bf16[8192,128]{1,0:T(8,128)(2,1)}, bf16[4,2,8192]{2,1,0:T(2,128)(2,1)S(1)}) custom-call(s32[2]{0:T(128)S(1)} %pad_add_fusion.me_ref, s32[64]{0:T(128)S(1)} %copy-done.4, s32[64]{0:T(128)S(1)} %collective-permute-done.ib, s32[64]{0:T(128)S(1)} %collective-permute-done.1.ic, ...), custom_call_target="tpu_custom_call" | custom-call | flops 1100000 | bytes 1024 | tf_op jit(solution)/shard_map/spectra/pallas_call | solution.py:163
  23.9 0.1 fusion.18
  24.0 0.5 collective-permute-start.5
  24.5 2.1 %collective-permute-start.4 = (bf16[2,2,8192]{2,1,0:T(2,128)(2,1)S(1)}, bf16[2,2,8192]{2,1,0:T(2,128)(2,1)S(1)}, u32[]{:S(2)}, u32[]{:S(2)}) collective-permute-start(bf16[2,2,8192]{2,1,0:T(2,128)(2,1)S(1)} %get-tuple-element.71), channel_id=1, source_target_pairs={{0,64},{1,65},{2,66},{3,67},{4,68},{5,69},{6,70},{7,71},{8,72},{9,... | collective-permute-start | bytes 196616 | tf_op jit(solution)/shard_map/ppermute | solution.py:408
  26.6 0.7 collective-permute-start.3
  27.4 2.8 %collective-permute-done.5.refs_3_ = bf16[2,2,8192]{2,1,0:T(2,128)(2,1)S(1)} collective-permute-done((bf16[2,2,8192]{2,1,0:T(2,128)(2,1)S(1)}, bf16[2,2,8192]{2,1,0:T(2,128)(2,1)S(1)}, u32[]{:S(2)}, u32[]{:S(2)}) %collective-permute-start.5) | collective-permute-done | bytes 65568 | tf_op jit(solution)/shard_map/ppermute | solution.py:408
  30.2 0.0 collective-permute-done.4.refs_2_
  30.2 0.5 collective-permute-done.3.refs_1_
  30.7 1.1 collective-permute-start.10
  31.8 1.5 %collective-permute-start.12 = (bf16[5120,128]{1,0:T(8,128)(2,1)S(1)}, bf16[5120,128]{1,0:T(8,128)(2,1)}, u32[]{:S(2)}, u32[]{:S(2)}) collective-permute-start(bf16[5120,128]{1,0:T(8,128)(2,1)S(1)} %get-tuple-element.52), channel_id=1, source_target_pairs={{0,64},{1,65},{2,66},{3,67},{4,68},{5,69},{6,70},{7,71},{8,72},{9,... | collective-permute-start | bytes 3932168 | tf_op jit(solution)/shard_map/ppermute | solution.py:408
  33.4 0.1 join_column.1
  33.5 0.4 collective-permute-start.6
  33.9 1.9 %collective-permute-done.6.refs_1_ = bf16[8,8192]{1,0:T(8,128)(2,1)S(1)} collective-permute-done((bf16[8,8192]{1,0:T(8,128)(2,1)S(1)}, bf16[8,8192]{1,0:T(8,128)(2,1)S(1)}, u32[]{:S(2)}, u32[]{:S(2)}) %collective-permute-start.6) | collective-permute-done | bytes 131104 | tf_op jit(solution)/shard_map/ppermute | solution.py:408
  35.8 0.0 copy-start.1
  35.8 2.8 %collective-permute-start.9 = (bf16[16,8192]{1,0:T(8,128)(2,1)S(1)}, bf16[16,8192]{1,0:T(8,128)(2,1)S(1)}, u32[]{:S(2)}, u32[]{:S(2)}) collective-permute-start(bf16[16,8192]{1,0:T(8,128)(2,1)S(1)} %join_cores.1.pa), channel_id=1, source_target_pairs={{0,3},{1,0},{2,1},{3,2},{4,7},{5,4},{6,5},{7,6},{8,11},{9,8},{10,9... | collective-permute-start | bytes 786440 | tf_op jit(solution)/shard_map/ppermute | solution.py:408
  38.6 1.6 %collective-permute-start.7 = (bf16[16,8192]{1,0:T(8,128)(2,1)S(1)}, bf16[16,8192]{1,0:T(8,128)(2,1)S(1)}, u32[]{:S(2)}, u32[]{:S(2)}) collective-permute-start(bf16[16,8192]{1,0:T(8,128)(2,1)S(1)} %join_cores.1.pa), channel_id=1, source_target_pairs={{0,2},{1,3},{2,0},{3,1},{4,6},{5,7},{6,4},{7,5},{8,10},{9,11},{10,... | collective-permute-start | bytes 786440 | tf_op jit(solution)/shard_map/ppermute | solution.py:408
  40.3 1.7 %collective-permute-done.9.pd = bf16[16,8192]{1,0:T(8,128)(2,1)S(1)} collective-permute-done((bf16[16,8192]{1,0:T(8,128)(2,1)S(1)}, bf16[16,8192]{1,0:T(8,128)(2,1)S(1)}, u32[]{:S(2)}, u32[]{:S(2)}) %collective-permute-start.9) | collective-permute-done | bytes 262176 | tf_op jit(solution)/shard_map/ppermute | solution.py:408
  42.0 6.3 %collective-permute-done.8.pc = bf16[16,8192]{1,0:T(8,128)(2,1)S(1)} collective-permute-done((bf16[16,8192]{1,0:T(8,128)(2,1)S(1)}, bf16[16,8192]{1,0:T(8,128)(2,1)S(1)}, u32[]{:S(2)}, u32[]{:S(2)}) %collective-permute-start.8) | collective-permute-done | bytes 262176 | tf_op jit(solution)/shard_map/ppermute | solution.py:408
  48.3 0.7 copy-done.10
  49.0 0.1 copy-done.11
  49.1 32.9 %split.1 = (bf16[64,5120]{1,0:T(8,128)(2,1)}, bf16[64,3072]{1,0:T(8,128)(2,1)}) custom-call(bf16[16,8192]{1,0:T(8,128)(2,1)} %copy-done.1, bf16[16,8192]{1,0:T(8,128)(2,1)} %copy-done.11, bf16[16,8192]{1,0:T(8,128)(2,1)} %copy-done.10, bf16[16,8192]{1,0:T(8,128)(2,1)} %copy-done.9), custom_call_target="tpu_custom_call" | custom-call | flops 1100000 | bytes 1024 | tf_op jit(solution)/shard_map/split/pallas_call | solution.py:225
  82.0 1.2 collective-permute-start.13
  83.3 1.4 collective-permute-start.16
  84.7 0.1 collective-permute-start.15
  84.7 1.7 %collective-permute-start.14 = (bf16[64,5120]{1,0:T(8,128)(2,1)}, bf16[64,5120]{1,0:T(8,128)(2,1)}, u32[]{:S(2)}, u32[]{:S(2)}) collective-permute-start(bf16[64,5120]{1,0:T(8,128)(2,1)} %get-tuple-element.60.refs_5_), channel_id=1, source_target_pairs={{0,16},{1,17},{2,18},{3,19},{4,20},{5,21},{6,22},{7,23},{8,24},{9,... | collective-permute-start | bytes 1966088 | tf_op jit(solution)/shard_map/ppermute | solution.py:408
  86.4 1.4 collective-permute-start.11
  87.8 5.5 %collective-permute-done.16.refs_8_ = bf16[64,5120]{1,0:T(8,128)(2,1)} collective-permute-done((bf16[64,5120]{1,0:T(8,128)(2,1)}, bf16[64,5120]{1,0:T(8,128)(2,1)}, u32[]{:S(2)}, u32[]{:S(2)}) %collective-permute-start.16) | collective-permute-done | bytes 655392 | tf_op jit(solution)/shard_map/ppermute | solution.py:408
  93.3 9.6 %collective-permute-done.15.refs_7_ = bf16[64,5120]{1,0:T(8,128)(2,1)} collective-permute-done((bf16[64,5120]{1,0:T(8,128)(2,1)}, bf16[64,5120]{1,0:T(8,128)(2,1)}, u32[]{:S(2)}, u32[]{:S(2)}) %collective-permute-start.15) | collective-permute-done | bytes 655392 | tf_op jit(solution)/shard_map/ppermute | solution.py:408
  103.0 0.0 collective-permute-start.19
  103.0 1.5 %collective-permute-start.18 = (bf16[64,3072]{1,0:T(8,128)(2,1)}, bf16[64,3072]{1,0:T(8,128)(2,1)}, u32[]{:S(2)}, u32[]{:S(2)}) collective-permute-start(bf16[64,3072]{1,0:T(8,128)(2,1)} %get-tuple-element.66.refs_5_), channel_id=1, source_target_pairs={{0,8},{1,9},{2,10},{3,11},{4,12},{5,13},{6,14},{7,15},{8,16},{9,17... | collective-permute-start | bytes 1179656 | tf_op jit(solution)/shard_map/ppermute | solution.py:408
  104.4 0.4 collective-permute-start.17
  104.8 0.6 fusion.refs_0_
  105.4 1.1 copy-done.5
  106.5 19.5 %correlate_first.1.refs_11_ = f32[64,208,128]{2,1,0:T(8,128)} custom-call(s32[64]{0:T(128)} %fusion.refs_0_, bf16[8192,128]{1,0:T(8,128)(2,1)} %get-tuple-element.42.refs_1_, bf16[8192,128]{1,0:T(8,128)(2,1)} %collective-permute-done.10.refs_2_, bf16[5120,128]{1,0:T(8,128)(2,1)} %collective-permute-done.12.refs_3_, bf16[5120,128]{1,0:T(8,128)(2,1)} %copy-done.5, ...), custom_call_target="tpu_custom_call" | custom-call | flops 1100000 | bytes 1024 | tf_op jit(solution)/shard_map/correlate_first/pallas_call | solution.py:382
  126.1 3.1 %collective-permute-start.20 = (bf16[3072,128]{1,0:T(8,128)(2,1)S(1)}, bf16[3072,128]{1,0:T(8,128)(2,1)S(1)}, u32[]{:S(2)}, u32[]{:S(2)}) collective-permute-start(bf16[3072,128]{1,0:T(8,128)(2,1)S(1)} %collective-permute-done.11.refs_3_), channel_id=1, source_target_pairs={{0,32},{1,33},{2,34},{3,35},{4,36},{5,37},{6,38},{7,39},{8,40},{9,... | collective-permute-start | bytes 2359304 | tf_op jit(solution)/shard_map/ppermute | solution.py:408
  129.2 1.9 %collective-permute-done.20.refs_4_ = bf16[3072,128]{1,0:T(8,128)(2,1)S(1)} collective-permute-done((bf16[3072,128]{1,0:T(8,128)(2,1)S(1)}, bf16[3072,128]{1,0:T(8,128)(2,1)S(1)}, u32[]{:S(2)}, u32[]{:S(2)}) %collective-permute-start.20) | collective-permute-done | bytes 786464 | tf_op jit(solution)/shard_map/ppermute | solution.py:408
  131.1 0.9 copy-done.7
  132.0 13.6 %correlate_last.1 = f32[201,64,128]{2,1,0:T(8,128)} custom-call(s32[64]{0:T(128)} %fusion.refs_0_, bf16[8192,128]{1,0:T(8,128)(2,1)} %get-tuple-element.42.refs_1_, bf16[8192,128]{1,0:T(8,128)(2,1)} %collective-permute-done.10.refs_2_, bf16[3072,128]{1,0:T(8,128)(2,1)} %copy-done.6, bf16[3072,128]{1,0:T(8,128)(2,1)} %copy-done.7, ...), custom_call_target="tpu_custom_call" | custom-call | flops 1100000 | bytes 1024 | tf_op jit(solution)/shard_map/correlate_last/pallas_call | solution.py:382
  (27 shorter events, 0.1 us)
Async XLA Ops:
  0.0 5.5 %collective-permute-start.1 = (s32[64]{0:T(128)}, s32[64]{0:T(128)S(1)}, u32[]{:S(2)}, u32[]{:S(2)}) collective-permute-start(s32[64]{0:T(128)} %ia.1), channel_id=1, source_target_pairs={{0,64},{1,65},{2,66},{3,67},{4,68},{5,69},{6,70},{7,71},{8,72},{9,... | collective-permute-start | bytes 776 | tf_op jit(solution)/shard_map/ppermute | solution.py:408
  4.4 1.9 %collective-permute-start = (s32[64]{0:T(128)}, s32[64]{0:T(128)S(1)}, u32[]{:S(2)}, u32[]{:S(2)}) collective-permute-start(s32[64]{0:T(128)} %ia.1), channel_id=1, source_target_pairs={{0,32},{1,33},{2,34},{3,35},{4,36},{5,37},{6,38},{7,39},{8,40},{9,... | collective-permute-start | bytes 776 | tf_op jit(solution)/shard_map/ppermute | solution.py:408
  5.4 4.6 %collective-permute-start.2 = (s32[64]{0:T(128)}, s32[64]{0:T(128)S(1)}, u32[]{:S(2)}, u32[]{:S(2)}) collective-permute-start(s32[64]{0:T(128)} %ia.1), channel_id=1, source_target_pairs={{0,96},{1,97},{2,98},{3,99},{4,100},{5,101},{6,102},{7,103},{8,104... | collective-permute-start | bytes 776 | tf_op jit(solution)/shard_map/ppermute | solution.py:408
  10.0 1.6 %copy-start = (bf16[128,4,2000]{0,2,1:T(8,128)(2,1)S(1)}, bf16[128,4,2000]{0,2,1:T(8,128)(2,1)}, u32[]{:S(2)}) copy-start(bf16[128,4,2000]{0,2,1:T(8,128)(2,1)} %param.6) | copy-start | bytes 6144004
  11.6 0.9 copy-start.2
  12.5 0.7 copy-start.3
  13.2 0.7 copy-start.4
  24.0 6.2 %collective-permute-start.5 = (bf16[2,2,8192]{2,1,0:T(2,128)(2,1)S(1)}, bf16[2,2,8192]{2,1,0:T(2,128)(2,1)S(1)}, u32[]{:S(2)}, u32[]{:S(2)}) collective-permute-start(bf16[2,2,8192]{2,1,0:T(2,128)(2,1)S(1)} %get-tuple-element.71), channel_id=1, source_target_pairs={{0,68},{1,69},{2,70},{3,71},{4,64},{5,65},{6,66},{7,67},{8,76},{9,... | collective-permute-start | bytes 196616 | tf_op jit(solution)/shard_map/ppermute | solution.py:408
  24.5 5.7 %collective-permute-start.4 = (bf16[2,2,8192]{2,1,0:T(2,128)(2,1)S(1)}, bf16[2,2,8192]{2,1,0:T(2,128)(2,1)S(1)}, u32[]{:S(2)}, u32[]{:S(2)}) collective-permute-start(bf16[2,2,8192]{2,1,0:T(2,128)(2,1)S(1)} %get-tuple-element.71), channel_id=1, source_target_pairs={{0,64},{1,65},{2,66},{3,67},{4,68},{5,69},{6,70},{7,71},{8,72},{9,... | collective-permute-start | bytes 196616 | tf_op jit(solution)/shard_map/ppermute | solution.py:408
  26.6 4.1 %collective-permute-start.3 = (bf16[2,2,8192]{2,1,0:T(2,128)(2,1)S(1)}, bf16[2,2,8192]{2,1,0:T(2,128)(2,1)S(1)}, u32[]{:S(2)}, u32[]{:S(2)}) collective-permute-start(bf16[2,2,8192]{2,1,0:T(2,128)(2,1)S(1)} %get-tuple-element.43.refs_0_), channel_id=1, source_target_pairs={{0,4},{1,5},{2,6},{3,7},{4,0},{5,1},{6,2},{7,3},{8,12},{9,13},{10,... | collective-permute-start | bytes 196616 | tf_op jit(solution)/shard_map/ppermute | solution.py:408
  30.7 17.6 %collective-permute-start.10 = (bf16[8192,128]{1,0:T(8,128)(2,1)}, bf16[8192,128]{1,0:T(8,128)(2,1)}, u32[]{:S(2)}, u32[]{:S(2)}) collective-permute-start(bf16[8192,128]{1,0:T(8,128)(2,1)} %get-tuple-element.42.refs_1_), channel_id=1, source_target_pairs={{0,32},{1,33},{2,34},{3,35},{4,36},{5,37},{6,38},{7,39},{8,40},{9,... | collective-permute-start | bytes 6291464 | tf_op jit(solution)/shard_map/ppermute | solution.py:408
  31.8 50.2 %collective-permute-start.12 = (bf16[5120,128]{1,0:T(8,128)(2,1)S(1)}, bf16[5120,128]{1,0:T(8,128)(2,1)}, u32[]{:S(2)}, u32[]{:S(2)}) collective-permute-start(bf16[5120,128]{1,0:T(8,128)(2,1)S(1)} %get-tuple-element.52), channel_id=1, source_target_pairs={{0,64},{1,65},{2,66},{3,67},{4,68},{5,69},{6,70},{7,71},{8,72},{9,... | collective-permute-start | bytes 3932168 | tf_op jit(solution)/shard_map/ppermute | solution.py:408
  33.5 2.3 %collective-permute-start.6 = (bf16[8,8192]{1,0:T(8,128)(2,1)S(1)}, bf16[8,8192]{1,0:T(8,128)(2,1)S(1)}, u32[]{:S(2)}, u32[]{:S(2)}) collective-permute-start(bf16[8,8192]{1,0:T(8,128)(2,1)S(1)} %get-tuple-element.48), channel_id=1, source_target_pairs={{0,32},{1,33},{2,34},{3,35},{4,36},{5,37},{6,38},{7,39},{8,40},{9,... | collective-permute-start | bytes 393224 | tf_op jit(solution)/shard_map/ppermute | solution.py:408
  35.8 12.5 %copy-start.1 = (bf16[16,8192]{1,0:T(8,128)(2,1)}, bf16[16,8192]{1,0:T(8,128)(2,1)S(1)}, u32[]{:S(2)}) copy-start(bf16[16,8192]{1,0:T(8,128)(2,1)S(1)} %join_cores.1.pa) | copy-start | bytes 786436
  35.8 6.1 %collective-permute-start.9 = (bf16[16,8192]{1,0:T(8,128)(2,1)S(1)}, bf16[16,8192]{1,0:T(8,128)(2,1)S(1)}, u32[]{:S(2)}, u32[]{:S(2)}) collective-permute-start(bf16[16,8192]{1,0:T(8,128)(2,1)S(1)} %join_cores.1.pa), channel_id=1, source_target_pairs={{0,3},{1,0},{2,1},{3,2},{4,7},{5,4},{6,5},{7,6},{8,11},{9,8},{10,9... | collective-permute-start | bytes 786440 | tf_op jit(solution)/shard_map/ppermute | solution.py:408
  38.6 9.6 %collective-permute-start.8 = (bf16[16,8192]{1,0:T(8,128)(2,1)S(1)}, bf16[16,8192]{1,0:T(8,128)(2,1)S(1)}, u32[]{:S(2)}, u32[]{:S(2)}) collective-permute-start(bf16[16,8192]{1,0:T(8,128)(2,1)S(1)} %join_cores.1.pa), channel_id=1, source_target_pairs={{0,1},{1,2},{2,3},{3,0},{4,5},{5,6},{6,7},{7,4},{8,9},{9,10},{10,1... | collective-permute-start | bytes 786440 | tf_op jit(solution)/shard_map/ppermute | solution.py:408
  38.6 9.6 %collective-permute-start.7 = (bf16[16,8192]{1,0:T(8,128)(2,1)S(1)}, bf16[16,8192]{1,0:T(8,128)(2,1)S(1)}, u32[]{:S(2)}, u32[]{:S(2)}) collective-permute-start(bf16[16,8192]{1,0:T(8,128)(2,1)S(1)} %join_cores.1.pa), channel_id=1, source_target_pairs={{0,2},{1,3},{2,0},{3,1},{4,6},{5,7},{6,4},{7,5},{8,10},{9,11},{10,... | collective-permute-start | bytes 786440 | tf_op jit(solution)/shard_map/ppermute | solution.py:408
  42.0 6.4 %copy-start.9 = (bf16[16,8192]{1,0:T(8,128)(2,1)}, bf16[16,8192]{1,0:T(8,128)(2,1)S(1)}, u32[]{:S(2)}) copy-start(bf16[16,8192]{1,0:T(8,128)(2,1)S(1)} %collective-permute-done.9.pd) | copy-start | bytes 786436
  48.3 0.7 copy-start.10
  48.3 0.8 copy-start.11
  82.0 23.4 %collective-permute-start.13 = (bf16[5120,128]{1,0:T(8,128)(2,1)}, bf16[5120,128]{1,0:T(8,128)(2,1)S(1)}, u32[]{:S(2)}, u32[]{:S(2)}) collective-permute-start(bf16[5120,128]{1,0:T(8,128)(2,1)} %collective-permute-done.12.refs_3_), channel_id=1, source_target_pairs={{0,32},{1,33},{2,34},{3,35},{4,36},{5,37},{6,38},{7,39},{8,40},{9,... | collective-permute-start | bytes 3932168 | tf_op jit(solution)/shard_map/ppermute | solution.py:408
  83.3 10.0 %collective-permute-start.16 = (bf16[64,5120]{1,0:T(8,128)(2,1)}, bf16[64,5120]{1,0:T(8,128)(2,1)}, u32[]{:S(2)}, u32[]{:S(2)}) collective-permute-start(bf16[64,5120]{1,0:T(8,128)(2,1)} %get-tuple-element.60.refs_5_), channel_id=1, source_target_pairs={{0,24},{1,25},{2,26},{3,27},{4,28},{5,29},{6,30},{7,31},{8,0},{9,1... | collective-permute-start | bytes 1966088 | tf_op jit(solution)/shard_map/ppermute | solution.py:408
  84.7 18.3 %collective-permute-start.15 = (bf16[64,5120]{1,0:T(8,128)(2,1)}, bf16[64,5120]{1,0:T(8,128)(2,1)}, u32[]{:S(2)}, u32[]{:S(2)}) collective-permute-start(bf16[64,5120]{1,0:T(8,128)(2,1)} %get-tuple-element.60.refs_5_), channel_id=1, source_target_pairs={{0,8},{1,9},{2,10},{3,11},{4,12},{5,13},{6,14},{7,15},{8,16},{9,17... | collective-permute-start | bytes 1966088 | tf_op jit(solution)/shard_map/ppermute | solution.py:408
  84.7 18.2 %collective-permute-start.14 = (bf16[64,5120]{1,0:T(8,128)(2,1)}, bf16[64,5120]{1,0:T(8,128)(2,1)}, u32[]{:S(2)}, u32[]{:S(2)}) collective-permute-start(bf16[64,5120]{1,0:T(8,128)(2,1)} %get-tuple-element.60.refs_5_), channel_id=1, source_target_pairs={{0,16},{1,17},{2,18},{3,19},{4,20},{5,21},{6,22},{7,23},{8,24},{9,... | collective-permute-start | bytes 1966088 | tf_op jit(solution)/shard_map/ppermute | solution.py:408
  86.4 39.6 %collective-permute-start.11 = (bf16[3072,128]{1,0:T(8,128)(2,1)S(1)}, bf16[3072,128]{1,0:T(8,128)(2,1)S(1)}, u32[]{:S(2)}, u32[]{:S(2)}) collective-permute-start(bf16[3072,128]{1,0:T(8,128)(2,1)S(1)} %get-tuple-element.51), channel_id=1, source_target_pairs={{0,64},{1,65},{2,66},{3,67},{4,68},{5,69},{6,70},{7,71},{8,72},{9,... | collective-permute-start | bytes 2359304 | tf_op jit(solution)/shard_map/ppermute | solution.py:408
  103.0 23.1 %collective-permute-start.19 = (bf16[64,3072]{1,0:T(8,128)(2,1)}, bf16[64,3072]{1,0:T(8,128)(2,1)S(1)}, u32[]{:S(2)}, u32[]{:S(2)}) collective-permute-start(bf16[64,3072]{1,0:T(8,128)(2,1)} %get-tuple-element.66.refs_5_), channel_id=1, source_target_pairs={{0,24},{1,25},{2,26},{3,27},{4,28},{5,29},{6,30},{7,31},{8,0},{9,1... | collective-permute-start | bytes 1179656 | tf_op jit(solution)/shard_map/ppermute | solution.py:408
  103.0 23.1 %collective-permute-start.18 = (bf16[64,3072]{1,0:T(8,128)(2,1)}, bf16[64,3072]{1,0:T(8,128)(2,1)}, u32[]{:S(2)}, u32[]{:S(2)}) collective-permute-start(bf16[64,3072]{1,0:T(8,128)(2,1)} %get-tuple-element.66.refs_5_), channel_id=1, source_target_pairs={{0,8},{1,9},{2,10},{3,11},{4,12},{5,13},{6,14},{7,15},{8,16},{9,17... | collective-permute-start | bytes 1179656 | tf_op jit(solution)/shard_map/ppermute | solution.py:408
  104.4 21.6 %collective-permute-start.17 = (bf16[64,3072]{1,0:T(8,128)(2,1)}, bf16[64,3072]{1,0:T(8,128)(2,1)}, u32[]{:S(2)}, u32[]{:S(2)}) collective-permute-start(bf16[64,3072]{1,0:T(8,128)(2,1)} %get-tuple-element.66.refs_5_), channel_id=1, source_target_pairs={{0,16},{1,17},{2,18},{3,19},{4,20},{5,21},{6,22},{7,23},{8,24},{9,... | collective-permute-start | bytes 1179656 | tf_op jit(solution)/shard_map/ppermute | solution.py:408
  105.4 1.1 copy-start.5
  126.0 5.1 %copy-start.6 = (bf16[3072,128]{1,0:T(8,128)(2,1)}, bf16[3072,128]{1,0:T(8,128)(2,1)S(1)}, u32[]{:S(2)}) copy-start(bf16[3072,128]{1,0:T(8,128)(2,1)S(1)} %collective-permute-done.11.refs_3_) | copy-start | bytes 2359300
  126.0 5.1 %copy-start.8 = (bf16[64,3072]{1,0:T(8,128)(2,1)}, bf16[64,3072]{1,0:T(8,128)(2,1)S(1)}, u32[]{:S(2)}) copy-start(bf16[64,3072]{1,0:T(8,128)(2,1)S(1)} %collective-permute-done.19.refs_8_) | copy-start | bytes 1179652
  126.1 5.0 %collective-permute-start.20 = (bf16[3072,128]{1,0:T(8,128)(2,1)S(1)}, bf16[3072,128]{1,0:T(8,128)(2,1)S(1)}, u32[]{:S(2)}, u32[]{:S(2)}) collective-permute-start(bf16[3072,128]{1,0:T(8,128)(2,1)S(1)} %collective-permute-done.11.refs_3_), channel_id=1, source_target_pairs={{0,32},{1,33},{2,34},{3,35},{4,36},{5,37},{6,38},{7,39},{8,40},{9,... | collective-permute-start | bytes 2359304 | tf_op jit(solution)/shard_map/ppermute | solution.py:408
  131.1 0.9 copy-start.7

commit v5 on v4

--- a/solution.py
+++ b/solution.py
@@ -46,7 +46,7 @@
 
 
 DBLK = 25
-CHUNKS = (640, 384)
+CHUNKS = (384, 640)
 
 
 def spectra_kernel(
@@ -116,6 +116,8 @@
             return 0
 
         lax.fori_loop(0, (hi - lo) // 5, some, 0)
+        for n in range(hi - (hi - lo) % 5, hi):
+            whiten(n)
 
     row = lax.broadcasted_iota(jnp.int32, (8, 128), 0)
     lane = lax.broadcasted_iota(jnp.int32, (8, 128), 1)
@@ -180,7 +182,7 @@
             pltpu.VMEM((8, 512), jnp.float32),
             pltpu.SemaphoreType.DMA((6,)),
         ],
-        compiler_params=pltpu.CompilerParams(vmem_limit_bytes=48 * MB),
+        compiler_params=pltpu.CompilerParams(vmem_limit_bytes=63 * MB),
         cost_estimate=cost(0.001),
         name="spectra",
     )(me, *lists, samples, start, qual_t)
@@ -205,29 +207,22 @@
     )(*values)
 
 
-def split_kernel(pa, pb, pc, pd, line0, line1, sems):
-    copies, start = [], 0
-    for k, (line, kc) in enumerate(zip((line0, line1), CHUNKS)):
+def lines_kernel(pa, pb, pc, pd, *lines):
+    start = 0
+    for line, kc in zip(lines, CHUNKS):
         for j, piece in enumerate((pa, pb, pc, pd)):
-            copies.append(
-                pltpu.make_async_copy(
-                    piece.at[:, pl.ds(start * 8, kc * 8)], line.at[pl.ds(j * 16, 16), :], sems.at[k * 4 + j]
-                )
-            )
-            copies[-1].start()
+            line[j * 16 : j * 16 + 16, :] = piece[:, start * 8 : (start + kc) * 8]
         start += kc
-    for copy in copies:
-        copy.wait()
 
 
 def split(pieces):
-    hbm = pl.BlockSpec(memory_space=pl.ANY)
+    vmem = pl.BlockSpec(memory_space=pltpu.VMEM)
     return pl.pallas_call(
-        split_kernel,
+        lines_kernel,
         out_shape=[jax.ShapeDtypeStruct((64, kc * 8), jnp.bfloat16) for kc in CHUNKS],
-        in_specs=[hbm] * 4,
-        out_specs=[hbm] * 2,
-        scratch_shapes=[pltpu.SemaphoreType.DMA((8,))],
+        in_specs=[vmem] * 4,
+        out_specs=[vmem] * 2,
+        compiler_params=pltpu.CompilerParams(vmem_limit_bytes=16 * MB),
         cost_estimate=cost(0.001),
         name="split",
     )(*pieces)
@@ -469,12 +464,11 @@
     theirs = send(theirs, sibling)
     (got,) = join((mine, theirs), [(0, 0, 0, None), (0, 8, 1, None)], [(16, lanes)], "join_cores")
     pieces = [got] + [send(got, ring(0, d)) for d in (2, 1, 3)]
-    *pieces, near, y1 = lax.optimization_barrier((*pieces, near, y1))
+    *pieces, near = lax.optimization_barrier((*pieces, near))
     far1 = send(y1, across)
     lines = split(pieces)
     xs0 = [lines[0]] + [send(lines[0], ring(1, d)) for d in (2, 1, 3)]
     *xs0, line1 = lax.optimization_barrier((*xs0, lines[1]))
-    far0 = lax.optimization_barrier((far0, lines[1]))[0]
     xs1 = [line1] + [send(line1, ring(1, d)) for d in (2, 1, 3)]
     acc = correlate(
         True, False, CHUNKS[0], 0, where, (y, near, far0, send(far0, sibling)), xs0, tables[0], qual_t

time: 146 us -> 108 us (0.74)
  Pallas kernels: 76.3 us -> 45.5 us
  waiting for transfers between devices: 34.9 us -> 29.1 us
  local copies, waits for them, and re-layouts: 6.7 us -> 3.29 us
    pallas_call x1, Pallas kernels: 32.9 us -> 0.07 us  [split(): pl.pallas_call(lines_kernel, out_shape=[jax.ShapeDtypeStruct((64, kc * 8)...]
    ppermute x21, waiting for transfers between devices: 34.9 us -> 29.1 us  [send(): return lax.ppermute(value, AXES, permutation(move))]
    unnamed x24 -> x20, local copies, waits for them, and re-layouts: 6.61 us -> 2.32 us
    pallas_call x1, Pallas kernels: 10 us -> 12.1 us  [spectra(): pl.pallas_call(functools.partial(spectra_kernel, half), out_shape=[jax.Sh...]
  transfers between devices with their start and end apart: 21 -> 21, of which waited for: 10 -> 13; matrix products, arithmetic and copies ran while one was open for 0% -> 1% of each run, Pallas kernels for 36% -> 14%
where the time goes in v5:
time: 108 us; the launch traced here: 107 us
  Pallas kernels  45.5 us (42%)
  waiting for transfers between devices  29.1 us (27%)
  starting transfers between devices  28.3 us (26%)
  local copies, waits for them, and re-layouts  3.29 us (3%)
  other arithmetic  1.25 us (1%)
    pallas_call x2, Pallas kernels, correlate(): pl.pallas_call(functools.partial(correlate_kernel, first, last, kc, offse...  33.2 us
    ppermute x21, waiting for transfers between devices, send(): return lax.ppermute(value, AXES, permutation(move))  29.1 us
    ppermute x21, starting transfers between devices, send(): return lax.ppermute(value, AXES, permutation(move))  28.3 us
    pallas_call x1, Pallas kernels, spectra(): pl.pallas_call(functools.partial(spectra_kernel, half), out_shape=[jax.Sh...  12.1 us
    unnamed x20, local copies, waits for them, and re-layouts  2.32 us
  transfers between devices with their start and end apart: 21, of which 13 were waited for; matrix products, arithmetic and copies ran while one was open for 1% of the time, Pallas kernels for 14%

profile of v5, /device:TPU:1, one launch (start us, length us, event | category | flops | bytes accessed | tf_op | source)
XLA Modules:
  0.0 107.5 jit_solution(2299843499618618658)
XLA Ops:
  0.0 4.4 %collective-permute-start.1 = (s32[64]{0:T(128)}, s32[64]{0:T(128)S(1)}, u32[]{:S(2)}, u32[]{:S(2)}) collective-permute-start(s32[64]{0:T(128)} %ia.1), channel_id=1, source_target_pairs={{0,64},{1,65},{2,66},{3,67},{4,68},{5,69},{6,70},{7,71},{8,72},{9,... | collective-permute-start | bytes 776 | tf_op jit(solution)/shard_map/ppermute | solution.py:403
  4.4 1.0 collective-permute-start
  5.4 0.0 collective-permute-start.2
  5.4 0.6 pad_add_fusion.me_ref
  6.0 0.0 collective-permute-done.1.ic
  6.0 0.3 collective-permute-done.ib
  6.3 3.6 %collective-permute-done.2.id_ = s32[64]{0:T(128)S(1)} collective-permute-done((s32[64]{0:T(128)}, s32[64]{0:T(128)S(1)}, u32[]{:S(2)}, u32[]{:S(2)}) %collective-permute-start.2) | collective-permute-done | bytes 288 | tf_op jit(solution)/shard_map/ppermute | solution.py:403
  10.0 0.5 copy-done.9
  10.5 12.1 %spectra.1 = (bf16[3072,128]{1,0:T(8,128)(2,1)}, bf16[5120,128]{1,0:T(8,128)(2,1)}, bf16[8192,128]{1,0:T(8,128)(2,1)}, bf16[4,2,8192]{2,1,0:T(2,128)(2,1)}) custom-call(s32[2]{0:T(128)} %pad_add_fusion.me_ref, s32[64]{0:T(128)} %ia.1, s32[64]{0:T(128)} %copy-done.8, s32[64]{0:T(128)} %copy-done.7, s32[64]{0:T(128)} %copy-done.9, ...), custom_call_target="tpu_custom_call" | custom-call | flops 1100000 | bytes 1024 | tf_op jit(solution)/shard_map/spectra/pallas_call | solution.py:165
  22.6 1.0 fusion.18
  23.5 0.5 collective-permute-start.5
  24.1 2.1 %collective-permute-start.4 = (bf16[2,2,8192]{2,1,0:T(2,128)(2,1)S(1)}, bf16[2,2,8192]{2,1,0:T(2,128)(2,1)S(1)}, u32[]{:S(2)}, u32[]{:S(2)}) collective-permute-start(bf16[2,2,8192]{2,1,0:T(2,128)(2,1)S(1)} %get-tuple-element.67), channel_id=1, source_target_pairs={{0,64},{1,65},{2,66},{3,67},{4,68},{5,69},{6,70},{7,71},{8,72},{9,... | collective-permute-start | bytes 196616 | tf_op jit(solution)/shard_map/ppermute | solution.py:403
  26.1 0.7 collective-permute-start.3
  26.9 2.7 %collective-permute-done.5.refs_3_ = bf16[2,2,8192]{2,1,0:T(2,128)(2,1)S(1)} collective-permute-done((bf16[2,2,8192]{2,1,0:T(2,128)(2,1)S(1)}, bf16[2,2,8192]{2,1,0:T(2,128)(2,1)S(1)}, u32[]{:S(2)}, u32[]{:S(2)}) %collective-permute-start.5) | collective-permute-done | bytes 65568 | tf_op jit(solution)/shard_map/ppermute | solution.py:403
  29.6 0.7 collective-permute-done.3.refs_1_
  30.2 1.1 %collective-permute-start.10 = (bf16[8192,128]{1,0:T(8,128)(2,1)}, bf16[8192,128]{1,0:T(8,128)(2,1)S(1)}, u32[]{:S(2)}, u32[]{:S(2)}) collective-permute-start(bf16[8192,128]{1,0:T(8,128)(2,1)} %get-tuple-element.40.refs_1_), channel_id=1, source_target_pairs={{0,32},{1,33},{2,34},{3,35},{4,36},{5,37},{6,38},{7,39},{8,40},{9,... | collective-permute-start | bytes 6291464 | tf_op jit(solution)/shard_map/ppermute | solution.py:403
  31.4 0.1 join_column.1
  31.5 0.1 collective-permute-start.6
  31.6 1.6 %collective-permute-start.12 = (bf16[3072,128]{1,0:T(8,128)(2,1)}, bf16[3072,128]{1,0:T(8,128)(2,1)}, u32[]{:S(2)}, u32[]{:S(2)}) collective-permute-start(bf16[3072,128]{1,0:T(8,128)(2,1)} %get-tuple-element.49), channel_id=1, source_target_pairs={{0,64},{1,65},{2,66},{3,67},{4,68},{5,69},{6,70},{7,71},{8,72},{9,... | collective-permute-start | bytes 2359304 | tf_op jit(solution)/shard_map/ppermute | solution.py:403
  33.2 2.0 %collective-permute-done.6.refs_1_ = bf16[8,8192]{1,0:T(8,128)(2,1)S(1)} collective-permute-done((bf16[8,8192]{1,0:T(8,128)(2,1)S(1)}, bf16[8,8192]{1,0:T(8,128)(2,1)S(1)}, u32[]{:S(2)}, u32[]{:S(2)}) %collective-permute-start.6) | collective-permute-done | bytes 131104 | tf_op jit(solution)/shard_map/ppermute | solution.py:403
  35.2 2.8 %collective-permute-start.9 = (bf16[16,8192]{1,0:T(8,128)(2,1)S(1)}, bf16[16,8192]{1,0:T(8,128)(2,1)S(1)}, u32[]{:S(2)}, u32[]{:S(2)}) collective-permute-start(bf16[16,8192]{1,0:T(8,128)(2,1)S(1)} %join_cores.1.pa), channel_id=1, source_target_pairs={{0,3},{1,0},{2,1},{3,2},{4,7},{5,4},{6,5},{7,6},{8,11},{9,8},{10,9... | collective-permute-start | bytes 786440 | tf_op jit(solution)/shard_map/ppermute | solution.py:403
  38.0 1.6 %collective-permute-start.7 = (bf16[16,8192]{1,0:T(8,128)(2,1)S(1)}, bf16[16,8192]{1,0:T(8,128)(2,1)S(1)}, u32[]{:S(2)}, u32[]{:S(2)}) collective-permute-start(bf16[16,8192]{1,0:T(8,128)(2,1)S(1)} %join_cores.1.pa), channel_id=1, source_target_pairs={{0,2},{1,3},{2,0},{3,1},{4,6},{5,7},{6,4},{7,5},{8,10},{9,11},{10,... | collective-permute-start | bytes 786440 | tf_op jit(solution)/shard_map/ppermute | solution.py:403
  39.7 1.7 %collective-permute-done.9.pd = bf16[16,8192]{1,0:T(8,128)(2,1)S(1)} collective-permute-done((bf16[16,8192]{1,0:T(8,128)(2,1)S(1)}, bf16[16,8192]{1,0:T(8,128)(2,1)S(1)}, u32[]{:S(2)}, u32[]{:S(2)}) %collective-permute-start.9) | collective-permute-done | bytes 262176 | tf_op jit(solution)/shard_map/ppermute | solution.py:403
  41.3 1.5 %collective-permute-start.11 = (bf16[5120,128]{1,0:T(8,128)(2,1)}, bf16[5120,128]{1,0:T(8,128)(2,1)}, u32[]{:S(2)}, u32[]{:S(2)}) collective-permute-start(bf16[5120,128]{1,0:T(8,128)(2,1)} %get-tuple-element.48), channel_id=1, source_target_pairs={{0,64},{1,65},{2,66},{3,67},{4,68},{5,69},{6,70},{7,71},{8,72},{9,... | collective-permute-start | bytes 3932168 | tf_op jit(solution)/shard_map/ppermute | solution.py:403
  42.9 4.8 %collective-permute-done.8.pc = bf16[16,8192]{1,0:T(8,128)(2,1)S(1)} collective-permute-done((bf16[16,8192]{1,0:T(8,128)(2,1)S(1)}, bf16[16,8192]{1,0:T(8,128)(2,1)S(1)}, u32[]{:S(2)}, u32[]{:S(2)}) %collective-permute-start.8) | collective-permute-done | bytes 262176 | tf_op jit(solution)/shard_map/ppermute | solution.py:403
  47.7 0.0 collective-permute-done.7.pb
  47.7 0.0 collective-permute-done.10.refs_2_
  47.7 0.1 split.1
  47.8 2.5 %collective-permute-start.16 = (bf16[64,3072]{1,0:T(8,128)(2,1)S(1)}, bf16[64,3072]{1,0:T(8,128)(2,1)S(1)}, u32[]{:S(2)}, u32[]{:S(2)}) collective-permute-start(bf16[64,3072]{1,0:T(8,128)(2,1)S(1)} %get-tuple-element.56.refs_5_), channel_id=1, source_target_pairs={{0,24},{1,25},{2,26},{3,27},{4,28},{5,29},{6,30},{7,31},{8,0},{9,1... | collective-permute-start | bytes 1179656 | tf_op jit(solution)/shard_map/ppermute | solution.py:403
  50.3 0.0 collective-permute-start.15
  50.3 1.7 %collective-permute-start.14 = (bf16[64,3072]{1,0:T(8,128)(2,1)S(1)}, bf16[64,3072]{1,0:T(8,128)(2,1)S(1)}, u32[]{:S(2)}, u32[]{:S(2)}) collective-permute-start(bf16[64,3072]{1,0:T(8,128)(2,1)S(1)} %get-tuple-element.56.refs_5_), channel_id=1, source_target_pairs={{0,16},{1,17},{2,18},{3,19},{4,20},{5,21},{6,22},{7,23},{8,24},{9,... | collective-permute-start | bytes 1179656 | tf_op jit(solution)/shard_map/ppermute | solution.py:403
  52.1 0.1 collective-permute-done.12.refs_3_
  52.2 2.1 %collective-permute-start.13 = (bf16[3072,128]{1,0:T(8,128)(2,1)}, bf16[3072,128]{1,0:T(8,128)(2,1)}, u32[]{:S(2)}, u32[]{:S(2)}) collective-permute-start(bf16[3072,128]{1,0:T(8,128)(2,1)} %collective-permute-done.12.refs_3_), channel_id=1, source_target_pairs={{0,32},{1,33},{2,34},{3,35},{4,36},{5,37},{6,38},{7,39},{8,40},{9,... | collective-permute-start | bytes 2359304 | tf_op jit(solution)/shard_map/ppermute | solution.py:403
  54.3 5.0 %collective-permute-done.16.refs_8_ = bf16[64,3072]{1,0:T(8,128)(2,1)S(1)} collective-permute-done((bf16[64,3072]{1,0:T(8,128)(2,1)S(1)}, bf16[64,3072]{1,0:T(8,128)(2,1)S(1)}, u32[]{:S(2)}, u32[]{:S(2)}) %collective-permute-start.16) | collective-permute-done | bytes 393248 | tf_op jit(solution)/shard_map/ppermute | solution.py:403
  59.3 3.5 %collective-permute-done.15.refs_7_ = bf16[64,3072]{1,0:T(8,128)(2,1)S(1)} collective-permute-done((bf16[64,3072]{1,0:T(8,128)(2,1)S(1)}, bf16[64,3072]{1,0:T(8,128)(2,1)S(1)}, u32[]{:S(2)}, u32[]{:S(2)}) %collective-permute-start.15) | collective-permute-done | bytes 393248 | tf_op jit(solution)/shard_map/ppermute | solution.py:403
  62.8 0.0 collective-permute-done.14.refs_6_
  62.8 0.1 collective-permute-start.19
  62.9 0.7 copy-done.5
  63.5 0.8 collective-permute-start.18
  64.3 0.4 collective-permute-start.17
  64.8 0.6 fusion.refs_0_
  65.4 14.3 %correlate_first.1.refs_11_ = f32[64,208,128]{2,1,0:T(8,128)} custom-call(s32[64]{0:T(128)} %fusion.refs_0_, bf16[8192,128]{1,0:T(8,128)(2,1)} %get-tuple-element.40.refs_1_, bf16[8192,128]{1,0:T(8,128)(2,1)} %copy-done.2, bf16[3072,128]{1,0:T(8,128)(2,1)} %collective-permute-done.12.refs_3_, bf16[3072,128]{1,0:T(8,128)(2,1)} %collective-permute-done.13.refs_4_, ...), custom_call_target="tpu_custom_call" | custom-call | flops 1100000 | bytes 1024 | tf_op jit(solution)/shard_map/correlate_first/pallas_call | solution.py:377
  79.7 0.5 collective-permute-done.11.refs_3_
  80.3 1.3 %collective-permute-done.18.refs_7_ = bf16[64,5120]{1,0:T(8,128)(2,1)} collective-permute-done((bf16[64,5120]{1,0:T(8,128)(2,1)S(1)}, bf16[64,5120]{1,0:T(8,128)(2,1)}, u32[]{:S(2)}, u32[]{:S(2)}) %collective-permute-start.18) | collective-permute-done | bytes 655392 | tf_op jit(solution)/shard_map/ppermute | solution.py:403
  81.6 3.1 %collective-permute-start.20 = (bf16[5120,128]{1,0:T(8,128)(2,1)}, bf16[5120,128]{1,0:T(8,128)(2,1)S(1)}, u32[]{:S(2)}, u32[]{:S(2)}) collective-permute-start(bf16[5120,128]{1,0:T(8,128)(2,1)} %collective-permute-done.11.refs_3_), channel_id=1, source_target_pairs={{0,32},{1,33},{2,34},{3,35},{4,36},{5,37},{6,38},{7,39},{8,40},{9,... | collective-permute-start | bytes 3932168 | tf_op jit(solution)/shard_map/ppermute | solution.py:403
  84.7 2.9 %collective-permute-done.20.refs_4_ = bf16[5120,128]{1,0:T(8,128)(2,1)S(1)} collective-permute-done((bf16[5120,128]{1,0:T(8,128)(2,1)}, bf16[5120,128]{1,0:T(8,128)(2,1)S(1)}, u32[]{:S(2)}, u32[]{:S(2)}) %collective-permute-start.20) | collective-permute-done | bytes 1310752 | tf_op jit(solution)/shard_map/ppermute | solution.py:403
  87.5 1.1 %copy-done.3 = bf16[5120,128]{1,0:T(8,128)(2,1)} copy-done((bf16[5120,128]{1,0:T(8,128)(2,1)}, bf16[5120,128]{1,0:T(8,128)(2,1)S(1)}, u32[]{:S(2)}) %copy-start.3) | copy-done | bytes 1310744
  88.7 18.8 %correlate_last.1 = f32[201,64,128]{2,1,0:T(8,128)} custom-call(s32[64]{0:T(128)} %fusion.refs_0_, bf16[8192,128]{1,0:T(8,128)(2,1)} %get-tuple-element.40.refs_1_, bf16[8192,128]{1,0:T(8,128)(2,1)} %copy-done.2, bf16[5120,128]{1,0:T(8,128)(2,1)} %collective-permute-done.11.refs_3_, bf16[5120,128]{1,0:T(8,128)(2,1)} %copy-done.3, bf16[64,5120]{1,0:T(8,128)(2,1)} %copy-done, ...), custom_call_target="tpu_custom_call" | custom-call | flops 1100000 | bytes 1024 | tf_op jit(solution)/shard_map/correlate_last/pallas_call | solution.py:377
  (23 shorter events, 0.1 us)
Async XLA Ops:
  0.0 6.0 %collective-permute-start.1 = (s32[64]{0:T(128)}, s32[64]{0:T(128)S(1)}, u32[]{:S(2)}, u32[]{:S(2)}) collective-permute-start(s32[64]{0:T(128)} %ia.1), channel_id=1, source_target_pairs={{0,64},{1,65},{2,66},{3,67},{4,68},{5,69},{6,70},{7,71},{8,72},{9,... | collective-permute-start | bytes 776 | tf_op jit(solution)/shard_map/ppermute | solution.py:403
  4.4 1.9 %collective-permute-start = (s32[64]{0:T(128)}, s32[64]{0:T(128)S(1)}, u32[]{:S(2)}, u32[]{:S(2)}) collective-permute-start(s32[64]{0:T(128)} %ia.1), channel_id=1, source_target_pairs={{0,32},{1,33},{2,34},{3,35},{4,36},{5,37},{6,38},{7,39},{8,40},{9,... | collective-permute-start | bytes 776 | tf_op jit(solution)/shard_map/ppermute | solution.py:403
  5.4 4.6 %collective-permute-start.2 = (s32[64]{0:T(128)}, s32[64]{0:T(128)S(1)}, u32[]{:S(2)}, u32[]{:S(2)}) collective-permute-start(s32[64]{0:T(128)} %ia.1), channel_id=1, source_target_pairs={{0,96},{1,97},{2,98},{3,99},{4,100},{5,101},{6,102},{7,103},{8,104... | collective-permute-start | bytes 776 | tf_op jit(solution)/shard_map/ppermute | solution.py:403
  6.0 4.0 %copy-start.7 = (s32[64]{0:T(128)}, s32[64]{0:T(128)S(1)}, u32[]{:S(2)}) copy-start(s32[64]{0:T(128)S(1)} %collective-permute-done.1.ic) | copy-start | bytes 772
  6.3 3.7 %copy-start.8 = (s32[64]{0:T(128)}, s32[64]{0:T(128)S(1)}, u32[]{:S(2)}) copy-start(s32[64]{0:T(128)S(1)} %collective-permute-done.ib) | copy-start | bytes 772
  10.0 0.5 copy-start.9
  23.5 6.0 %collective-permute-start.5 = (bf16[2,2,8192]{2,1,0:T(2,128)(2,1)S(1)}, bf16[2,2,8192]{2,1,0:T(2,128)(2,1)S(1)}, u32[]{:S(2)}, u32[]{:S(2)}) collective-permute-start(bf16[2,2,8192]{2,1,0:T(2,128)(2,1)S(1)} %get-tuple-element.67), channel_id=1, source_target_pairs={{0,68},{1,69},{2,70},{3,71},{4,64},{5,65},{6,66},{7,67},{8,76},{9,... | collective-permute-start | bytes 196616 | tf_op jit(solution)/shard_map/ppermute | solution.py:403
  24.1 5.5 %collective-permute-start.4 = (bf16[2,2,8192]{2,1,0:T(2,128)(2,1)S(1)}, bf16[2,2,8192]{2,1,0:T(2,128)(2,1)S(1)}, u32[]{:S(2)}, u32[]{:S(2)}) collective-permute-start(bf16[2,2,8192]{2,1,0:T(2,128)(2,1)S(1)} %get-tuple-element.67), channel_id=1, source_target_pairs={{0,64},{1,65},{2,66},{3,67},{4,68},{5,69},{6,70},{7,71},{8,72},{9,... | collective-permute-start | bytes 196616 | tf_op jit(solution)/shard_map/ppermute | solution.py:403
  26.1 4.1 %collective-permute-start.3 = (bf16[2,2,8192]{2,1,0:T(2,128)(2,1)S(1)}, bf16[2,2,8192]{2,1,0:T(2,128)(2,1)S(1)}, u32[]{:S(2)}, u32[]{:S(2)}) collective-permute-start(bf16[2,2,8192]{2,1,0:T(2,128)(2,1)S(1)} %get-tuple-element.41.refs_0_), channel_id=1, source_target_pairs={{0,4},{1,5},{2,6},{3,7},{4,0},{5,1},{6,2},{7,3},{8,12},{9,13},{10,... | collective-permute-start | bytes 196616 | tf_op jit(solution)/shard_map/ppermute | solution.py:403
  30.2 17.4 %collective-permute-start.10 = (bf16[8192,128]{1,0:T(8,128)(2,1)}, bf16[8192,128]{1,0:T(8,128)(2,1)S(1)}, u32[]{:S(2)}, u32[]{:S(2)}) collective-permute-start(bf16[8192,128]{1,0:T(8,128)(2,1)} %get-tuple-element.40.refs_1_), channel_id=1, source_target_pairs={{0,32},{1,33},{2,34},{3,35},{4,36},{5,37},{6,38},{7,39},{8,40},{9,... | collective-permute-start | bytes 6291464 | tf_op jit(solution)/shard_map/ppermute | solution.py:403
  31.5 3.7 %collective-permute-start.6 = (bf16[8,8192]{1,0:T(8,128)(2,1)S(1)}, bf16[8,8192]{1,0:T(8,128)(2,1)S(1)}, u32[]{:S(2)}, u32[]{:S(2)}) collective-permute-start(bf16[8,8192]{1,0:T(8,128)(2,1)S(1)} %get-tuple-element.46), channel_id=1, source_target_pairs={{0,32},{1,33},{2,34},{3,35},{4,36},{5,37},{6,38},{7,39},{8,40},{9,... | collective-permute-start | bytes 393224 | tf_op jit(solution)/shard_map/ppermute | solution.py:403
  31.6 20.6 %collective-permute-start.12 = (bf16[3072,128]{1,0:T(8,128)(2,1)}, bf16[3072,128]{1,0:T(8,128)(2,1)}, u32[]{:S(2)}, u32[]{:S(2)}) collective-permute-start(bf16[3072,128]{1,0:T(8,128)(2,1)} %get-tuple-element.49), channel_id=1, source_target_pairs={{0,64},{1,65},{2,66},{3,67},{4,68},{5,69},{6,70},{7,71},{8,72},{9,... | collective-permute-start | bytes 2359304 | tf_op jit(solution)/shard_map/ppermute | solution.py:403
  35.2 6.1 %collective-permute-start.9 = (bf16[16,8192]{1,0:T(8,128)(2,1)S(1)}, bf16[16,8192]{1,0:T(8,128)(2,1)S(1)}, u32[]{:S(2)}, u32[]{:S(2)}) collective-permute-start(bf16[16,8192]{1,0:T(8,128)(2,1)S(1)} %join_cores.1.pa), channel_id=1, source_target_pairs={{0,3},{1,0},{2,1},{3,2},{4,7},{5,4},{6,5},{7,6},{8,11},{9,8},{10,9... | collective-permute-start | bytes 786440 | tf_op jit(solution)/shard_map/ppermute | solution.py:403
  38.0 9.6 %collective-permute-start.8 = (bf16[16,8192]{1,0:T(8,128)(2,1)S(1)}, bf16[16,8192]{1,0:T(8,128)(2,1)S(1)}, u32[]{:S(2)}, u32[]{:S(2)}) collective-permute-start(bf16[16,8192]{1,0:T(8,128)(2,1)S(1)} %join_cores.1.pa), channel_id=1, source_target_pairs={{0,1},{1,2},{2,3},{3,0},{4,5},{5,6},{6,7},{7,4},{8,9},{9,10},{10,1... | collective-permute-start | bytes 786440 | tf_op jit(solution)/shard_map/ppermute | solution.py:403
  38.0 9.6 %collective-permute-start.7 = (bf16[16,8192]{1,0:T(8,128)(2,1)S(1)}, bf16[16,8192]{1,0:T(8,128)(2,1)S(1)}, u32[]{:S(2)}, u32[]{:S(2)}) collective-permute-start(bf16[16,8192]{1,0:T(8,128)(2,1)S(1)} %join_cores.1.pa), channel_id=1, source_target_pairs={{0,2},{1,3},{2,0},{3,1},{4,6},{5,7},{6,4},{7,5},{8,10},{9,11},{10,... | collective-permute-start | bytes 786440 | tf_op jit(solution)/shard_map/ppermute | solution.py:403
  41.3 38.9 %collective-permute-start.11 = (bf16[5120,128]{1,0:T(8,128)(2,1)}, bf16[5120,128]{1,0:T(8,128)(2,1)}, u32[]{:S(2)}, u32[]{:S(2)}) collective-permute-start(bf16[5120,128]{1,0:T(8,128)(2,1)} %get-tuple-element.48), channel_id=1, source_target_pairs={{0,64},{1,65},{2,66},{3,67},{4,68},{5,69},{6,70},{7,71},{8,72},{9,... | collective-permute-start | bytes 3932168 | tf_op jit(solution)/shard_map/ppermute | solution.py:403
  47.7 17.7 %copy-start.2 = (bf16[8192,128]{1,0:T(8,128)(2,1)}, bf16[8192,128]{1,0:T(8,128)(2,1)S(1)}, u32[]{:S(2)}) copy-start(bf16[8192,128]{1,0:T(8,128)(2,1)S(1)} %collective-permute-done.10.refs_2_) | copy-start | bytes 6291460
  47.8 17.6 %copy-start.1 = (bf16[64,3072]{1,0:T(8,128)(2,1)}, bf16[64,3072]{1,0:T(8,128)(2,1)S(1)}, u32[]{:S(2)}) copy-start(bf16[64,3072]{1,0:T(8,128)(2,1)S(1)} %get-tuple-element.56.refs_5_) | copy-start | bytes 1179652
  47.8 32.0 %copy-start = (bf16[64,5120]{1,0:T(8,128)(2,1)}, bf16[64,5120]{1,0:T(8,128)(2,1)S(1)}, u32[]{:S(2)}) copy-start(bf16[64,5120]{1,0:T(8,128)(2,1)S(1)} %get-tuple-element.62.refs_5_) | copy-start | bytes 1966084
  47.8 11.5 %collective-permute-start.16 = (bf16[64,3072]{1,0:T(8,128)(2,1)S(1)}, bf16[64,3072]{1,0:T(8,128)(2,1)S(1)}, u32[]{:S(2)}, u32[]{:S(2)}) collective-permute-start(bf16[64,3072]{1,0:T(8,128)(2,1)S(1)} %get-tuple-element.56.refs_5_), channel_id=1, source_target_pairs={{0,24},{1,25},{2,26},{3,27},{4,28},{5,29},{6,30},{7,31},{8,0},{9,1... | collective-permute-start | bytes 1179656 | tf_op jit(solution)/shard_map/ppermute | solution.py:403
  50.3 12.5 %collective-permute-start.15 = (bf16[64,3072]{1,0:T(8,128)(2,1)S(1)}, bf16[64,3072]{1,0:T(8,128)(2,1)S(1)}, u32[]{:S(2)}, u32[]{:S(2)}) collective-permute-start(bf16[64,3072]{1,0:T(8,128)(2,1)S(1)} %get-tuple-element.56.refs_5_), channel_id=1, source_target_pairs={{0,8},{1,9},{2,10},{3,11},{4,12},{5,13},{6,14},{7,15},{8,16},{9,17... | collective-permute-start | bytes 1179656 | tf_op jit(solution)/shard_map/ppermute | solution.py:403
  50.3 12.5 %collective-permute-start.14 = (bf16[64,3072]{1,0:T(8,128)(2,1)S(1)}, bf16[64,3072]{1,0:T(8,128)(2,1)S(1)}, u32[]{:S(2)}, u32[]{:S(2)}) collective-permute-start(bf16[64,3072]{1,0:T(8,128)(2,1)S(1)} %get-tuple-element.56.refs_5_), channel_id=1, source_target_pairs={{0,16},{1,17},{2,18},{3,19},{4,20},{5,21},{6,22},{7,23},{8,24},{9,... | collective-permute-start | bytes 1179656 | tf_op jit(solution)/shard_map/ppermute | solution.py:403
  52.2 13.2 %collective-permute-start.13 = (bf16[3072,128]{1,0:T(8,128)(2,1)}, bf16[3072,128]{1,0:T(8,128)(2,1)}, u32[]{:S(2)}, u32[]{:S(2)}) collective-permute-start(bf16[3072,128]{1,0:T(8,128)(2,1)} %collective-permute-done.12.refs_3_), channel_id=1, source_target_pairs={{0,32},{1,33},{2,34},{3,35},{4,36},{5,37},{6,38},{7,39},{8,40},{9,... | collective-permute-start | bytes 2359304 | tf_op jit(solution)/shard_map/ppermute | solution.py:403
  59.3 6.1 %copy-start.4 = (bf16[64,3072]{1,0:T(8,128)(2,1)}, bf16[64,3072]{1,0:T(8,128)(2,1)S(1)}, u32[]{:S(2)}) copy-start(bf16[64,3072]{1,0:T(8,128)(2,1)S(1)} %collective-permute-done.16.refs_8_) | copy-start | bytes 1179652
  62.8 0.8 copy-start.5
  62.8 1.5 %copy-start.6 = (bf16[64,3072]{1,0:T(8,128)(2,1)}, bf16[64,3072]{1,0:T(8,128)(2,1)S(1)}, u32[]{:S(2)}) copy-start(bf16[64,3072]{1,0:T(8,128)(2,1)S(1)} %collective-permute-done.14.refs_6_) | copy-start | bytes 1179652
  62.8 17.5 %collective-permute-start.19 = (bf16[64,5120]{1,0:T(8,128)(2,1)S(1)}, bf16[64,5120]{1,0:T(8,128)(2,1)}, u32[]{:S(2)}, u32[]{:S(2)}) collective-permute-start(bf16[64,5120]{1,0:T(8,128)(2,1)S(1)} %get-tuple-element.62.refs_5_), channel_id=1, source_target_pairs={{0,24},{1,25},{2,26},{3,27},{4,28},{5,29},{6,30},{7,31},{8,0},{9,1... | collective-permute-start | bytes 1966088 | tf_op jit(solution)/shard_map/ppermute | solution.py:403
  63.5 18.1 %collective-permute-start.18 = (bf16[64,5120]{1,0:T(8,128)(2,1)S(1)}, bf16[64,5120]{1,0:T(8,128)(2,1)}, u32[]{:S(2)}, u32[]{:S(2)}) collective-permute-start(bf16[64,5120]{1,0:T(8,128)(2,1)S(1)} %get-tuple-element.62.refs_5_), channel_id=1, source_target_pairs={{0,8},{1,9},{2,10},{3,11},{4,12},{5,13},{6,14},{7,15},{8,16},{9,17... | collective-permute-start | bytes 1966088 | tf_op jit(solution)/shard_map/ppermute | solution.py:403
  64.3 17.3 %collective-permute-start.17 = (bf16[64,5120]{1,0:T(8,128)(2,1)S(1)}, bf16[64,5120]{1,0:T(8,128)(2,1)}, u32[]{:S(2)}, u32[]{:S(2)}) collective-permute-start(bf16[64,5120]{1,0:T(8,128)(2,1)S(1)} %get-tuple-element.62.refs_5_), channel_id=1, source_target_pairs={{0,16},{1,17},{2,18},{3,19},{4,20},{5,21},{6,22},{7,23},{8,24},{9,... | collective-permute-start | bytes 1966088 | tf_op jit(solution)/shard_map/ppermute | solution.py:403
  81.6 5.9 %collective-permute-start.20 = (bf16[5120,128]{1,0:T(8,128)(2,1)}, bf16[5120,128]{1,0:T(8,128)(2,1)S(1)}, u32[]{:S(2)}, u32[]{:S(2)}) collective-permute-start(bf16[5120,128]{1,0:T(8,128)(2,1)} %collective-permute-done.11.refs_3_), channel_id=1, source_target_pairs={{0,32},{1,33},{2,34},{3,35},{4,36},{5,37},{6,38},{7,39},{8,40},{9,... | collective-permute-start | bytes 3932168 | tf_op jit(solution)/shard_map/ppermute | solution.py:403
  87.5 1.1 %copy-start.3 = (bf16[5120,128]{1,0:T(8,128)(2,1)}, bf16[5120,128]{1,0:T(8,128)(2,1)S(1)}, u32[]{:S(2)}) copy-start(bf16[5120,128]{1,0:T(8,128)(2,1)S(1)} %collective-permute-done.20.refs_4_) | copy-start | bytes 3932164

commit v6 on v5

--- a/solution.py
+++ b/solution.py
@@ -50,7 +50,7 @@
 
 
 def spectra_kernel(
-    half, me_ref, ia, ib, ic, id_, x_hbm, start_hbm, qual_ref, y0_hbm, y1_hbm, y_hbm, sel_ref,
+    half, me_ref, ia, ib, ic, id_, x_hbm, start_hbm, qual_ref, y0_hbm, y1_hbm, y_hbm, stay_ref, away_ref,
     x_ref, start_ref, y_ref, state, table, spec, power, sems,
 ):
     ngrp = half // GRP
@@ -140,7 +140,8 @@
         picked = lax.dot_general(hot, value, (((1,), (1,)), ((), ())), preferred_element_type=jnp.float32)
         picked = picked.astype(jnp.bfloat16)
         for rel in range(4):
-            sel_ref[rel, :, lo * ROWS : hi * ROWS] = picked[rel * 2 : rel * 2 + 2]
+            out_ref = stay_ref if rel < 2 else away_ref
+            out_ref[rel % 2, :, lo * ROWS : hi * ROWS] = picked[rel * 2 : rel * 2 + 2]
         return copies
 
     first = CHUNKS[0] // GRP
@@ -168,10 +169,11 @@
             jax.ShapeDtypeStruct((CHUNKS[0] * 8, 128), jnp.bfloat16),
             jax.ShapeDtypeStruct((CHUNKS[1] * 8, 128), jnp.bfloat16),
             jax.ShapeDtypeStruct((NGRP * ROWS, 128), jnp.bfloat16),
-            jax.ShapeDtypeStruct((4, 2, NGRP * ROWS), jnp.bfloat16),
+            jax.ShapeDtypeStruct((2, 2, NGRP * ROWS), jnp.bfloat16),
+            jax.ShapeDtypeStruct((2, 2, NGRP * ROWS), jnp.bfloat16),
         ],
         in_specs=[smem] * 5 + [hbm, hbm, vmem],
-        out_specs=[hbm, hbm, hbm, vmem],
+        out_specs=[hbm, hbm, hbm, vmem, vmem],
         scratch_shapes=[
             pltpu.VMEM((4, length, 128), jnp.bfloat16),
             pltpu.VMEM((4, 8, length), jnp.float32),
@@ -228,17 +230,16 @@
     )(*pieces)
 
 
-UNROLL = 4
+UNROLL = 8
 HEAD = 128
 
 
 def correlate_kernel(first, last, kc, offset, *refs):
     where_ref, ya, yb, yc, yd, xa, xb, xc, xd, lag_ref, qual_ref = refs[:11]
     if first:
-        out_ref, ybuf, xbuf, xrow, cross, sems = refs[11:]
-        acc_ref = None
+        out_ref, ybuf, xbuf, xrow, cross, sems, table_ref, acc_ref, osem = refs[11:]
     else:
-        acc_hbm, out_ref, ybuf, xbuf, xrow, cross, sems, acc_ref, scale, stage, osem = refs[11:]
+        acc_hbm, out_ref, ybuf, xbuf, xrow, cross, sems, table_ref, acc_ref, scale, stage, osem = refs[11:]
     parts = ((0, HEAD), (HEAD, kc - HEAD))
     copies = []
     for k, (lo, size) in enumerate(parts):
@@ -252,9 +253,9 @@
         copies.append(some)
         for copy in some:
             copy.start()
+    later = [pltpu.make_async_copy(lag_ref, table_ref, sems.at[16])]
     if not first:
-        prefetch = pltpu.make_async_copy(acc_hbm, acc_ref, sems.at[16])
-        prefetch.start()
+        later.append(pltpu.make_async_copy(acc_hbm, acc_ref, sems.at[17]))
 
     rowid = lax.broadcasted_iota(jnp.int32, (16, 256), 0) % GRP
     lane = lax.broadcasted_iota(jnp.int32, (16, 256), 1) % GRP
@@ -302,11 +303,15 @@
             pair(m * UNROLL + v, v)
         return 0
 
-    for (lo, size), some in zip(parts, copies):
+    for k, ((lo, size), some) in enumerate(zip(parts, copies)):
         for copy in some:
             copy.wait()
+        if k:
+            for copy in later:
+                copy.start()
         lax.fori_loop(lo // 16 // UNROLL, (lo + size) // 16 // UNROLL, pairs, 0)
-    table = lag_ref[...]
+    later[0].wait()
+    table = table_ref[...]
     if last:
         flags = []
         for far in range(4):
@@ -316,10 +321,14 @@
         quality = qual_ref[...].astype(jnp.float32).astype(jnp.bfloat16)
         count = jnp.dot(flags, quality, preferred_element_type=jnp.float32)
         scale[...] = 1.0 / jnp.maximum(count, 1.0)
-        prefetch.wait()
+        later[1].wait()
 
     def flush(n, slot):
         return pltpu.make_async_copy(stage.at[slot], out_ref.at[:, pl.ds(pl.multiple_of(n * 8, 8), 8), :], osem.at[slot])
+
+    def save(n):
+        span = pl.ds(n * 8, 8)
+        return pltpu.make_async_copy(acc_ref.at[span], out_ref.at[span], osem.at[n])
 
     def lags(n, _):
         spots = [where_ref[n * 8 + j] for j in range(8)]
@@ -330,7 +339,7 @@
             parts += [prod[:, :128], prod[:, 128:]]
         if last:
             slot = n % 2
-            parts = [(part + acc_ref[p]) * scale[pl.ds(p, 1), :] for part, p in zip(parts, spots)]
+            parts = [(part + acc_ref[n * 8 + j]) * scale[pl.ds(spots[j], 1), :] for j, part in enumerate(parts)]
 
             @pl.when(n >= 2)
             def _():
@@ -339,14 +348,18 @@
             stage[slot] = pltpu.einshape("itj->tij", jnp.stack(parts, axis=0))[:NLAG]
             flush(n, slot).start()
         else:
-            for part, p in zip(parts, spots):
-                out_ref[p] = part
+            for j, part in enumerate(parts):
+                acc_ref[n * 8 + j] = part
+            save(n).start()
         return 0
 
     lax.fori_loop(0, 8, lags, 0)
     if last:
         flush(6, 0).wait()
         flush(7, 1).wait()
+    else:
+        for n in range(8):
+            save(n).wait()
 
 
 def correlate(first, last, kc, offset, where, ys, xs, table, qual_t, acc=None):
@@ -354,22 +367,24 @@
     hbm = pl.BlockSpec(memory_space=pl.ANY)
     vmem = pl.BlockSpec(memory_space=pltpu.VMEM)
     args = (where, *ys, *xs, table, qual_t)
-    in_specs = [smem] + [hbm] * 8 + [vmem, vmem]
+    in_specs = [smem] + [hbm] * 9 + [vmem]
     scratch = [
         pltpu.VMEM((4, kc * 8, 128), jnp.bfloat16),
         pltpu.VMEM((4, 64, kc * 8), jnp.bfloat16),
         pltpu.VMEM((UNROLL, 128, 256), jnp.float32),
         pltpu.VMEM((64, 2 * kc, 128), jnp.bfloat16),
-        pltpu.SemaphoreType.DMA((17,)),
+        pltpu.SemaphoreType.DMA((18,)),
+        pltpu.VMEM((TAU, 2 * kc), jnp.bfloat16),
+        pltpu.VMEM((64, TAU, 128), jnp.float32),
     ]
     if first:
-        out_shape, out_specs = (64, TAU, 128), vmem
+        out_shape, out_specs = (64, TAU, 128), hbm
+        scratch += [pltpu.SemaphoreType.DMA((8,))]
     else:
         out_shape, out_specs = (NLAG, 64, 128), hbm
         args += (acc,)
         in_specs += [hbm]
         scratch += [
-            pltpu.VMEM((64, TAU, 128), jnp.float32),
             pltpu.VMEM((64, 128), jnp.float32),
             pltpu.VMEM((2, NLAG, 8, 128), jnp.float32),
             pltpu.SemaphoreType.DMA((2,)),
@@ -450,9 +465,8 @@
         start += kc
 
     lists = [src_index] + [send(src_index, move) for move in (sibling, across, both)]
-    y0, y1, y, sel = spectra(samples, qual_t, spot, lists)
-
-    stay, away = sel[:2], sel[2:]
+    y0, y1, y, stay, away = spectra(samples, qual_t, spot, lists)
+
     out = [send(stay, beside), send(away, across), send(away, aside)]
     y0, y1, y, stay, *out = lax.optimization_barrier((y0, y1, y, stay, *out))
     far0 = send(y0, across)

time: 108 us -> 107 us (level)
  Pallas kernels: 45.5 us -> 41.3 us
  waiting for transfers between devices: 29.1 us -> 31.7 us
    pallas_call x2, Pallas kernels: 33.2 us -> 29 us  [correlate(): pl.pallas_call(functools.partial(correlate_kernel, first, last, kc, offse...]
    ppermute x21, waiting for transfers between devices: 29.1 us -> 31.7 us  [send(): return lax.ppermute(value, AXES, permutation(move))]
    unnamed x20 -> x22, local copies, waits for them, and re-layouts: 2.32 us -> 3.16 us
  transfers between devices with their start and end apart: 21 -> 21, of which waited for: 13 -> 13; matrix products, arithmetic and copies ran while one was open for 1% -> 1% of each run, Pallas kernels for 14% -> 11%
where the time goes in v6:
time: 107 us; the launch traced here: 106 us
  Pallas kernels  41.3 us (39%)
  waiting for transfers between devices  31.7 us (30%)
  starting transfers between devices  28.5 us (27%)
  local copies, waits for them, and re-layouts  3.16 us (3%)
  other arithmetic  1.25 us (1%)
    ppermute x21, waiting for transfers between devices, send(): return lax.ppermute(value, AXES, permutation(move))  31.7 us
    pallas_call x2, Pallas kernels, correlate(): pl.pallas_call(functools.partial(correlate_kernel, first, last, kc, offse...  29 us
    ppermute x21, starting transfers between devices, send(): return lax.ppermute(value, AXES, permutation(move))  28.5 us
    pallas_call x1, Pallas kernels, spectra(): pl.pallas_call(functools.partial(spectra_kernel, half), out_shape=[jax.Sh...  12.1 us
    unnamed x22, local copies, waits for them, and re-layouts  3.16 us
  transfers between devices with their start and end apart: 21, of which 13 were waited for; matrix products, arithmetic and copies ran while one was open for 1% of the time, Pallas kernels for 11%

profile of v6, /device:TPU:1, one launch (start us, length us, event | category | flops | bytes accessed | tf_op | source)
XLA Modules:
  0.0 106.3 jit_solution(15535373250321649231)
XLA Ops:
  0.0 4.4 %collective-permute-start.1 = (s32[64]{0:T(128)}, s32[64]{0:T(128)S(1)}, u32[]{:S(2)}, u32[]{:S(2)}) collective-permute-start(s32[64]{0:T(128)} %ia.1), channel_id=1, source_target_pairs={{0,64},{1,65},{2,66},{3,67},{4,68},{5,69},{6,70},{7,71},{8,72},{9,... | collective-permute-start | bytes 776 | tf_op jit(solution)/shard_map/ppermute | solution.py:418
  4.4 1.0 collective-permute-start
  5.4 0.0 collective-permute-start.2
  5.4 0.6 pad_add_fusion.me_ref
  6.0 0.0 collective-permute-done.1.ic
  6.0 0.3 collective-permute-done.ib
  6.3 3.6 %collective-permute-done.2.id_ = s32[64]{0:T(128)S(1)} collective-permute-done((s32[64]{0:T(128)}, s32[64]{0:T(128)S(1)}, u32[]{:S(2)}, u32[]{:S(2)}) %collective-permute-start.2) | collective-permute-done | bytes 288 | tf_op jit(solution)/shard_map/ppermute | solution.py:418
  10.0 0.5 copy-done.10
  10.5 12.1 %spectra.1 = (bf16[3072,128]{1,0:T(8,128)(2,1)}, bf16[5120,128]{1,0:T(8,128)(2,1)}, bf16[8192,128]{1,0:T(8,128)(2,1)}, bf16[2,2,8192]{2,1,0:T(2,128)(2,1)}, bf16[2,2,8192]{2,1,0:T(2,128)(2,1)}) custom-call(s32[2]{0:T(128)} %pad_add_fusion.me_ref, s32[64]{0:T(128)} %ia.1, s32[64]{0:T(128)} %copy-done.9, s32[64]{0:T(128)} %copy-done.8, s32[64]{0:T(128)} %copy-done.10, ...), custom_call_target="tpu_custom_call" | custom-call | flops 1100000 | bytes 1024 | tf_op jit(solution)/shard_map/spectra/pallas_call | solution.py:166
  22.6 0.8 collective-permute-start.3
  23.4 0.0 collective-permute-start.5
  23.4 2.5 %collective-permute-start.4 = (bf16[2,2,8192]{2,1,0:T(2,128)(2,1)}, bf16[2,2,8192]{2,1,0:T(2,128)(2,1)S(1)}, u32[]{:S(2)}, u32[]{:S(2)}) collective-permute-start(bf16[2,2,8192]{2,1,0:T(2,128)(2,1)} %get-tuple-element.41), channel_id=1, source_target_pairs={{0,64},{1,65},{2,66},{3,67},{4,68},{5,69},{6,70},{7,71},{8,72},{9,... | collective-permute-start | bytes 196616 | tf_op jit(solution)/shard_map/ppermute | solution.py:418
  25.9 0.7 collective-permute-done.3.refs_1_
  26.6 3.4 %collective-permute-done.5.refs_3_ = bf16[2,2,8192]{2,1,0:T(2,128)(2,1)S(1)} collective-permute-done((bf16[2,2,8192]{2,1,0:T(2,128)(2,1)}, bf16[2,2,8192]{2,1,0:T(2,128)(2,1)S(1)}, u32[]{:S(2)}, u32[]{:S(2)}) %collective-permute-start.5) | collective-permute-done | bytes 65568 | tf_op jit(solution)/shard_map/ppermute | solution.py:418
  30.0 0.0 collective-permute-done.4.refs_2_
  30.0 0.8 collective-permute-start.10
  30.7 0.8 copy-done.2
  31.6 0.1 join_column.1
  31.7 0.1 collective-permute-start.6
  31.8 1.8 %collective-permute-start.12 = (bf16[3072,128]{1,0:T(8,128)(2,1)}, bf16[3072,128]{1,0:T(8,128)(2,1)}, u32[]{:S(2)}, u32[]{:S(2)}) collective-permute-start(bf16[3072,128]{1,0:T(8,128)(2,1)} %get-tuple-element.51), channel_id=1, source_target_pairs={{0,64},{1,65},{2,66},{3,67},{4,68},{5,69},{6,70},{7,71},{8,72},{9,... | collective-permute-start | bytes 2359304 | tf_op jit(solution)/shard_map/ppermute | solution.py:418
  33.6 1.1 %collective-permute-done.6.refs_1_ = bf16[8,8192]{1,0:T(8,128)(2,1)S(1)} collective-permute-done((bf16[8,8192]{1,0:T(8,128)(2,1)S(1)}, bf16[8,8192]{1,0:T(8,128)(2,1)S(1)}, u32[]{:S(2)}, u32[]{:S(2)}) %collective-permute-start.6) | collective-permute-done | bytes 131104 | tf_op jit(solution)/shard_map/ppermute | solution.py:418
  34.7 2.8 %collective-permute-start.9 = (bf16[16,8192]{1,0:T(8,128)(2,1)S(1)}, bf16[16,8192]{1,0:T(8,128)(2,1)S(1)}, u32[]{:S(2)}, u32[]{:S(2)}) collective-permute-start(bf16[16,8192]{1,0:T(8,128)(2,1)S(1)} %join_cores.1.pa), channel_id=1, source_target_pairs={{0,3},{1,0},{2,1},{3,2},{4,7},{5,4},{6,5},{7,6},{8,11},{9,8},{10,9... | collective-permute-start | bytes 786440 | tf_op jit(solution)/shard_map/ppermute | solution.py:418
  37.5 0.0 collective-permute-start.8
  37.5 1.6 %collective-permute-start.7 = (bf16[16,8192]{1,0:T(8,128)(2,1)S(1)}, bf16[16,8192]{1,0:T(8,128)(2,1)S(1)}, u32[]{:S(2)}, u32[]{:S(2)}) collective-permute-start(bf16[16,8192]{1,0:T(8,128)(2,1)S(1)} %join_cores.1.pa), channel_id=1, source_target_pairs={{0,2},{1,3},{2,0},{3,1},{4,6},{5,7},{6,4},{7,5},{8,10},{9,11},{10,... | collective-permute-start | bytes 786440 | tf_op jit(solution)/shard_map/ppermute | solution.py:418
  39.2 1.7 %collective-permute-done.9.pd = bf16[16,8192]{1,0:T(8,128)(2,1)S(1)} collective-permute-done((bf16[16,8192]{1,0:T(8,128)(2,1)S(1)}, bf16[16,8192]{1,0:T(8,128)(2,1)S(1)}, u32[]{:S(2)}, u32[]{:S(2)}) %collective-permute-start.9) | collective-permute-done | bytes 262176 | tf_op jit(solution)/shard_map/ppermute | solution.py:418
  40.8 1.7 %collective-permute-start.11 = (bf16[5120,128]{1,0:T(8,128)(2,1)}, bf16[5120,128]{1,0:T(8,128)(2,1)}, u32[]{:S(2)}, u32[]{:S(2)}) collective-permute-start(bf16[5120,128]{1,0:T(8,128)(2,1)} %get-tuple-element.50), channel_id=1, source_target_pairs={{0,64},{1,65},{2,66},{3,67},{4,68},{5,69},{6,70},{7,71},{8,72},{9,... | collective-permute-start | bytes 3932168 | tf_op jit(solution)/shard_map/ppermute | solution.py:418
  42.6 4.6 %collective-permute-done.8.pc = bf16[16,8192]{1,0:T(8,128)(2,1)S(1)} collective-permute-done((bf16[16,8192]{1,0:T(8,128)(2,1)S(1)}, bf16[16,8192]{1,0:T(8,128)(2,1)S(1)}, u32[]{:S(2)}, u32[]{:S(2)}) %collective-permute-start.8) | collective-permute-done | bytes 262176 | tf_op jit(solution)/shard_map/ppermute | solution.py:418
  47.2 0.0 collective-permute-done.7.pb
  47.2 0.1 split.1
  47.3 2.5 %collective-permute-start.16 = (bf16[64,3072]{1,0:T(8,128)(2,1)S(1)}, bf16[64,3072]{1,0:T(8,128)(2,1)S(1)}, u32[]{:S(2)}, u32[]{:S(2)}) collective-permute-start(bf16[64,3072]{1,0:T(8,128)(2,1)S(1)} %get-tuple-element.58.refs_5_), channel_id=1, source_target_pairs={{0,24},{1,25},{2,26},{3,27},{4,28},{5,29},{6,30},{7,31},{8,0},{9,1... | collective-permute-start | bytes 1179656 | tf_op jit(solution)/shard_map/ppermute | solution.py:418
  49.8 1.7 %collective-permute-start.14 = (bf16[64,3072]{1,0:T(8,128)(2,1)S(1)}, bf16[64,3072]{1,0:T(8,128)(2,1)S(1)}, u32[]{:S(2)}, u32[]{:S(2)}) collective-permute-start(bf16[64,3072]{1,0:T(8,128)(2,1)S(1)} %get-tuple-element.58.refs_5_), channel_id=1, source_target_pairs={{0,16},{1,17},{2,18},{3,19},{4,20},{5,21},{6,22},{7,23},{8,24},{9,... | collective-permute-start | bytes 1179656 | tf_op jit(solution)/shard_map/ppermute | solution.py:418
  51.6 0.8 collective-permute-done.12.refs_3_
  52.4 2.1 %collective-permute-start.13 = (bf16[3072,128]{1,0:T(8,128)(2,1)}, bf16[3072,128]{1,0:T(8,128)(2,1)}, u32[]{:S(2)}, u32[]{:S(2)}) collective-permute-start(bf16[3072,128]{1,0:T(8,128)(2,1)} %collective-permute-done.12.refs_3_), channel_id=1, source_target_pairs={{0,32},{1,33},{2,34},{3,35},{4,36},{5,37},{6,38},{7,39},{8,40},{9,... | collective-permute-start | bytes 2359304 | tf_op jit(solution)/shard_map/ppermute | solution.py:418
  54.5 4.2 %collective-permute-done.16.refs_8_ = bf16[64,3072]{1,0:T(8,128)(2,1)S(1)} collective-permute-done((bf16[64,3072]{1,0:T(8,128)(2,1)S(1)}, bf16[64,3072]{1,0:T(8,128)(2,1)S(1)}, u32[]{:S(2)}, u32[]{:S(2)}) %collective-permute-start.16) | collective-permute-done | bytes 393248 | tf_op jit(solution)/shard_map/ppermute | solution.py:418
  58.8 3.5 %collective-permute-done.15.refs_7_ = bf16[64,3072]{1,0:T(8,128)(2,1)S(1)} collective-permute-done((bf16[64,3072]{1,0:T(8,128)(2,1)S(1)}, bf16[64,3072]{1,0:T(8,128)(2,1)S(1)}, u32[]{:S(2)}, u32[]{:S(2)}) %collective-permute-start.15) | collective-permute-done | bytes 393248 | tf_op jit(solution)/shard_map/ppermute | solution.py:418
  62.3 0.1 collective-permute-start.19
  62.4 0.7 copy-done.6
  63.0 0.8 collective-permute-start.18
  63.8 0.4 collective-permute-start.17
  64.3 0.6 fusion.refs_0_
  64.9 11.3 %correlate_first.1.refs_11_ = f32[64,208,128]{2,1,0:T(8,128)} custom-call(s32[64]{0:T(128)} %fusion.refs_0_, bf16[8192,128]{1,0:T(8,128)(2,1)} %get-tuple-element.42.refs_1_, bf16[8192,128]{1,0:T(8,128)(2,1)} %copy-done.3, bf16[3072,128]{1,0:T(8,128)(2,1)} %collective-permute-done.12.refs_3_, bf16[3072,128]{1,0:T(8,128)(2,1)} %collective-permute-done.13.refs_4_, ...), custom_call_target="tpu_custom_call" | custom-call | flops 1100000 | bytes 1024 | tf_op jit(solution)/shard_map/correlate_first/pallas_call | solution.py:392
  76.2 4.3 %collective-permute-done.11.refs_3_ = bf16[5120,128]{1,0:T(8,128)(2,1)} collective-permute-done((bf16[5120,128]{1,0:T(8,128)(2,1)}, bf16[5120,128]{1,0:T(8,128)(2,1)}, u32[]{:S(2)}, u32[]{:S(2)}) %collective-permute-start.11) | collective-permute-done | bytes 1310752 | tf_op jit(solution)/shard_map/ppermute | solution.py:418
  80.5 0.0 collective-permute-done.19.refs_8_
  80.5 0.6 collective-permute-done.18.refs_7_
  81.1 3.3 %collective-permute-start.20 = (bf16[5120,128]{1,0:T(8,128)(2,1)}, bf16[5120,128]{1,0:T(8,128)(2,1)S(1)}, u32[]{:S(2)}, u32[]{:S(2)}) collective-permute-start(bf16[5120,128]{1,0:T(8,128)(2,1)} %collective-permute-done.11.refs_3_), channel_id=1, source_target_pairs={{0,32},{1,33},{2,34},{3,35},{4,36},{5,37},{6,38},{7,39},{8,40},{9,... | collective-permute-start | bytes 3932168 | tf_op jit(solution)/shard_map/ppermute | solution.py:418
  84.4 2.9 %collective-permute-done.20.refs_4_ = bf16[5120,128]{1,0:T(8,128)(2,1)S(1)} collective-permute-done((bf16[5120,128]{1,0:T(8,128)(2,1)}, bf16[5120,128]{1,0:T(8,128)(2,1)S(1)}, u32[]{:S(2)}, u32[]{:S(2)}) %collective-permute-start.20) | collective-permute-done | bytes 1310752 | tf_op jit(solution)/shard_map/ppermute | solution.py:418
  87.3 1.1 %copy-done.4 = bf16[5120,128]{1,0:T(8,128)(2,1)} copy-done((bf16[5120,128]{1,0:T(8,128)(2,1)}, bf16[5120,128]{1,0:T(8,128)(2,1)S(1)}, u32[]{:S(2)}) %copy-start.4) | copy-done | bytes 1310744
  88.4 17.7 %correlate_last.1 = f32[201,64,128]{2,1,0:T(8,128)} custom-call(s32[64]{0:T(128)} %fusion.refs_0_, bf16[8192,128]{1,0:T(8,128)(2,1)} %get-tuple-element.42.refs_1_, bf16[8192,128]{1,0:T(8,128)(2,1)} %copy-done.3, bf16[5120,128]{1,0:T(8,128)(2,1)} %collective-permute-done.11.refs_3_, bf16[5120,128]{1,0:T(8,128)(2,1)} %copy-done.4, bf16[64,5120]{1,0:T(8,128)(2,1)} %copy-done, ...), custom_call_target="tpu_custom_call" | custom-call | flops 1100000 | bytes 1024 | tf_op jit(solution)/shard_map/correlate_last/pallas_call | solution.py:392
  (24 shorter events, 0.1 us)
Async XLA Ops:
  0.0 6.0 %collective-permute-start.1 = (s32[64]{0:T(128)}, s32[64]{0:T(128)S(1)}, u32[]{:S(2)}, u32[]{:S(2)}) collective-permute-start(s32[64]{0:T(128)} %ia.1), channel_id=1, source_target_pairs={{0,64},{1,65},{2,66},{3,67},{4,68},{5,69},{6,70},{7,71},{8,72},{9,... | collective-permute-start | bytes 776 | tf_op jit(solution)/shard_map/ppermute | solution.py:418
  4.4 1.9 %collective-permute-start = (s32[64]{0:T(128)}, s32[64]{0:T(128)S(1)}, u32[]{:S(2)}, u32[]{:S(2)}) collective-permute-start(s32[64]{0:T(128)} %ia.1), channel_id=1, source_target_pairs={{0,32},{1,33},{2,34},{3,35},{4,36},{5,37},{6,38},{7,39},{8,40},{9,... | collective-permute-start | bytes 776 | tf_op jit(solution)/shard_map/ppermute | solution.py:418
  5.4 4.6 %collective-permute-start.2 = (s32[64]{0:T(128)}, s32[64]{0:T(128)S(1)}, u32[]{:S(2)}, u32[]{:S(2)}) collective-permute-start(s32[64]{0:T(128)} %ia.1), channel_id=1, source_target_pairs={{0,96},{1,97},{2,98},{3,99},{4,100},{5,101},{6,102},{7,103},{8,104... | collective-permute-start | bytes 776 | tf_op jit(solution)/shard_map/ppermute | solution.py:418
  6.0 4.0 %copy-start.8 = (s32[64]{0:T(128)}, s32[64]{0:T(128)S(1)}, u32[]{:S(2)}) copy-start(s32[64]{0:T(128)S(1)} %collective-permute-done.1.ic) | copy-start | bytes 772
  6.3 3.7 %copy-start.9 = (s32[64]{0:T(128)}, s32[64]{0:T(128)S(1)}, u32[]{:S(2)}) copy-start(s32[64]{0:T(128)S(1)} %collective-permute-done.ib) | copy-start | bytes 772
  10.0 0.5 copy-start.10
  22.6 4.0 %collective-permute-start.3 = (bf16[2,2,8192]{2,1,0:T(2,128)(2,1)}, bf16[2,2,8192]{2,1,0:T(2,128)(2,1)S(1)}, u32[]{:S(2)}, u32[]{:S(2)}) collective-permute-start(bf16[2,2,8192]{2,1,0:T(2,128)(2,1)} %get-tuple-element.43.refs_0_), channel_id=1, source_target_pairs={{0,4},{1,5},{2,6},{3,7},{4,0},{5,1},{6,2},{7,3},{8,12},{9,13},{10,... | collective-permute-start | bytes 196616 | tf_op jit(solution)/shard_map/ppermute | solution.py:418
  23.4 6.6 %collective-permute-start.5 = (bf16[2,2,8192]{2,1,0:T(2,128)(2,1)}, bf16[2,2,8192]{2,1,0:T(2,128)(2,1)S(1)}, u32[]{:S(2)}, u32[]{:S(2)}) collective-permute-start(bf16[2,2,8192]{2,1,0:T(2,128)(2,1)} %get-tuple-element.41), channel_id=1, source_target_pairs={{0,68},{1,69},{2,70},{3,71},{4,64},{5,65},{6,66},{7,67},{8,76},{9,... | collective-permute-start | bytes 196616 | tf_op jit(solution)/shard_map/ppermute | solution.py:418
  23.4 6.6 %collective-permute-start.4 = (bf16[2,2,8192]{2,1,0:T(2,128)(2,1)}, bf16[2,2,8192]{2,1,0:T(2,128)(2,1)S(1)}, u32[]{:S(2)}, u32[]{:S(2)}) collective-permute-start(bf16[2,2,8192]{2,1,0:T(2,128)(2,1)} %get-tuple-element.41), channel_id=1, source_target_pairs={{0,64},{1,65},{2,66},{3,67},{4,68},{5,69},{6,70},{7,71},{8,72},{9,... | collective-permute-start | bytes 196616 | tf_op jit(solution)/shard_map/ppermute | solution.py:418
  30.0 17.2 %collective-permute-start.10 = (bf16[8192,128]{1,0:T(8,128)(2,1)}, bf16[8192,128]{1,0:T(8,128)(2,1)S(1)}, u32[]{:S(2)}, u32[]{:S(2)}) collective-permute-start(bf16[8192,128]{1,0:T(8,128)(2,1)} %get-tuple-element.42.refs_1_), channel_id=1, source_target_pairs={{0,32},{1,33},{2,34},{3,35},{4,36},{5,37},{6,38},{7,39},{8,40},{9,... | collective-permute-start | bytes 6291464 | tf_op jit(solution)/shard_map/ppermute | solution.py:418
  30.7 0.8 copy-start.2
  31.7 3.0 %collective-permute-start.6 = (bf16[8,8192]{1,0:T(8,128)(2,1)S(1)}, bf16[8,8192]{1,0:T(8,128)(2,1)S(1)}, u32[]{:S(2)}, u32[]{:S(2)}) collective-permute-start(bf16[8,8192]{1,0:T(8,128)(2,1)S(1)} %get-tuple-element.48), channel_id=1, source_target_pairs={{0,32},{1,33},{2,34},{3,35},{4,36},{5,37},{6,38},{7,39},{8,40},{9,... | collective-permute-start | bytes 393224 | tf_op jit(solution)/shard_map/ppermute | solution.py:418
  31.8 20.6 %collective-permute-start.12 = (bf16[3072,128]{1,0:T(8,128)(2,1)}, bf16[3072,128]{1,0:T(8,128)(2,1)}, u32[]{:S(2)}, u32[]{:S(2)}) collective-permute-start(bf16[3072,128]{1,0:T(8,128)(2,1)} %get-tuple-element.51), channel_id=1, source_target_pairs={{0,64},{1,65},{2,66},{3,67},{4,68},{5,69},{6,70},{7,71},{8,72},{9,... | collective-permute-start | bytes 2359304 | tf_op jit(solution)/shard_map/ppermute | solution.py:418
  34.7 6.1 %collective-permute-start.9 = (bf16[16,8192]{1,0:T(8,128)(2,1)S(1)}, bf16[16,8192]{1,0:T(8,128)(2,1)S(1)}, u32[]{:S(2)}, u32[]{:S(2)}) collective-permute-start(bf16[16,8192]{1,0:T(8,128)(2,1)S(1)} %join_cores.1.pa), channel_id=1, source_target_pairs={{0,3},{1,0},{2,1},{3,2},{4,7},{5,4},{6,5},{7,6},{8,11},{9,8},{10,9... | collective-permute-start | bytes 786440 | tf_op jit(solution)/shard_map/ppermute | solution.py:418
  37.5 9.6 %collective-permute-start.8 = (bf16[16,8192]{1,0:T(8,128)(2,1)S(1)}, bf16[16,8192]{1,0:T(8,128)(2,1)S(1)}, u32[]{:S(2)}, u32[]{:S(2)}) collective-permute-start(bf16[16,8192]{1,0:T(8,128)(2,1)S(1)} %join_cores.1.pa), channel_id=1, source_target_pairs={{0,1},{1,2},{2,3},{3,0},{4,5},{5,6},{6,7},{7,4},{8,9},{9,10},{10,1... | collective-permute-start | bytes 786440 | tf_op jit(solution)/shard_map/ppermute | solution.py:418
  37.5 9.6 %collective-permute-start.7 = (bf16[16,8192]{1,0:T(8,128)(2,1)S(1)}, bf16[16,8192]{1,0:T(8,128)(2,1)S(1)}, u32[]{:S(2)}, u32[]{:S(2)}) collective-permute-start(bf16[16,8192]{1,0:T(8,128)(2,1)S(1)} %join_cores.1.pa), channel_id=1, source_target_pairs={{0,2},{1,3},{2,0},{3,1},{4,6},{5,7},{6,4},{7,5},{8,10},{9,11},{10,... | collective-permute-start | bytes 786440 | tf_op jit(solution)/shard_map/ppermute | solution.py:418
  40.8 39.7 %collective-permute-start.11 = (bf16[5120,128]{1,0:T(8,128)(2,1)}, bf16[5120,128]{1,0:T(8,128)(2,1)}, u32[]{:S(2)}, u32[]{:S(2)}) collective-permute-start(bf16[5120,128]{1,0:T(8,128)(2,1)} %get-tuple-element.50), channel_id=1, source_target_pairs={{0,64},{1,65},{2,66},{3,67},{4,68},{5,69},{6,70},{7,71},{8,72},{9,... | collective-permute-start | bytes 3932168 | tf_op jit(solution)/shard_map/ppermute | solution.py:418
  47.2 17.7 %copy-start.3 = (bf16[8192,128]{1,0:T(8,128)(2,1)}, bf16[8192,128]{1,0:T(8,128)(2,1)S(1)}, u32[]{:S(2)}) copy-start(bf16[8192,128]{1,0:T(8,128)(2,1)S(1)} %collective-permute-done.10.refs_2_) | copy-start | bytes 6291460
  47.3 17.6 %copy-start.1 = (bf16[64,3072]{1,0:T(8,128)(2,1)}, bf16[64,3072]{1,0:T(8,128)(2,1)S(1)}, u32[]{:S(2)}) copy-start(bf16[64,3072]{1,0:T(8,128)(2,1)S(1)} %get-tuple-element.58.refs_5_) | copy-start | bytes 1179652
  47.3 29.0 %copy-start = (bf16[64,5120]{1,0:T(8,128)(2,1)}, bf16[64,5120]{1,0:T(8,128)(2,1)S(1)}, u32[]{:S(2)}) copy-start(bf16[64,5120]{1,0:T(8,128)(2,1)S(1)} %get-tuple-element.64.refs_5_) | copy-start | bytes 1966084
  47.3 11.5 %collective-permute-start.16 = (bf16[64,3072]{1,0:T(8,128)(2,1)S(1)}, bf16[64,3072]{1,0:T(8,128)(2,1)S(1)}, u32[]{:S(2)}, u32[]{:S(2)}) collective-permute-start(bf16[64,3072]{1,0:T(8,128)(2,1)S(1)} %get-tuple-element.58.refs_5_), channel_id=1, source_target_pairs={{0,24},{1,25},{2,26},{3,27},{4,28},{5,29},{6,30},{7,31},{8,0},{9,1... | collective-permute-start | bytes 1179656 | tf_op jit(solution)/shard_map/ppermute | solution.py:418
  49.8 12.5 %collective-permute-start.15 = (bf16[64,3072]{1,0:T(8,128)(2,1)S(1)}, bf16[64,3072]{1,0:T(8,128)(2,1)S(1)}, u32[]{:S(2)}, u32[]{:S(2)}) collective-permute-start(bf16[64,3072]{1,0:T(8,128)(2,1)S(1)} %get-tuple-element.58.refs_5_), channel_id=1, source_target_pairs={{0,8},{1,9},{2,10},{3,11},{4,12},{5,13},{6,14},{7,15},{8,16},{9,17... | collective-permute-start | bytes 1179656 | tf_op jit(solution)/shard_map/ppermute | solution.py:418
  49.8 12.5 %collective-permute-start.14 = (bf16[64,3072]{1,0:T(8,128)(2,1)S(1)}, bf16[64,3072]{1,0:T(8,128)(2,1)S(1)}, u32[]{:S(2)}, u32[]{:S(2)}) collective-permute-start(bf16[64,3072]{1,0:T(8,128)(2,1)S(1)} %get-tuple-element.58.refs_5_), channel_id=1, source_target_pairs={{0,16},{1,17},{2,18},{3,19},{4,20},{5,21},{6,22},{7,23},{8,24},{9,... | collective-permute-start | bytes 1179656 | tf_op jit(solution)/shard_map/ppermute | solution.py:418
  52.4 12.5 %collective-permute-start.13 = (bf16[3072,128]{1,0:T(8,128)(2,1)}, bf16[3072,128]{1,0:T(8,128)(2,1)}, u32[]{:S(2)}, u32[]{:S(2)}) collective-permute-start(bf16[3072,128]{1,0:T(8,128)(2,1)} %collective-permute-done.12.refs_3_), channel_id=1, source_target_pairs={{0,32},{1,33},{2,34},{3,35},{4,36},{5,37},{6,38},{7,39},{8,40},{9,... | collective-permute-start | bytes 2359304 | tf_op jit(solution)/shard_map/ppermute | solution.py:418
  58.8 6.1 %copy-start.5 = (bf16[64,3072]{1,0:T(8,128)(2,1)}, bf16[64,3072]{1,0:T(8,128)(2,1)S(1)}, u32[]{:S(2)}) copy-start(bf16[64,3072]{1,0:T(8,128)(2,1)S(1)} %collective-permute-done.16.refs_8_) | copy-start | bytes 1179652
  62.3 0.8 copy-start.6
  62.3 1.5 %copy-start.7 = (bf16[64,3072]{1,0:T(8,128)(2,1)}, bf16[64,3072]{1,0:T(8,128)(2,1)S(1)}, u32[]{:S(2)}) copy-start(bf16[64,3072]{1,0:T(8,128)(2,1)S(1)} %collective-permute-done.14.refs_6_) | copy-start | bytes 1179652
  62.3 18.2 %collective-permute-start.19 = (bf16[64,5120]{1,0:T(8,128)(2,1)S(1)}, bf16[64,5120]{1,0:T(8,128)(2,1)}, u32[]{:S(2)}, u32[]{:S(2)}) collective-permute-start(bf16[64,5120]{1,0:T(8,128)(2,1)S(1)} %get-tuple-element.64.refs_5_), channel_id=1, source_target_pairs={{0,24},{1,25},{2,26},{3,27},{4,28},{5,29},{6,30},{7,31},{8,0},{9,1... | collective-permute-start | bytes 1966088 | tf_op jit(solution)/shard_map/ppermute | solution.py:418
  63.0 18.1 %collective-permute-start.18 = (bf16[64,5120]{1,0:T(8,128)(2,1)S(1)}, bf16[64,5120]{1,0:T(8,128)(2,1)}, u32[]{:S(2)}, u32[]{:S(2)}) collective-permute-start(bf16[64,5120]{1,0:T(8,128)(2,1)S(1)} %get-tuple-element.64.refs_5_), channel_id=1, source_target_pairs={{0,8},{1,9},{2,10},{3,11},{4,12},{5,13},{6,14},{7,15},{8,16},{9,17... | collective-permute-start | bytes 1966088 | tf_op jit(solution)/shard_map/ppermute | solution.py:418
  63.8 17.3 %collective-permute-start.17 = (bf16[64,5120]{1,0:T(8,128)(2,1)S(1)}, bf16[64,5120]{1,0:T(8,128)(2,1)}, u32[]{:S(2)}, u32[]{:S(2)}) collective-permute-start(bf16[64,5120]{1,0:T(8,128)(2,1)S(1)} %get-tuple-element.64.refs_5_), channel_id=1, source_target_pairs={{0,16},{1,17},{2,18},{3,19},{4,20},{5,21},{6,22},{7,23},{8,24},{9,... | collective-permute-start | bytes 1966088 | tf_op jit(solution)/shard_map/ppermute | solution.py:418
  81.1 6.2 %collective-permute-start.20 = (bf16[5120,128]{1,0:T(8,128)(2,1)}, bf16[5120,128]{1,0:T(8,128)(2,1)S(1)}, u32[]{:S(2)}, u32[]{:S(2)}) collective-permute-start(bf16[5120,128]{1,0:T(8,128)(2,1)} %collective-permute-done.11.refs_3_), channel_id=1, source_target_pairs={{0,32},{1,33},{2,34},{3,35},{4,36},{5,37},{6,38},{7,39},{8,40},{9,... | collective-permute-start | bytes 3932168 | tf_op jit(solution)/shard_map/ppermute | solution.py:418
  87.3 1.1 %copy-start.4 = (bf16[5120,128]{1,0:T(8,128)(2,1)}, bf16[5120,128]{1,0:T(8,128)(2,1)S(1)}, u32[]{:S(2)}) copy-start(bf16[5120,128]{1,0:T(8,128)(2,1)S(1)} %collective-permute-done.20.refs_4_) | copy-start | bytes 3932164

commit v7 on v6

--- a/solution.py
+++ b/solution.py
@@ -46,7 +46,7 @@
 
 
 DBLK = 25
-CHUNKS = (384, 640)
+CHUNKS = (448, 576)
 
 
 def spectra_kernel(
@@ -231,7 +231,7 @@
 
 
 UNROLL = 8
-HEAD = 128
+HEAD = 64
 
 
 def correlate_kernel(first, last, kc, offset, *refs):
@@ -300,7 +300,7 @@
 
     def pairs(m, _):
         for v in range(UNROLL):
-            pair(m * UNROLL + v, v)
+            pair(HEAD // 16 + m * UNROLL + v, v)
         return 0
 
     for k, ((lo, size), some) in enumerate(zip(parts, copies)):
@@ -309,7 +309,11 @@
         if k:
             for copy in later:
                 copy.start()
-        lax.fori_loop(lo // 16 // UNROLL, (lo + size) // 16 // UNROLL, pairs, 0)
+        if k:
+            lax.fori_loop(0, size // 16 // UNROLL, pairs, 0)
+        else:
+            for v in range(HEAD // 16):
+                pair(v, v)
     later[0].wait()
     table = table_ref[...]
     if last:

time: 107 us -> 106 us (level)
  Pallas kernels: 41.3 us -> 43.3 us
  waiting for transfers between devices: 31.7 us -> 29.9 us
    pallas_call x2, Pallas kernels: 29 us -> 31.1 us  [correlate(): pl.pallas_call(functools.partial(correlate_kernel, first, last, kc, offse...]
    ppermute x21, waiting for transfers between devices: 31.7 us -> 29.9 us  [send(): return lax.ppermute(value, AXES, permutation(move))]
  transfers between devices with their start and end apart: 21 -> 21, of which waited for: 13 -> 12; matrix products, arithmetic and copies ran while one was open for 1% -> 1% of each run, Pallas kernels for 11% -> 13%
where the time goes in v7:
time: 106 us; the launch traced here: 105 us
  Pallas kernels  43.3 us (41%)
  waiting for transfers between devices  29.9 us (28%)
  starting transfers between devices  28.2 us (27%)
  local copies, waits for them, and re-layouts  2.47 us (2%)
  other arithmetic  1.19 us (1%)
    pallas_call x2, Pallas kernels, correlate(): pl.pallas_call(functools.partial(correlate_kernel, first, last, kc, offse...  31.1 us
    ppermute x21, waiting for transfers between devices, send(): return lax.ppermute(value, AXES, permutation(move))  29.9 us
    ppermute x21, starting transfers between devices, send(): return lax.ppermute(value, AXES, permutation(move))  28.2 us
    pallas_call x1, Pallas kernels, spectra(): pl.pallas_call(functools.partial(spectra_kernel, half), out_shape=[jax.Sh...  12 us
    unnamed x22, local copies, waits for them, and re-layouts  2.47 us
  transfers between devices with their start and end apart: 21, of which 12 were waited for; matrix products, arithmetic and copies ran while one was open for 1% of the time, Pallas kernels for 13%

profile of v7, /device:TPU:1, one launch (start us, length us, event | category | flops | bytes accessed | tf_op | source)
XLA Modules:
  0.0 105.3 jit_solution(1439226446536610393)
XLA Ops:
  0.0 4.4 %collective-permute-start.1 = (s32[64]{0:T(128)}, s32[64]{0:T(128)S(1)}, u32[]{:S(2)}, u32[]{:S(2)}) collective-permute-start(s32[64]{0:T(128)} %ia.1), channel_id=1, source_target_pairs={{0,64},{1,65},{2,66},{3,67},{4,68},{5,69},{6,70},{7,71},{8,72},{9,... | collective-permute-start | bytes 776 | tf_op jit(solution)/shard_map/ppermute | solution.py:422
  4.4 1.0 collective-permute-start
  5.4 0.0 collective-permute-start.2
  5.4 0.6 pad_add_fusion.me_ref
  6.0 0.0 collective-permute-done.1.ic
  6.0 0.4 collective-permute-done.ib
  6.3 3.6 %collective-permute-done.2.id_ = s32[64]{0:T(128)S(1)} collective-permute-done((s32[64]{0:T(128)}, s32[64]{0:T(128)S(1)}, u32[]{:S(2)}, u32[]{:S(2)}) %collective-permute-start.2) | collective-permute-done | bytes 288 | tf_op jit(solution)/shard_map/ppermute | solution.py:422
  10.0 0.5 copy-done.10
  10.5 12.0 %spectra.1 = (bf16[3584,128]{1,0:T(8,128)(2,1)}, bf16[4608,128]{1,0:T(8,128)(2,1)}, bf16[8192,128]{1,0:T(8,128)(2,1)}, bf16[2,2,8192]{2,1,0:T(2,128)(2,1)}, bf16[2,2,8192]{2,1,0:T(2,128)(2,1)}) custom-call(s32[2]{0:T(128)} %pad_add_fusion.me_ref, s32[64]{0:T(128)} %ia.1, s32[64]{0:T(128)} %copy-done.9, s32[64]{0:T(128)} %copy-done.8, s32[64]{0:T(128)} %copy-done.10, ...), custom_call_target="tpu_custom_call" | custom-call | flops 1100000 | bytes 1024 | tf_op jit(solution)/shard_map/spectra/pallas_call | solution.py:166
  22.5 0.8 collective-permute-start.3
  23.3 0.0 collective-permute-start.5
  23.3 2.5 %collective-permute-start.4 = (bf16[2,2,8192]{2,1,0:T(2,128)(2,1)}, bf16[2,2,8192]{2,1,0:T(2,128)(2,1)S(1)}, u32[]{:S(2)}, u32[]{:S(2)}) collective-permute-start(bf16[2,2,8192]{2,1,0:T(2,128)(2,1)} %get-tuple-element.41), channel_id=1, source_target_pairs={{0,64},{1,65},{2,66},{3,67},{4,68},{5,69},{6,70},{7,71},{8,72},{9,... | collective-permute-start | bytes 196616 | tf_op jit(solution)/shard_map/ppermute | solution.py:422
  25.8 0.7 collective-permute-done.3.refs_1_
  26.5 3.4 %collective-permute-done.5.refs_3_ = bf16[2,2,8192]{2,1,0:T(2,128)(2,1)S(1)} collective-permute-done((bf16[2,2,8192]{2,1,0:T(2,128)(2,1)}, bf16[2,2,8192]{2,1,0:T(2,128)(2,1)S(1)}, u32[]{:S(2)}, u32[]{:S(2)}) %collective-permute-start.5) | collective-permute-done | bytes 65568 | tf_op jit(solution)/shard_map/ppermute | solution.py:422
  29.9 0.0 collective-permute-done.4.refs_2_
  29.9 0.8 collective-permute-start.10
  30.7 1.7 %collective-permute-start.12 = (bf16[3584,128]{1,0:T(8,128)(2,1)}, bf16[3584,128]{1,0:T(8,128)(2,1)}, u32[]{:S(2)}, u32[]{:S(2)}) collective-permute-start(bf16[3584,128]{1,0:T(8,128)(2,1)} %get-tuple-element.51), channel_id=1, source_target_pairs={{0,64},{1,65},{2,66},{3,67},{4,68},{5,69},{6,70},{7,71},{8,72},{9,... | collective-permute-start | bytes 2752520 | tf_op jit(solution)/shard_map/ppermute | solution.py:422
  32.4 0.8 copy-done.2
  33.2 0.1 join_column.1
  33.4 0.4 collective-permute-start.6
  33.7 1.1 %collective-permute-done.6.refs_1_ = bf16[8,8192]{1,0:T(8,128)(2,1)S(1)} collective-permute-done((bf16[8,8192]{1,0:T(8,128)(2,1)S(1)}, bf16[8,8192]{1,0:T(8,128)(2,1)S(1)}, u32[]{:S(2)}, u32[]{:S(2)}) %collective-permute-start.6) | collective-permute-done | bytes 131104 | tf_op jit(solution)/shard_map/ppermute | solution.py:422
  34.8 2.8 %collective-permute-start.9 = (bf16[16,8192]{1,0:T(8,128)(2,1)S(1)}, bf16[16,8192]{1,0:T(8,128)(2,1)S(1)}, u32[]{:S(2)}, u32[]{:S(2)}) collective-permute-start(bf16[16,8192]{1,0:T(8,128)(2,1)S(1)} %join_cores.1.pa), channel_id=1, source_target_pairs={{0,3},{1,0},{2,1},{3,2},{4,7},{5,4},{6,5},{7,6},{8,11},{9,8},{10,9... | collective-permute-start | bytes 786440 | tf_op jit(solution)/shard_map/ppermute | solution.py:422
  37.6 0.0 collective-permute-start.8
  37.6 1.6 %collective-permute-start.7 = (bf16[16,8192]{1,0:T(8,128)(2,1)S(1)}, bf16[16,8192]{1,0:T(8,128)(2,1)S(1)}, u32[]{:S(2)}, u32[]{:S(2)}) collective-permute-start(bf16[16,8192]{1,0:T(8,128)(2,1)S(1)} %join_cores.1.pa), channel_id=1, source_target_pairs={{0,2},{1,3},{2,0},{3,1},{4,6},{5,7},{6,4},{7,5},{8,10},{9,11},{10,... | collective-permute-start | bytes 786440 | tf_op jit(solution)/shard_map/ppermute | solution.py:422
  39.3 1.7 %collective-permute-done.9.pd = bf16[16,8192]{1,0:T(8,128)(2,1)S(1)} collective-permute-done((bf16[16,8192]{1,0:T(8,128)(2,1)S(1)}, bf16[16,8192]{1,0:T(8,128)(2,1)S(1)}, u32[]{:S(2)}, u32[]{:S(2)}) %collective-permute-start.9) | collective-permute-done | bytes 262176 | tf_op jit(solution)/shard_map/ppermute | solution.py:422
  40.9 1.6 %collective-permute-start.11 = (bf16[4608,128]{1,0:T(8,128)(2,1)}, bf16[4608,128]{1,0:T(8,128)(2,1)}, u32[]{:S(2)}, u32[]{:S(2)}) collective-permute-start(bf16[4608,128]{1,0:T(8,128)(2,1)} %get-tuple-element.50), channel_id=1, source_target_pairs={{0,64},{1,65},{2,66},{3,67},{4,68},{5,69},{6,70},{7,71},{8,72},{9,... | collective-permute-start | bytes 3538952 | tf_op jit(solution)/shard_map/ppermute | solution.py:422
  42.5 4.8 %collective-permute-done.8.pc = bf16[16,8192]{1,0:T(8,128)(2,1)S(1)} collective-permute-done((bf16[16,8192]{1,0:T(8,128)(2,1)S(1)}, bf16[16,8192]{1,0:T(8,128)(2,1)S(1)}, u32[]{:S(2)}, u32[]{:S(2)}) %collective-permute-start.8) | collective-permute-done | bytes 262176 | tf_op jit(solution)/shard_map/ppermute | solution.py:422
  47.3 0.1 split.1
  47.4 2.5 %collective-permute-start.16 = (bf16[64,3584]{1,0:T(8,128)(2,1)S(1)}, bf16[64,3584]{1,0:T(8,128)(2,1)S(1)}, u32[]{:S(2)}, u32[]{:S(2)}) collective-permute-start(bf16[64,3584]{1,0:T(8,128)(2,1)S(1)} %get-tuple-element.58.refs_5_), channel_id=1, source_target_pairs={{0,24},{1,25},{2,26},{3,27},{4,28},{5,29},{6,30},{7,31},{8,0},{9,1... | collective-permute-start | bytes 1376264 | tf_op jit(solution)/shard_map/ppermute | solution.py:422
  49.9 0.0 collective-permute-start.15
  49.9 1.7 %collective-permute-start.14 = (bf16[64,3584]{1,0:T(8,128)(2,1)S(1)}, bf16[64,3584]{1,0:T(8,128)(2,1)S(1)}, u32[]{:S(2)}, u32[]{:S(2)}) collective-permute-start(bf16[64,3584]{1,0:T(8,128)(2,1)S(1)} %get-tuple-element.58.refs_5_), channel_id=1, source_target_pairs={{0,16},{1,17},{2,18},{3,19},{4,20},{5,21},{6,22},{7,23},{8,24},{9,... | collective-permute-start | bytes 1376264 | tf_op jit(solution)/shard_map/ppermute | solution.py:422
  51.7 2.8 %collective-permute-done.12.refs_3_ = bf16[3584,128]{1,0:T(8,128)(2,1)} collective-permute-done((bf16[3584,128]{1,0:T(8,128)(2,1)}, bf16[3584,128]{1,0:T(8,128)(2,1)}, u32[]{:S(2)}, u32[]{:S(2)}) %collective-permute-start.12) | collective-permute-done | bytes 917536 | tf_op jit(solution)/shard_map/ppermute | solution.py:422
  54.5 1.2 %collective-permute-start.13 = (bf16[3584,128]{1,0:T(8,128)(2,1)}, bf16[3584,128]{1,0:T(8,128)(2,1)}, u32[]{:S(2)}, u32[]{:S(2)}) collective-permute-start(bf16[3584,128]{1,0:T(8,128)(2,1)} %collective-permute-done.12.refs_3_), channel_id=1, source_target_pairs={{0,32},{1,33},{2,34},{3,35},{4,36},{5,37},{6,38},{7,39},{8,40},{9,... | collective-permute-start | bytes 2752520 | tf_op jit(solution)/shard_map/ppermute | solution.py:422
  55.6 4.6 %collective-permute-done.16.refs_8_ = bf16[64,3584]{1,0:T(8,128)(2,1)S(1)} collective-permute-done((bf16[64,3584]{1,0:T(8,128)(2,1)S(1)}, bf16[64,3584]{1,0:T(8,128)(2,1)S(1)}, u32[]{:S(2)}, u32[]{:S(2)}) %collective-permute-start.16) | collective-permute-done | bytes 458784 | tf_op jit(solution)/shard_map/ppermute | solution.py:422
  60.3 3.5 %collective-permute-done.15.refs_7_ = bf16[64,3584]{1,0:T(8,128)(2,1)S(1)} collective-permute-done((bf16[64,3584]{1,0:T(8,128)(2,1)S(1)}, bf16[64,3584]{1,0:T(8,128)(2,1)S(1)}, u32[]{:S(2)}, u32[]{:S(2)}) %collective-permute-start.15) | collective-permute-done | bytes 458784 | tf_op jit(solution)/shard_map/ppermute | solution.py:422
  63.8 0.0 collective-permute-done.14.refs_6_
  63.8 0.1 collective-permute-start.19
  63.9 1.4 %collective-permute-start.18 = (bf16[64,4608]{1,0:T(8,128)(2,1)S(1)}, bf16[64,4608]{1,0:T(8,128)(2,1)}, u32[]{:S(2)}, u32[]{:S(2)}) collective-permute-start(bf16[64,4608]{1,0:T(8,128)(2,1)S(1)} %get-tuple-element.64.refs_5_), channel_id=1, source_target_pairs={{0,8},{1,9},{2,10},{3,11},{4,12},{5,13},{6,14},{7,15},{8,16},{9,17... | collective-permute-start | bytes 1769480 | tf_op jit(solution)/shard_map/ppermute | solution.py:422
  65.3 0.4 collective-permute-start.17
  65.8 0.6 fusion.refs_0_
  66.4 0.0 collective-permute-done.13.refs_4_
  66.4 13.5 %correlate_first.1.refs_11_ = f32[64,208,128]{2,1,0:T(8,128)} custom-call(s32[64]{0:T(128)} %fusion.refs_0_, bf16[8192,128]{1,0:T(8,128)(2,1)} %get-tuple-element.42.refs_1_, bf16[8192,128]{1,0:T(8,128)(2,1)} %copy-done.3, bf16[3584,128]{1,0:T(8,128)(2,1)} %collective-permute-done.12.refs_3_, bf16[3584,128]{1,0:T(8,128)(2,1)} %collective-permute-done.13.refs_4_, ...), custom_call_target="tpu_custom_call" | custom-call | flops 1100000 | bytes 1024 | tf_op jit(solution)/shard_map/correlate_first/pallas_call | solution.py:396
  79.9 0.0 collective-permute-done.11.refs_3_
  80.0 0.7 collective-permute-done.18.refs_7_
  80.6 3.2 %collective-permute-start.20 = (bf16[4608,128]{1,0:T(8,128)(2,1)}, bf16[4608,128]{1,0:T(8,128)(2,1)S(1)}, u32[]{:S(2)}, u32[]{:S(2)}) collective-permute-start(bf16[4608,128]{1,0:T(8,128)(2,1)} %collective-permute-done.11.refs_3_), channel_id=1, source_target_pairs={{0,32},{1,33},{2,34},{3,35},{4,36},{5,37},{6,38},{7,39},{8,40},{9,... | collective-permute-start | bytes 3538952 | tf_op jit(solution)/shard_map/ppermute | solution.py:422
  83.8 2.7 %collective-permute-done.20.refs_4_ = bf16[4608,128]{1,0:T(8,128)(2,1)S(1)} collective-permute-done((bf16[4608,128]{1,0:T(8,128)(2,1)}, bf16[4608,128]{1,0:T(8,128)(2,1)S(1)}, u32[]{:S(2)}, u32[]{:S(2)}) %collective-permute-start.20) | collective-permute-done | bytes 1179680 | tf_op jit(solution)/shard_map/ppermute | solution.py:422
  86.5 1.1 %copy-done.4 = bf16[4608,128]{1,0:T(8,128)(2,1)} copy-done((bf16[4608,128]{1,0:T(8,128)(2,1)}, bf16[4608,128]{1,0:T(8,128)(2,1)S(1)}, u32[]{:S(2)}) %copy-start.4) | copy-done | bytes 1179672
  87.6 17.5 %correlate_last.1 = f32[201,64,128]{2,1,0:T(8,128)} custom-call(s32[64]{0:T(128)} %fusion.refs_0_, bf16[8192,128]{1,0:T(8,128)(2,1)} %get-tuple-element.42.refs_1_, bf16[8192,128]{1,0:T(8,128)(2,1)} %copy-done.3, bf16[4608,128]{1,0:T(8,128)(2,1)} %collective-permute-done.11.refs_3_, bf16[4608,128]{1,0:T(8,128)(2,1)} %copy-done.4, bf16[64,4608]{1,0:T(8,128)(2,1)} %copy-done, ...), custom_call_target="tpu_custom_call" | custom-call | flops 1100000 | bytes 1024 | tf_op jit(solution)/shard_map/correlate_last/pallas_call | solution.py:396
  (24 shorter events, 0.1 us)
Async XLA Ops:
  0.0 6.0 %collective-permute-start.1 = (s32[64]{0:T(128)}, s32[64]{0:T(128)S(1)}, u32[]{:S(2)}, u32[]{:S(2)}) collective-permute-start(s32[64]{0:T(128)} %ia.1), channel_id=1, source_target_pairs={{0,64},{1,65},{2,66},{3,67},{4,68},{5,69},{6,70},{7,71},{8,72},{9,... | collective-permute-start | bytes 776 | tf_op jit(solution)/shard_map/ppermute | solution.py:422
  4.4 1.9 %collective-permute-start = (s32[64]{0:T(128)}, s32[64]{0:T(128)S(1)}, u32[]{:S(2)}, u32[]{:S(2)}) collective-permute-start(s32[64]{0:T(128)} %ia.1), channel_id=1, source_target_pairs={{0,32},{1,33},{2,34},{3,35},{4,36},{5,37},{6,38},{7,39},{8,40},{9,... | collective-permute-start | bytes 776 | tf_op jit(solution)/shard_map/ppermute | solution.py:422
  5.4 4.6 %collective-permute-start.2 = (s32[64]{0:T(128)}, s32[64]{0:T(128)S(1)}, u32[]{:S(2)}, u32[]{:S(2)}) collective-permute-start(s32[64]{0:T(128)} %ia.1), channel_id=1, source_target_pairs={{0,96},{1,97},{2,98},{3,99},{4,100},{5,101},{6,102},{7,103},{8,104... | collective-permute-start | bytes 776 | tf_op jit(solution)/shard_map/ppermute | solution.py:422
  6.0 4.0 %copy-start.8 = (s32[64]{0:T(128)}, s32[64]{0:T(128)S(1)}, u32[]{:S(2)}) copy-start(s32[64]{0:T(128)S(1)} %collective-permute-done.1.ic) | copy-start | bytes 772
  6.3 3.7 %copy-start.9 = (s32[64]{0:T(128)}, s32[64]{0:T(128)S(1)}, u32[]{:S(2)}) copy-start(s32[64]{0:T(128)S(1)} %collective-permute-done.ib) | copy-start | bytes 772
  10.0 0.5 copy-start.10
  22.5 4.0 %collective-permute-start.3 = (bf16[2,2,8192]{2,1,0:T(2,128)(2,1)}, bf16[2,2,8192]{2,1,0:T(2,128)(2,1)S(1)}, u32[]{:S(2)}, u32[]{:S(2)}) collective-permute-start(bf16[2,2,8192]{2,1,0:T(2,128)(2,1)} %get-tuple-element.43.refs_0_), channel_id=1, source_target_pairs={{0,4},{1,5},{2,6},{3,7},{4,0},{5,1},{6,2},{7,3},{8,12},{9,13},{10,... | collective-permute-start | bytes 196616 | tf_op jit(solution)/shard_map/ppermute | solution.py:422
  23.3 6.6 %collective-permute-start.5 = (bf16[2,2,8192]{2,1,0:T(2,128)(2,1)}, bf16[2,2,8192]{2,1,0:T(2,128)(2,1)S(1)}, u32[]{:S(2)}, u32[]{:S(2)}) collective-permute-start(bf16[2,2,8192]{2,1,0:T(2,128)(2,1)} %get-tuple-element.41), channel_id=1, source_target_pairs={{0,68},{1,69},{2,70},{3,71},{4,64},{5,65},{6,66},{7,67},{8,76},{9,... | collective-permute-start | bytes 196616 | tf_op jit(solution)/shard_map/ppermute | solution.py:422
  23.3 6.6 %collective-permute-start.4 = (bf16[2,2,8192]{2,1,0:T(2,128)(2,1)}, bf16[2,2,8192]{2,1,0:T(2,128)(2,1)S(1)}, u32[]{:S(2)}, u32[]{:S(2)}) collective-permute-start(bf16[2,2,8192]{2,1,0:T(2,128)(2,1)} %get-tuple-element.41), channel_id=1, source_target_pairs={{0,64},{1,65},{2,66},{3,67},{4,68},{5,69},{6,70},{7,71},{8,72},{9,... | collective-permute-start | bytes 196616 | tf_op jit(solution)/shard_map/ppermute | solution.py:422
  29.9 17.4 %collective-permute-start.10 = (bf16[8192,128]{1,0:T(8,128)(2,1)}, bf16[8192,128]{1,0:T(8,128)(2,1)S(1)}, u32[]{:S(2)}, u32[]{:S(2)}) collective-permute-start(bf16[8192,128]{1,0:T(8,128)(2,1)} %get-tuple-element.42.refs_1_), channel_id=1, source_target_pairs={{0,32},{1,33},{2,34},{3,35},{4,36},{5,37},{6,38},{7,39},{8,40},{9,... | collective-permute-start | bytes 6291464 | tf_op jit(solution)/shard_map/ppermute | solution.py:422
  30.7 23.8 %collective-permute-start.12 = (bf16[3584,128]{1,0:T(8,128)(2,1)}, bf16[3584,128]{1,0:T(8,128)(2,1)}, u32[]{:S(2)}, u32[]{:S(2)}) collective-permute-start(bf16[3584,128]{1,0:T(8,128)(2,1)} %get-tuple-element.51), channel_id=1, source_target_pairs={{0,64},{1,65},{2,66},{3,67},{4,68},{5,69},{6,70},{7,71},{8,72},{9,... | collective-permute-start | bytes 2752520 | tf_op jit(solution)/shard_map/ppermute | solution.py:422
  32.4 0.8 copy-start.2
  33.4 1.4 %collective-permute-start.6 = (bf16[8,8192]{1,0:T(8,128)(2,1)S(1)}, bf16[8,8192]{1,0:T(8,128)(2,1)S(1)}, u32[]{:S(2)}, u32[]{:S(2)}) collective-permute-start(bf16[8,8192]{1,0:T(8,128)(2,1)S(1)} %get-tuple-element.48), channel_id=1, source_target_pairs={{0,32},{1,33},{2,34},{3,35},{4,36},{5,37},{6,38},{7,39},{8,40},{9,... | collective-permute-start | bytes 393224 | tf_op jit(solution)/shard_map/ppermute | solution.py:422
  34.8 6.1 %collective-permute-start.9 = (bf16[16,8192]{1,0:T(8,128)(2,1)S(1)}, bf16[16,8192]{1,0:T(8,128)(2,1)S(1)}, u32[]{:S(2)}, u32[]{:S(2)}) collective-permute-start(bf16[16,8192]{1,0:T(8,128)(2,1)S(1)} %join_cores.1.pa), channel_id=1, source_target_pairs={{0,3},{1,0},{2,1},{3,2},{4,7},{5,4},{6,5},{7,6},{8,11},{9,8},{10,9... | collective-permute-start | bytes 786440 | tf_op jit(solution)/shard_map/ppermute | solution.py:422
  37.6 9.6 %collective-permute-start.8 = (bf16[16,8192]{1,0:T(8,128)(2,1)S(1)}, bf16[16,8192]{1,0:T(8,128)(2,1)S(1)}, u32[]{:S(2)}, u32[]{:S(2)}) collective-permute-start(bf16[16,8192]{1,0:T(8,128)(2,1)S(1)} %join_cores.1.pa), channel_id=1, source_target_pairs={{0,1},{1,2},{2,3},{3,0},{4,5},{5,6},{6,7},{7,4},{8,9},{9,10},{10,1... | collective-permute-start | bytes 786440 | tf_op jit(solution)/shard_map/ppermute | solution.py:422
  37.6 9.6 %collective-permute-start.7 = (bf16[16,8192]{1,0:T(8,128)(2,1)S(1)}, bf16[16,8192]{1,0:T(8,128)(2,1)S(1)}, u32[]{:S(2)}, u32[]{:S(2)}) collective-permute-start(bf16[16,8192]{1,0:T(8,128)(2,1)S(1)} %join_cores.1.pa), channel_id=1, source_target_pairs={{0,2},{1,3},{2,0},{3,1},{4,6},{5,7},{6,4},{7,5},{8,10},{9,11},{10,... | collective-permute-start | bytes 786440 | tf_op jit(solution)/shard_map/ppermute | solution.py:422
  40.9 39.0 %collective-permute-start.11 = (bf16[4608,128]{1,0:T(8,128)(2,1)}, bf16[4608,128]{1,0:T(8,128)(2,1)}, u32[]{:S(2)}, u32[]{:S(2)}) collective-permute-start(bf16[4608,128]{1,0:T(8,128)(2,1)} %get-tuple-element.50), channel_id=1, source_target_pairs={{0,64},{1,65},{2,66},{3,67},{4,68},{5,69},{6,70},{7,71},{8,72},{9,... | collective-permute-start | bytes 3538952 | tf_op jit(solution)/shard_map/ppermute | solution.py:422
  47.3 19.1 %copy-start.3 = (bf16[8192,128]{1,0:T(8,128)(2,1)}, bf16[8192,128]{1,0:T(8,128)(2,1)S(1)}, u32[]{:S(2)}) copy-start(bf16[8192,128]{1,0:T(8,128)(2,1)S(1)} %collective-permute-done.10.refs_2_) | copy-start | bytes 6291460
  47.4 19.0 %copy-start.1 = (bf16[64,3584]{1,0:T(8,128)(2,1)}, bf16[64,3584]{1,0:T(8,128)(2,1)S(1)}, u32[]{:S(2)}) copy-start(bf16[64,3584]{1,0:T(8,128)(2,1)S(1)} %get-tuple-element.58.refs_5_) | copy-start | bytes 1376260
  47.4 32.6 %copy-start = (bf16[64,4608]{1,0:T(8,128)(2,1)}, bf16[64,4608]{1,0:T(8,128)(2,1)S(1)}, u32[]{:S(2)}) copy-start(bf16[64,4608]{1,0:T(8,128)(2,1)S(1)} %get-tuple-element.64.refs_5_) | copy-start | bytes 1769476
  47.4 12.9 %collective-permute-start.16 = (bf16[64,3584]{1,0:T(8,128)(2,1)S(1)}, bf16[64,3584]{1,0:T(8,128)(2,1)S(1)}, u32[]{:S(2)}, u32[]{:S(2)}) collective-permute-start(bf16[64,3584]{1,0:T(8,128)(2,1)S(1)} %get-tuple-element.58.refs_5_), channel_id=1, source_target_pairs={{0,24},{1,25},{2,26},{3,27},{4,28},{5,29},{6,30},{7,31},{8,0},{9,1... | collective-permute-start | bytes 1376264 | tf_op jit(solution)/shard_map/ppermute | solution.py:422
  49.9 13.9 %collective-permute-start.15 = (bf16[64,3584]{1,0:T(8,128)(2,1)S(1)}, bf16[64,3584]{1,0:T(8,128)(2,1)S(1)}, u32[]{:S(2)}, u32[]{:S(2)}) collective-permute-start(bf16[64,3584]{1,0:T(8,128)(2,1)S(1)} %get-tuple-element.58.refs_5_), channel_id=1, source_target_pairs={{0,8},{1,9},{2,10},{3,11},{4,12},{5,13},{6,14},{7,15},{8,16},{9,17... | collective-permute-start | bytes 1376264 | tf_op jit(solution)/shard_map/ppermute | solution.py:422
  49.9 13.9 %collective-permute-start.14 = (bf16[64,3584]{1,0:T(8,128)(2,1)S(1)}, bf16[64,3584]{1,0:T(8,128)(2,1)S(1)}, u32[]{:S(2)}, u32[]{:S(2)}) collective-permute-start(bf16[64,3584]{1,0:T(8,128)(2,1)S(1)} %get-tuple-element.58.refs_5_), channel_id=1, source_target_pairs={{0,16},{1,17},{2,18},{3,19},{4,20},{5,21},{6,22},{7,23},{8,24},{9,... | collective-permute-start | bytes 1376264 | tf_op jit(solution)/shard_map/ppermute | solution.py:422
  54.5 11.9 %collective-permute-start.13 = (bf16[3584,128]{1,0:T(8,128)(2,1)}, bf16[3584,128]{1,0:T(8,128)(2,1)}, u32[]{:S(2)}, u32[]{:S(2)}) collective-permute-start(bf16[3584,128]{1,0:T(8,128)(2,1)} %collective-permute-done.12.refs_3_), channel_id=1, source_target_pairs={{0,32},{1,33},{2,34},{3,35},{4,36},{5,37},{6,38},{7,39},{8,40},{9,... | collective-permute-start | bytes 2752520 | tf_op jit(solution)/shard_map/ppermute | solution.py:422
  60.3 3.6 %copy-start.5 = (bf16[64,3584]{1,0:T(8,128)(2,1)}, bf16[64,3584]{1,0:T(8,128)(2,1)S(1)}, u32[]{:S(2)}) copy-start(bf16[64,3584]{1,0:T(8,128)(2,1)S(1)} %collective-permute-done.16.refs_8_) | copy-start | bytes 1376260
  63.8 1.5 %copy-start.6 = (bf16[64,3584]{1,0:T(8,128)(2,1)}, bf16[64,3584]{1,0:T(8,128)(2,1)S(1)}, u32[]{:S(2)}) copy-start(bf16[64,3584]{1,0:T(8,128)(2,1)S(1)} %collective-permute-done.15.refs_7_) | copy-start | bytes 1376260
  63.8 1.5 %copy-start.7 = (bf16[64,3584]{1,0:T(8,128)(2,1)}, bf16[64,3584]{1,0:T(8,128)(2,1)S(1)}, u32[]{:S(2)}) copy-start(bf16[64,3584]{1,0:T(8,128)(2,1)S(1)} %collective-permute-done.14.refs_6_) | copy-start | bytes 1376260
  63.8 16.2 %collective-permute-start.19 = (bf16[64,4608]{1,0:T(8,128)(2,1)S(1)}, bf16[64,4608]{1,0:T(8,128)(2,1)}, u32[]{:S(2)}, u32[]{:S(2)}) collective-permute-start(bf16[64,4608]{1,0:T(8,128)(2,1)S(1)} %get-tuple-element.64.refs_5_), channel_id=1, source_target_pairs={{0,24},{1,25},{2,26},{3,27},{4,28},{5,29},{6,30},{7,31},{8,0},{9,1... | collective-permute-start | bytes 1769480 | tf_op jit(solution)/shard_map/ppermute | solution.py:422
  63.9 16.7 %collective-permute-start.18 = (bf16[64,4608]{1,0:T(8,128)(2,1)S(1)}, bf16[64,4608]{1,0:T(8,128)(2,1)}, u32[]{:S(2)}, u32[]{:S(2)}) collective-permute-start(bf16[64,4608]{1,0:T(8,128)(2,1)S(1)} %get-tuple-element.64.refs_5_), channel_id=1, source_target_pairs={{0,8},{1,9},{2,10},{3,11},{4,12},{5,13},{6,14},{7,15},{8,16},{9,17... | collective-permute-start | bytes 1769480 | tf_op jit(solution)/shard_map/ppermute | solution.py:422
  65.3 15.3 %collective-permute-start.17 = (bf16[64,4608]{1,0:T(8,128)(2,1)S(1)}, bf16[64,4608]{1,0:T(8,128)(2,1)}, u32[]{:S(2)}, u32[]{:S(2)}) collective-permute-start(bf16[64,4608]{1,0:T(8,128)(2,1)S(1)} %get-tuple-element.64.refs_5_), channel_id=1, source_target_pairs={{0,16},{1,17},{2,18},{3,19},{4,20},{5,21},{6,22},{7,23},{8,24},{9,... | collective-permute-start | bytes 1769480 | tf_op jit(solution)/shard_map/ppermute | solution.py:422
  80.6 5.9 %collective-permute-start.20 = (bf16[4608,128]{1,0:T(8,128)(2,1)}, bf16[4608,128]{1,0:T(8,128)(2,1)S(1)}, u32[]{:S(2)}, u32[]{:S(2)}) collective-permute-start(bf16[4608,128]{1,0:T(8,128)(2,1)} %collective-permute-done.11.refs_3_), channel_id=1, source_target_pairs={{0,32},{1,33},{2,34},{3,35},{4,36},{5,37},{6,38},{7,39},{8,40},{9,... | collective-permute-start | bytes 3538952 | tf_op jit(solution)/shard_map/ppermute | solution.py:422
  86.5 1.1 %copy-start.4 = (bf16[4608,128]{1,0:T(8,128)(2,1)}, bf16[4608,128]{1,0:T(8,128)(2,1)S(1)}, u32[]{:S(2)}) copy-start(bf16[4608,128]{1,0:T(8,128)(2,1)S(1)} %collective-permute-done.20.refs_4_) | copy-start | bytes 3538948

commit v8 on v7

--- a/solution.py
+++ b/solution.py
@@ -240,7 +240,7 @@
         out_ref, ybuf, xbuf, xrow, cross, sems, table_ref, acc_ref, osem = refs[11:]
     else:
         acc_hbm, out_ref, ybuf, xbuf, xrow, cross, sems, table_ref, acc_ref, scale, stage, osem = refs[11:]
-    parts = ((0, HEAD), (HEAD, kc - HEAD))
+    parts = ((0, HEAD), (HEAD, 128), (HEAD + 128, kc - HEAD - 128))
     copies = []
     for k, (lo, size) in enumerate(parts):
         span = pl.ds(lo * 8, size * 8)
@@ -253,9 +253,9 @@
         copies.append(some)
         for copy in some:
             copy.start()
-    later = [pltpu.make_async_copy(lag_ref, table_ref, sems.at[16])]
+    later = [pltpu.make_async_copy(lag_ref, table_ref, sems.at[24])]
     if not first:
-        later.append(pltpu.make_async_copy(acc_hbm, acc_ref, sems.at[17]))
+        later.append(pltpu.make_async_copy(acc_hbm, acc_ref, sems.at[25]))
 
     rowid = lax.broadcasted_iota(jnp.int32, (16, 256), 0) % GRP
     lane = lax.broadcasted_iota(jnp.int32, (16, 256), 1) % GRP
@@ -306,11 +306,11 @@
     for k, ((lo, size), some) in enumerate(zip(parts, copies)):
         for copy in some:
             copy.wait()
-        if k:
+        if k == 2:
             for copy in later:
                 copy.start()
         if k:
-            lax.fori_loop(0, size // 16 // UNROLL, pairs, 0)
+            lax.fori_loop((lo - HEAD) // 16 // UNROLL, (lo + size - HEAD) // 16 // UNROLL, pairs, 0)
         else:
             for v in range(HEAD // 16):
                 pair(v, v)
@@ -377,7 +377,7 @@
         pltpu.VMEM((4, 64, kc * 8), jnp.bfloat16),
         pltpu.VMEM((UNROLL, 128, 256), jnp.float32),
         pltpu.VMEM((64, 2 * kc, 128), jnp.bfloat16),
-        pltpu.SemaphoreType.DMA((18,)),
+        pltpu.SemaphoreType.DMA((26,)),
         pltpu.VMEM((TAU, 2 * kc), jnp.bfloat16),
         pltpu.VMEM((64, TAU, 128), jnp.float32),
     ]

time: 106 us -> 105 us (level)
  Pallas kernels: 43.3 us -> 41.6 us
    pallas_call x2, Pallas kernels: 31.1 us -> 29.4 us  [correlate(): pl.pallas_call(functools.partial(correlate_kernel, first, last, kc, offse...]
  transfers between devices with their start and end apart: 21 -> 21, of which waited for: 12 -> 13; matrix products, arithmetic and copies ran while one was open for 1% -> 1% of each run, Pallas kernels for 13% -> 13%
where the time goes in v8:
time: 105 us; the launch traced here: 104 us
  Pallas kernels  41.6 us (40%)
  waiting for transfers between devices  30.5 us (29%)
  starting transfers between devices  28.2 us (27%)
  local copies, waits for them, and re-layouts  2.47 us (2%)
  other arithmetic  1.19 us (1%)
    ppermute x21, waiting for transfers between devices, send(): return lax.ppermute(value, AXES, permutation(move))  30.5 us
    pallas_call x2, Pallas kernels, correlate(): pl.pallas_call(functools.partial(correlate_kernel, first, last, kc, offse...  29.4 us
    ppermute x21, starting transfers between devices, send(): return lax.ppermute(value, AXES, permutation(move))  28.2 us
    pallas_call x1, Pallas kernels, spectra(): pl.pallas_call(functools.partial(spectra_kernel, half), out_shape=[jax.Sh...  12 us
    unnamed x22, local copies, waits for them, and re-layouts  2.47 us
  transfers between devices with their start and end apart: 21, of which 13 were waited for; matrix products, arithmetic and copies ran while one was open for 1% of the time, Pallas kernels for 13%

profile of v8, /device:TPU:1, one launch (start us, length us, event | category | flops | bytes accessed | tf_op | source)
XLA Modules:
  0.0 104.2 jit_solution(1265271342041238406)
XLA Ops:
  0.0 4.4 %collective-permute-start.1 = (s32[64]{0:T(128)}, s32[64]{0:T(128)S(1)}, u32[]{:S(2)}, u32[]{:S(2)}) collective-permute-start(s32[64]{0:T(128)} %ia.1), channel_id=1, source_target_pairs={{0,64},{1,65},{2,66},{3,67},{4,68},{5,69},{6,70},{7,71},{8,72},{9,... | collective-permute-start | bytes 776 | tf_op jit(solution)/shard_map/ppermute | solution.py:422
  4.4 1.0 collective-permute-start
  5.4 0.0 collective-permute-start.2
  5.4 0.6 pad_add_fusion.me_ref
  6.0 0.4 collective-permute-done.ib
  6.3 3.6 %collective-permute-done.2.id_ = s32[64]{0:T(128)S(1)} collective-permute-done((s32[64]{0:T(128)}, s32[64]{0:T(128)S(1)}, u32[]{:S(2)}, u32[]{:S(2)}) %collective-permute-start.2) | collective-permute-done | bytes 288 | tf_op jit(solution)/shard_map/ppermute | solution.py:422
  10.0 0.5 copy-done.10
  10.5 12.0 %spectra.1 = (bf16[3584,128]{1,0:T(8,128)(2,1)}, bf16[4608,128]{1,0:T(8,128)(2,1)}, bf16[8192,128]{1,0:T(8,128)(2,1)}, bf16[2,2,8192]{2,1,0:T(2,128)(2,1)}, bf16[2,2,8192]{2,1,0:T(2,128)(2,1)}) custom-call(s32[2]{0:T(128)} %pad_add_fusion.me_ref, s32[64]{0:T(128)} %ia.1, s32[64]{0:T(128)} %copy-done.9, s32[64]{0:T(128)} %copy-done.8, s32[64]{0:T(128)} %copy-done.10, ...), custom_call_target="tpu_custom_call" | custom-call | flops 1100000 | bytes 1024 | tf_op jit(solution)/shard_map/spectra/pallas_call | solution.py:166
  22.5 0.8 collective-permute-start.3
  23.3 0.0 collective-permute-start.5
  23.3 2.5 %collective-permute-start.4 = (bf16[2,2,8192]{2,1,0:T(2,128)(2,1)}, bf16[2,2,8192]{2,1,0:T(2,128)(2,1)S(1)}, u32[]{:S(2)}, u32[]{:S(2)}) collective-permute-start(bf16[2,2,8192]{2,1,0:T(2,128)(2,1)} %get-tuple-element.41), channel_id=1, source_target_pairs={{0,64},{1,65},{2,66},{3,67},{4,68},{5,69},{6,70},{7,71},{8,72},{9,... | collective-permute-start | bytes 196616 | tf_op jit(solution)/shard_map/ppermute | solution.py:422
  25.8 0.7 collective-permute-done.3.refs_1_
  26.5 3.4 %collective-permute-done.5.refs_3_ = bf16[2,2,8192]{2,1,0:T(2,128)(2,1)S(1)} collective-permute-done((bf16[2,2,8192]{2,1,0:T(2,128)(2,1)}, bf16[2,2,8192]{2,1,0:T(2,128)(2,1)S(1)}, u32[]{:S(2)}, u32[]{:S(2)}) %collective-permute-start.5) | collective-permute-done | bytes 65568 | tf_op jit(solution)/shard_map/ppermute | solution.py:422
  29.9 0.0 collective-permute-done.4.refs_2_
  29.9 0.8 collective-permute-start.10
  30.7 1.7 %collective-permute-start.12 = (bf16[3584,128]{1,0:T(8,128)(2,1)}, bf16[3584,128]{1,0:T(8,128)(2,1)}, u32[]{:S(2)}, u32[]{:S(2)}) collective-permute-start(bf16[3584,128]{1,0:T(8,128)(2,1)} %get-tuple-element.51), channel_id=1, source_target_pairs={{0,64},{1,65},{2,66},{3,67},{4,68},{5,69},{6,70},{7,71},{8,72},{9,... | collective-permute-start | bytes 2752520 | tf_op jit(solution)/shard_map/ppermute | solution.py:422
  32.4 0.8 copy-done.2
  33.2 0.1 join_column.1
  33.4 0.4 collective-permute-start.6
  33.7 1.1 %collective-permute-done.6.refs_1_ = bf16[8,8192]{1,0:T(8,128)(2,1)S(1)} collective-permute-done((bf16[8,8192]{1,0:T(8,128)(2,1)S(1)}, bf16[8,8192]{1,0:T(8,128)(2,1)S(1)}, u32[]{:S(2)}, u32[]{:S(2)}) %collective-permute-start.6) | collective-permute-done | bytes 131104 | tf_op jit(solution)/shard_map/ppermute | solution.py:422
  34.8 2.8 %collective-permute-start.9 = (bf16[16,8192]{1,0:T(8,128)(2,1)S(1)}, bf16[16,8192]{1,0:T(8,128)(2,1)S(1)}, u32[]{:S(2)}, u32[]{:S(2)}) collective-permute-start(bf16[16,8192]{1,0:T(8,128)(2,1)S(1)} %join_cores.1.pa), channel_id=1, source_target_pairs={{0,3},{1,0},{2,1},{3,2},{4,7},{5,4},{6,5},{7,6},{8,11},{9,8},{10,9... | collective-permute-start | bytes 786440 | tf_op jit(solution)/shard_map/ppermute | solution.py:422
  37.6 1.6 %collective-permute-start.7 = (bf16[16,8192]{1,0:T(8,128)(2,1)S(1)}, bf16[16,8192]{1,0:T(8,128)(2,1)S(1)}, u32[]{:S(2)}, u32[]{:S(2)}) collective-permute-start(bf16[16,8192]{1,0:T(8,128)(2,1)S(1)} %join_cores.1.pa), channel_id=1, source_target_pairs={{0,2},{1,3},{2,0},{3,1},{4,6},{5,7},{6,4},{7,5},{8,10},{9,11},{10,... | collective-permute-start | bytes 786440 | tf_op jit(solution)/shard_map/ppermute | solution.py:422
  39.3 1.7 %collective-permute-done.9.pd = bf16[16,8192]{1,0:T(8,128)(2,1)S(1)} collective-permute-done((bf16[16,8192]{1,0:T(8,128)(2,1)S(1)}, bf16[16,8192]{1,0:T(8,128)(2,1)S(1)}, u32[]{:S(2)}, u32[]{:S(2)}) %collective-permute-start.9) | collective-permute-done | bytes 262176 | tf_op jit(solution)/shard_map/ppermute | solution.py:422
  40.9 1.6 %collective-permute-start.11 = (bf16[4608,128]{1,0:T(8,128)(2,1)}, bf16[4608,128]{1,0:T(8,128)(2,1)}, u32[]{:S(2)}, u32[]{:S(2)}) collective-permute-start(bf16[4608,128]{1,0:T(8,128)(2,1)} %get-tuple-element.50), channel_id=1, source_target_pairs={{0,64},{1,65},{2,66},{3,67},{4,68},{5,69},{6,70},{7,71},{8,72},{9,... | collective-permute-start | bytes 3538952 | tf_op jit(solution)/shard_map/ppermute | solution.py:422
  42.5 4.8 %collective-permute-done.8.pc = bf16[16,8192]{1,0:T(8,128)(2,1)S(1)} collective-permute-done((bf16[16,8192]{1,0:T(8,128)(2,1)S(1)}, bf16[16,8192]{1,0:T(8,128)(2,1)S(1)}, u32[]{:S(2)}, u32[]{:S(2)}) %collective-permute-start.8) | collective-permute-done | bytes 262176 | tf_op jit(solution)/shard_map/ppermute | solution.py:422
  47.3 0.0 collective-permute-done.7.pb
  47.3 0.0 collective-permute-done.10.refs_2_
  47.3 0.1 split.1
  47.4 2.5 %collective-permute-start.16 = (bf16[64,3584]{1,0:T(8,128)(2,1)S(1)}, bf16[64,3584]{1,0:T(8,128)(2,1)S(1)}, u32[]{:S(2)}, u32[]{:S(2)}) collective-permute-start(bf16[64,3584]{1,0:T(8,128)(2,1)S(1)} %get-tuple-element.58.refs_5_), channel_id=1, source_target_pairs={{0,24},{1,25},{2,26},{3,27},{4,28},{5,29},{6,30},{7,31},{8,0},{9,1... | collective-permute-start | bytes 1376264 | tf_op jit(solution)/shard_map/ppermute | solution.py:422
  49.9 0.0 collective-permute-start.15
  49.9 1.7 %collective-permute-start.14 = (bf16[64,3584]{1,0:T(8,128)(2,1)S(1)}, bf16[64,3584]{1,0:T(8,128)(2,1)S(1)}, u32[]{:S(2)}, u32[]{:S(2)}) collective-permute-start(bf16[64,3584]{1,0:T(8,128)(2,1)S(1)} %get-tuple-element.58.refs_5_), channel_id=1, source_target_pairs={{0,16},{1,17},{2,18},{3,19},{4,20},{5,21},{6,22},{7,23},{8,24},{9,... | collective-permute-start | bytes 1376264 | tf_op jit(solution)/shard_map/ppermute | solution.py:422
  51.7 2.8 %collective-permute-done.12.refs_3_ = bf16[3584,128]{1,0:T(8,128)(2,1)} collective-permute-done((bf16[3584,128]{1,0:T(8,128)(2,1)}, bf16[3584,128]{1,0:T(8,128)(2,1)}, u32[]{:S(2)}, u32[]{:S(2)}) %collective-permute-start.12) | collective-permute-done | bytes 917536 | tf_op jit(solution)/shard_map/ppermute | solution.py:422
  54.5 1.2 %collective-permute-start.13 = (bf16[3584,128]{1,0:T(8,128)(2,1)}, bf16[3584,128]{1,0:T(8,128)(2,1)}, u32[]{:S(2)}, u32[]{:S(2)}) collective-permute-start(bf16[3584,128]{1,0:T(8,128)(2,1)} %collective-permute-done.12.refs_3_), channel_id=1, source_target_pairs={{0,32},{1,33},{2,34},{3,35},{4,36},{5,37},{6,38},{7,39},{8,40},{9,... | collective-permute-start | bytes 2752520 | tf_op jit(solution)/shard_map/ppermute | solution.py:422
  55.6 4.6 %collective-permute-done.16.refs_8_ = bf16[64,3584]{1,0:T(8,128)(2,1)S(1)} collective-permute-done((bf16[64,3584]{1,0:T(8,128)(2,1)S(1)}, bf16[64,3584]{1,0:T(8,128)(2,1)S(1)}, u32[]{:S(2)}, u32[]{:S(2)}) %collective-permute-start.16) | collective-permute-done | bytes 458784 | tf_op jit(solution)/shard_map/ppermute | solution.py:422
  60.3 3.5 %collective-permute-done.15.refs_7_ = bf16[64,3584]{1,0:T(8,128)(2,1)S(1)} collective-permute-done((bf16[64,3584]{1,0:T(8,128)(2,1)S(1)}, bf16[64,3584]{1,0:T(8,128)(2,1)S(1)}, u32[]{:S(2)}, u32[]{:S(2)}) %collective-permute-start.15) | collective-permute-done | bytes 458784 | tf_op jit(solution)/shard_map/ppermute | solution.py:422
  63.8 0.1 collective-permute-start.19
  63.9 1.4 %collective-permute-start.18 = (bf16[64,4608]{1,0:T(8,128)(2,1)S(1)}, bf16[64,4608]{1,0:T(8,128)(2,1)}, u32[]{:S(2)}, u32[]{:S(2)}) collective-permute-start(bf16[64,4608]{1,0:T(8,128)(2,1)S(1)} %get-tuple-element.64.refs_5_), channel_id=1, source_target_pairs={{0,8},{1,9},{2,10},{3,11},{4,12},{5,13},{6,14},{7,15},{8,16},{9,17... | collective-permute-start | bytes 1769480 | tf_op jit(solution)/shard_map/ppermute | solution.py:422
  65.3 0.4 collective-permute-start.17
  65.8 0.6 fusion.refs_0_
  66.4 0.0 collective-permute-done.13.refs_4_
  66.4 12.9 %correlate_first.1.refs_11_ = f32[64,208,128]{2,1,0:T(8,128)} custom-call(s32[64]{0:T(128)} %fusion.refs_0_, bf16[8192,128]{1,0:T(8,128)(2,1)} %get-tuple-element.42.refs_1_, bf16[8192,128]{1,0:T(8,128)(2,1)} %copy-done.3, bf16[3584,128]{1,0:T(8,128)(2,1)} %collective-permute-done.12.refs_3_, bf16[3584,128]{1,0:T(8,128)(2,1)} %collective-permute-done.13.refs_4_, ...), custom_call_target="tpu_custom_call" | custom-call | flops 1100000 | bytes 1024 | tf_op jit(solution)/shard_map/correlate_first/pallas_call | solution.py:396
  79.3 0.4 collective-permute-done.11.refs_3_
  79.7 0.0 collective-permute-done.19.refs_8_
  79.8 0.9 collective-permute-done.18.refs_7_
  80.6 3.2 %collective-permute-start.20 = (bf16[4608,128]{1,0:T(8,128)(2,1)}, bf16[4608,128]{1,0:T(8,128)(2,1)S(1)}, u32[]{:S(2)}, u32[]{:S(2)}) collective-permute-start(bf16[4608,128]{1,0:T(8,128)(2,1)} %collective-permute-done.11.refs_3_), channel_id=1, source_target_pairs={{0,32},{1,33},{2,34},{3,35},{4,36},{5,37},{6,38},{7,39},{8,40},{9,... | collective-permute-start | bytes 3538952 | tf_op jit(solution)/shard_map/ppermute | solution.py:422
  83.8 2.7 %collective-permute-done.20.refs_4_ = bf16[4608,128]{1,0:T(8,128)(2,1)S(1)} collective-permute-done((bf16[4608,128]{1,0:T(8,128)(2,1)}, bf16[4608,128]{1,0:T(8,128)(2,1)S(1)}, u32[]{:S(2)}, u32[]{:S(2)}) %collective-permute-start.20) | collective-permute-done | bytes 1179680 | tf_op jit(solution)/shard_map/ppermute | solution.py:422
  86.5 1.1 %copy-done.4 = bf16[4608,128]{1,0:T(8,128)(2,1)} copy-done((bf16[4608,128]{1,0:T(8,128)(2,1)}, bf16[4608,128]{1,0:T(8,128)(2,1)S(1)}, u32[]{:S(2)}) %copy-start.4) | copy-done | bytes 1179672
  87.6 16.5 %correlate_last.1 = f32[201,64,128]{2,1,0:T(8,128)} custom-call(s32[64]{0:T(128)} %fusion.refs_0_, bf16[8192,128]{1,0:T(8,128)(2,1)} %get-tuple-element.42.refs_1_, bf16[8192,128]{1,0:T(8,128)(2,1)} %copy-done.3, bf16[4608,128]{1,0:T(8,128)(2,1)} %collective-permute-done.11.refs_3_, bf16[4608,128]{1,0:T(8,128)(2,1)} %copy-done.4, bf16[64,4608]{1,0:T(8,128)(2,1)} %copy-done, ...), custom_call_target="tpu_custom_call" | custom-call | flops 1100000 | bytes 1024 | tf_op jit(solution)/shard_map/correlate_last/pallas_call | solution.py:396
  (24 shorter events, 0.1 us)
Async XLA Ops:
  0.0 6.0 %collective-permute-start.1 = (s32[64]{0:T(128)}, s32[64]{0:T(128)S(1)}, u32[]{:S(2)}, u32[]{:S(2)}) collective-permute-start(s32[64]{0:T(128)} %ia.1), channel_id=1, source_target_pairs={{0,64},{1,65},{2,66},{3,67},{4,68},{5,69},{6,70},{7,71},{8,72},{9,... | collective-permute-start | bytes 776 | tf_op jit(solution)/shard_map/ppermute | solution.py:422
  4.4 1.9 %collective-permute-start = (s32[64]{0:T(128)}, s32[64]{0:T(128)S(1)}, u32[]{:S(2)}, u32[]{:S(2)}) collective-permute-start(s32[64]{0:T(128)} %ia.1), channel_id=1, source_target_pairs={{0,32},{1,33},{2,34},{3,35},{4,36},{5,37},{6,38},{7,39},{8,40},{9,... | collective-permute-start | bytes 776 | tf_op jit(solution)/shard_map/ppermute | solution.py:422
  5.4 4.6 %collective-permute-start.2 = (s32[64]{0:T(128)}, s32[64]{0:T(128)S(1)}, u32[]{:S(2)}, u32[]{:S(2)}) collective-permute-start(s32[64]{0:T(128)} %ia.1), channel_id=1, source_target_pairs={{0,96},{1,97},{2,98},{3,99},{4,100},{5,101},{6,102},{7,103},{8,104... | collective-permute-start | bytes 776 | tf_op jit(solution)/shard_map/ppermute | solution.py:422
  6.0 4.0 %copy-start.8 = (s32[64]{0:T(128)}, s32[64]{0:T(128)S(1)}, u32[]{:S(2)}) copy-start(s32[64]{0:T(128)S(1)} %collective-permute-done.1.ic) | copy-start | bytes 772
  6.3 3.7 %copy-start.9 = (s32[64]{0:T(128)}, s32[64]{0:T(128)S(1)}, u32[]{:S(2)}) copy-start(s32[64]{0:T(128)S(1)} %collective-permute-done.ib) | copy-start | bytes 772
  10.0 0.5 copy-start.10
  22.5 4.0 %collective-permute-start.3 = (bf16[2,2,8192]{2,1,0:T(2,128)(2,1)}, bf16[2,2,8192]{2,1,0:T(2,128)(2,1)S(1)}, u32[]{:S(2)}, u32[]{:S(2)}) collective-permute-start(bf16[2,2,8192]{2,1,0:T(2,128)(2,1)} %get-tuple-element.43.refs_0_), channel_id=1, source_target_pairs={{0,4},{1,5},{2,6},{3,7},{4,0},{5,1},{6,2},{7,3},{8,12},{9,13},{10,... | collective-permute-start | bytes 196616 | tf_op jit(solution)/shard_map/ppermute | solution.py:422
  23.3 6.6 %collective-permute-start.5 = (bf16[2,2,8192]{2,1,0:T(2,128)(2,1)}, bf16[2,2,8192]{2,1,0:T(2,128)(2,1)S(1)}, u32[]{:S(2)}, u32[]{:S(2)}) collective-permute-start(bf16[2,2,8192]{2,1,0:T(2,128)(2,1)} %get-tuple-element.41), channel_id=1, source_target_pairs={{0,68},{1,69},{2,70},{3,71},{4,64},{5,65},{6,66},{7,67},{8,76},{9,... | collective-permute-start | bytes 196616 | tf_op jit(solution)/shard_map/ppermute | solution.py:422
  23.3 6.6 %collective-permute-start.4 = (bf16[2,2,8192]{2,1,0:T(2,128)(2,1)}, bf16[2,2,8192]{2,1,0:T(2,128)(2,1)S(1)}, u32[]{:S(2)}, u32[]{:S(2)}) collective-permute-start(bf16[2,2,8192]{2,1,0:T(2,128)(2,1)} %get-tuple-element.41), channel_id=1, source_target_pairs={{0,64},{1,65},{2,66},{3,67},{4,68},{5,69},{6,70},{7,71},{8,72},{9,... | collective-permute-start | bytes 196616 | tf_op jit(solution)/shard_map/ppermute | solution.py:422
  29.9 17.4 %collective-permute-start.10 = (bf16[8192,128]{1,0:T(8,128)(2,1)}, bf16[8192,128]{1,0:T(8,128)(2,1)S(1)}, u32[]{:S(2)}, u32[]{:S(2)}) collective-permute-start(bf16[8192,128]{1,0:T(8,128)(2,1)} %get-tuple-element.42.refs_1_), channel_id=1, source_target_pairs={{0,32},{1,33},{2,34},{3,35},{4,36},{5,37},{6,38},{7,39},{8,40},{9,... | collective-permute-start | bytes 6291464 | tf_op jit(solution)/shard_map/ppermute | solution.py:422
  30.7 23.8 %collective-permute-start.12 = (bf16[3584,128]{1,0:T(8,128)(2,1)}, bf16[3584,128]{1,0:T(8,128)(2,1)}, u32[]{:S(2)}, u32[]{:S(2)}) collective-permute-start(bf16[3584,128]{1,0:T(8,128)(2,1)} %get-tuple-element.51), channel_id=1, source_target_pairs={{0,64},{1,65},{2,66},{3,67},{4,68},{5,69},{6,70},{7,71},{8,72},{9,... | collective-permute-start | bytes 2752520 | tf_op jit(solution)/shard_map/ppermute | solution.py:422
  32.4 0.8 copy-start.2
  33.4 1.4 %collective-permute-start.6 = (bf16[8,8192]{1,0:T(8,128)(2,1)S(1)}, bf16[8,8192]{1,0:T(8,128)(2,1)S(1)}, u32[]{:S(2)}, u32[]{:S(2)}) collective-permute-start(bf16[8,8192]{1,0:T(8,128)(2,1)S(1)} %get-tuple-element.48), channel_id=1, source_target_pairs={{0,32},{1,33},{2,34},{3,35},{4,36},{5,37},{6,38},{7,39},{8,40},{9,... | collective-permute-start | bytes 393224 | tf_op jit(solution)/shard_map/ppermute | solution.py:422
  34.8 6.1 %collective-permute-start.9 = (bf16[16,8192]{1,0:T(8,128)(2,1)S(1)}, bf16[16,8192]{1,0:T(8,128)(2,1)S(1)}, u32[]{:S(2)}, u32[]{:S(2)}) collective-permute-start(bf16[16,8192]{1,0:T(8,128)(2,1)S(1)} %join_cores.1.pa), channel_id=1, source_target_pairs={{0,3},{1,0},{2,1},{3,2},{4,7},{5,4},{6,5},{7,6},{8,11},{9,8},{10,9... | collective-permute-start | bytes 786440 | tf_op jit(solution)/shard_map/ppermute | solution.py:422
  37.6 9.6 %collective-permute-start.8 = (bf16[16,8192]{1,0:T(8,128)(2,1)S(1)}, bf16[16,8192]{1,0:T(8,128)(2,1)S(1)}, u32[]{:S(2)}, u32[]{:S(2)}) collective-permute-start(bf16[16,8192]{1,0:T(8,128)(2,1)S(1)} %join_cores.1.pa), channel_id=1, source_target_pairs={{0,1},{1,2},{2,3},{3,0},{4,5},{5,6},{6,7},{7,4},{8,9},{9,10},{10,1... | collective-permute-start | bytes 786440 | tf_op jit(solution)/shard_map/ppermute | solution.py:422
  37.6 9.6 %collective-permute-start.7 = (bf16[16,8192]{1,0:T(8,128)(2,1)S(1)}, bf16[16,8192]{1,0:T(8,128)(2,1)S(1)}, u32[]{:S(2)}, u32[]{:S(2)}) collective-permute-start(bf16[16,8192]{1,0:T(8,128)(2,1)S(1)} %join_cores.1.pa), channel_id=1, source_target_pairs={{0,2},{1,3},{2,0},{3,1},{4,6},{5,7},{6,4},{7,5},{8,10},{9,11},{10,... | collective-permute-start | bytes 786440 | tf_op jit(solution)/shard_map/ppermute | solution.py:422
  40.9 38.8 %collective-permute-start.11 = (bf16[4608,128]{1,0:T(8,128)(2,1)}, bf16[4608,128]{1,0:T(8,128)(2,1)}, u32[]{:S(2)}, u32[]{:S(2)}) collective-permute-start(bf16[4608,128]{1,0:T(8,128)(2,1)} %get-tuple-element.50), channel_id=1, source_target_pairs={{0,64},{1,65},{2,66},{3,67},{4,68},{5,69},{6,70},{7,71},{8,72},{9,... | collective-permute-start | bytes 3538952 | tf_op jit(solution)/shard_map/ppermute | solution.py:422
  47.3 19.1 %copy-start.3 = (bf16[8192,128]{1,0:T(8,128)(2,1)}, bf16[8192,128]{1,0:T(8,128)(2,1)S(1)}, u32[]{:S(2)}) copy-start(bf16[8192,128]{1,0:T(8,128)(2,1)S(1)} %collective-permute-done.10.refs_2_) | copy-start | bytes 6291460
  47.4 19.0 %copy-start.1 = (bf16[64,3584]{1,0:T(8,128)(2,1)}, bf16[64,3584]{1,0:T(8,128)(2,1)S(1)}, u32[]{:S(2)}) copy-start(bf16[64,3584]{1,0:T(8,128)(2,1)S(1)} %get-tuple-element.58.refs_5_) | copy-start | bytes 1376260
  47.4 31.9 %copy-start = (bf16[64,4608]{1,0:T(8,128)(2,1)}, bf16[64,4608]{1,0:T(8,128)(2,1)S(1)}, u32[]{:S(2)}) copy-start(bf16[64,4608]{1,0:T(8,128)(2,1)S(1)} %get-tuple-element.64.refs_5_) | copy-start | bytes 1769476
  47.4 12.9 %collective-permute-start.16 = (bf16[64,3584]{1,0:T(8,128)(2,1)S(1)}, bf16[64,3584]{1,0:T(8,128)(2,1)S(1)}, u32[]{:S(2)}, u32[]{:S(2)}) collective-permute-start(bf16[64,3584]{1,0:T(8,128)(2,1)S(1)} %get-tuple-element.58.refs_5_), channel_id=1, source_target_pairs={{0,24},{1,25},{2,26},{3,27},{4,28},{5,29},{6,30},{7,31},{8,0},{9,1... | collective-permute-start | bytes 1376264 | tf_op jit(solution)/shard_map/ppermute | solution.py:422
  49.9 13.9 %collective-permute-start.15 = (bf16[64,3584]{1,0:T(8,128)(2,1)S(1)}, bf16[64,3584]{1,0:T(8,128)(2,1)S(1)}, u32[]{:S(2)}, u32[]{:S(2)}) collective-permute-start(bf16[64,3584]{1,0:T(8,128)(2,1)S(1)} %get-tuple-element.58.refs_5_), channel_id=1, source_target_pairs={{0,8},{1,9},{2,10},{3,11},{4,12},{5,13},{6,14},{7,15},{8,16},{9,17... | collective-permute-start | bytes 1376264 | tf_op jit(solution)/shard_map/ppermute | solution.py:422
  49.9 13.9 %collective-permute-start.14 = (bf16[64,3584]{1,0:T(8,128)(2,1)S(1)}, bf16[64,3584]{1,0:T(8,128)(2,1)S(1)}, u32[]{:S(2)}, u32[]{:S(2)}) collective-permute-start(bf16[64,3584]{1,0:T(8,128)(2,1)S(1)} %get-tuple-element.58.refs_5_), channel_id=1, source_target_pairs={{0,16},{1,17},{2,18},{3,19},{4,20},{5,21},{6,22},{7,23},{8,24},{9,... | collective-permute-start | bytes 1376264 | tf_op jit(solution)/shard_map/ppermute | solution.py:422
  54.5 11.9 %collective-permute-start.13 = (bf16[3584,128]{1,0:T(8,128)(2,1)}, bf16[3584,128]{1,0:T(8,128)(2,1)}, u32[]{:S(2)}, u32[]{:S(2)}) collective-permute-start(bf16[3584,128]{1,0:T(8,128)(2,1)} %collective-permute-done.12.refs_3_), channel_id=1, source_target_pairs={{0,32},{1,33},{2,34},{3,35},{4,36},{5,37},{6,38},{7,39},{8,40},{9,... | collective-permute-start | bytes 2752520 | tf_op jit(solution)/shard_map/ppermute | solution.py:422
  60.3 3.6 %copy-start.5 = (bf16[64,3584]{1,0:T(8,128)(2,1)}, bf16[64,3584]{1,0:T(8,128)(2,1)S(1)}, u32[]{:S(2)}) copy-start(bf16[64,3584]{1,0:T(8,128)(2,1)S(1)} %collective-permute-done.16.refs_8_) | copy-start | bytes 1376260
  63.8 1.5 %copy-start.6 = (bf16[64,3584]{1,0:T(8,128)(2,1)}, bf16[64,3584]{1,0:T(8,128)(2,1)S(1)}, u32[]{:S(2)}) copy-start(bf16[64,3584]{1,0:T(8,128)(2,1)S(1)} %collective-permute-done.15.refs_7_) | copy-start | bytes 1376260
  63.8 1.5 %copy-start.7 = (bf16[64,3584]{1,0:T(8,128)(2,1)}, bf16[64,3584]{1,0:T(8,128)(2,1)S(1)}, u32[]{:S(2)}) copy-start(bf16[64,3584]{1,0:T(8,128)(2,1)S(1)} %collective-permute-done.14.refs_6_) | copy-start | bytes 1376260
  63.8 16.0 %collective-permute-start.19 = (bf16[64,4608]{1,0:T(8,128)(2,1)S(1)}, bf16[64,4608]{1,0:T(8,128)(2,1)}, u32[]{:S(2)}, u32[]{:S(2)}) collective-permute-start(bf16[64,4608]{1,0:T(8,128)(2,1)S(1)} %get-tuple-element.64.refs_5_), channel_id=1, source_target_pairs={{0,24},{1,25},{2,26},{3,27},{4,28},{5,29},{6,30},{7,31},{8,0},{9,1... | collective-permute-start | bytes 1769480 | tf_op jit(solution)/shard_map/ppermute | solution.py:422
  63.9 16.7 %collective-permute-start.18 = (bf16[64,4608]{1,0:T(8,128)(2,1)S(1)}, bf16[64,4608]{1,0:T(8,128)(2,1)}, u32[]{:S(2)}, u32[]{:S(2)}) collective-permute-start(bf16[64,4608]{1,0:T(8,128)(2,1)S(1)} %get-tuple-element.64.refs_5_), channel_id=1, source_target_pairs={{0,8},{1,9},{2,10},{3,11},{4,12},{5,13},{6,14},{7,15},{8,16},{9,17... | collective-permute-start | bytes 1769480 | tf_op jit(solution)/shard_map/ppermute | solution.py:422
  65.3 15.3 %collective-permute-start.17 = (bf16[64,4608]{1,0:T(8,128)(2,1)S(1)}, bf16[64,4608]{1,0:T(8,128)(2,1)}, u32[]{:S(2)}, u32[]{:S(2)}) collective-permute-start(bf16[64,4608]{1,0:T(8,128)(2,1)S(1)} %get-tuple-element.64.refs_5_), channel_id=1, source_target_pairs={{0,16},{1,17},{2,18},{3,19},{4,20},{5,21},{6,22},{7,23},{8,24},{9,... | collective-permute-start | bytes 1769480 | tf_op jit(solution)/shard_map/ppermute | solution.py:422
  80.6 5.9 %collective-permute-start.20 = (bf16[4608,128]{1,0:T(8,128)(2,1)}, bf16[4608,128]{1,0:T(8,128)(2,1)S(1)}, u32[]{:S(2)}, u32[]{:S(2)}) collective-permute-start(bf16[4608,128]{1,0:T(8,128)(2,1)} %collective-permute-done.11.refs_3_), channel_id=1, source_target_pairs={{0,32},{1,33},{2,34},{3,35},{4,36},{5,37},{6,38},{7,39},{8,40},{9,... | collective-permute-start | bytes 3538952 | tf_op jit(solution)/shard_map/ppermute | solution.py:422
  86.5 1.1 %copy-start.4 = (bf16[4608,128]{1,0:T(8,128)(2,1)}, bf16[4608,128]{1,0:T(8,128)(2,1)S(1)}, u32[]{:S(2)}) copy-start(bf16[4608,128]{1,0:T(8,128)(2,1)S(1)} %collective-permute-done.20.refs_4_) | copy-start | bytes 3538948

commit v9 on v8

--- a/solution.py
+++ b/solution.py
@@ -46,7 +46,7 @@
 
 
 DBLK = 25
-CHUNKS = (448, 576)
+CHUNKS = (384, 640)
 
 
 def spectra_kernel(
@@ -231,7 +231,7 @@
 
 
 UNROLL = 8
-HEAD = 64
+HEAD = 128
 
 
 def correlate_kernel(first, last, kc, offset, *refs):

time: 105 us -> 106 us (level)
  waiting for transfers between devices: 30.5 us -> 31.7 us
    ppermute x21, waiting for transfers between devices: 30.5 us -> 31.7 us  [send(): return lax.ppermute(value, AXES, permutation(move))]
  transfers between devices with their start and end apart: 21 -> 21, of which waited for: 13 -> 13; matrix products, arithmetic and copies ran while one was open for 1% -> 1% of each run, Pallas kernels for 13% -> 11%
where the time goes in v9:
time: 106 us
  Pallas kernels  40.9 us (39%)
  waiting for transfers between devices  31.7 us (30%)
  starting transfers between devices  28.5 us (27%)
  local copies, waits for them, and re-layouts  3.16 us (3%)
  other arithmetic  1.25 us (1%)
    ppermute x21, waiting for transfers between devices, send(): return lax.ppermute(value, AXES, permutation(move))  31.7 us
    pallas_call x2, Pallas kernels, correlate(): pl.pallas_call(functools.partial(correlate_kernel, first, last, kc, offse...  28.6 us
    ppermute x21, starting transfers between devices, send(): return lax.ppermute(value, AXES, permutation(move))  28.5 us
    pallas_call x1, Pallas kernels, spectra(): pl.pallas_call(functools.partial(spectra_kernel, half), out_shape=[jax.Sh...  12.1 us
    unnamed x22, local copies, waits for them, and re-layouts  3.16 us
  transfers between devices with their start and end apart: 21, of which 13 were waited for; matrix products, arithmetic and copies ran while one was open for 1% of the time, Pallas kernels for 11%

profile of v9, /device:TPU:1, one launch (start us, length us, event | category | flops | bytes accessed | tf_op | source)
XLA Modules:
  0.0 105.8 jit_solution(9485264113344707648)
XLA Ops:
  0.0 4.4 %collective-permute-start.1 = (s32[64]{0:T(128)}, s32[64]{0:T(128)S(1)}, u32[]{:S(2)}, u32[]{:S(2)}) collective-permute-start(s32[64]{0:T(128)} %ia.1), channel_id=1, source_target_pairs={{0,64},{1,65},{2,66},{3,67},{4,68},{5,69},{6,70},{7,71},{8,72},{9,... | collective-permute-start | bytes 776 | tf_op jit(solution)/shard_map/ppermute | solution.py:422
  4.4 1.0 collective-permute-start
  5.4 0.0 collective-permute-start.2
  5.4 0.6 pad_add_fusion.me_ref
  6.0 0.0 collective-permute-done.1.ic
  6.0 0.3 collective-permute-done.ib
  6.3 3.6 %collective-permute-done.2.id_ = s32[64]{0:T(128)S(1)} collective-permute-done((s32[64]{0:T(128)}, s32[64]{0:T(128)S(1)}, u32[]{:S(2)}, u32[]{:S(2)}) %collective-permute-start.2) | collective-permute-done | bytes 288 | tf_op jit(solution)/shard_map/ppermute | solution.py:422
  10.0 0.5 copy-done.10
  10.5 12.1 %spectra.1 = (bf16[3072,128]{1,0:T(8,128)(2,1)}, bf16[5120,128]{1,0:T(8,128)(2,1)}, bf16[8192,128]{1,0:T(8,128)(2,1)}, bf16[2,2,8192]{2,1,0:T(2,128)(2,1)}, bf16[2,2,8192]{2,1,0:T(2,128)(2,1)}) custom-call(s32[2]{0:T(128)} %pad_add_fusion.me_ref, s32[64]{0:T(128)} %ia.1, s32[64]{0:T(128)} %copy-done.9, s32[64]{0:T(128)} %copy-done.8, s32[64]{0:T(128)} %copy-done.10, ...), custom_call_target="tpu_custom_call" | custom-call | flops 1100000 | bytes 1024 | tf_op jit(solution)/shard_map/spectra/pallas_call | solution.py:166
  22.6 0.8 collective-permute-start.3
  23.4 2.5 %collective-permute-start.4 = (bf16[2,2,8192]{2,1,0:T(2,128)(2,1)}, bf16[2,2,8192]{2,1,0:T(2,128)(2,1)S(1)}, u32[]{:S(2)}, u32[]{:S(2)}) collective-permute-start(bf16[2,2,8192]{2,1,0:T(2,128)(2,1)} %get-tuple-element.41), channel_id=1, source_target_pairs={{0,64},{1,65},{2,66},{3,67},{4,68},{5,69},{6,70},{7,71},{8,72},{9,... | collective-permute-start | bytes 196616 | tf_op jit(solution)/shard_map/ppermute | solution.py:422
  25.9 0.7 collective-permute-done.3.refs_1_
  26.6 3.4 %collective-permute-done.5.refs_3_ = bf16[2,2,8192]{2,1,0:T(2,128)(2,1)S(1)} collective-permute-done((bf16[2,2,8192]{2,1,0:T(2,128)(2,1)}, bf16[2,2,8192]{2,1,0:T(2,128)(2,1)S(1)}, u32[]{:S(2)}, u32[]{:S(2)}) %collective-permute-start.5) | collective-permute-done | bytes 65568 | tf_op jit(solution)/shard_map/ppermute | solution.py:422
  30.0 0.8 collective-permute-start.10
  30.7 0.8 copy-done.2
  31.6 0.1 join_column.1
  31.7 0.1 collective-permute-start.6
  31.8 1.8 %collective-permute-start.12 = (bf16[3072,128]{1,0:T(8,128)(2,1)}, bf16[3072,128]{1,0:T(8,128)(2,1)}, u32[]{:S(2)}, u32[]{:S(2)}) collective-permute-start(bf16[3072,128]{1,0:T(8,128)(2,1)} %get-tuple-element.51), channel_id=1, source_target_pairs={{0,64},{1,65},{2,66},{3,67},{4,68},{5,69},{6,70},{7,71},{8,72},{9,... | collective-permute-start | bytes 2359304 | tf_op jit(solution)/shard_map/ppermute | solution.py:422
  33.6 1.1 %collective-permute-done.6.refs_1_ = bf16[8,8192]{1,0:T(8,128)(2,1)S(1)} collective-permute-done((bf16[8,8192]{1,0:T(8,128)(2,1)S(1)}, bf16[8,8192]{1,0:T(8,128)(2,1)S(1)}, u32[]{:S(2)}, u32[]{:S(2)}) %collective-permute-start.6) | collective-permute-done | bytes 131104 | tf_op jit(solution)/shard_map/ppermute | solution.py:422
  34.7 2.8 %collective-permute-start.9 = (bf16[16,8192]{1,0:T(8,128)(2,1)S(1)}, bf16[16,8192]{1,0:T(8,128)(2,1)S(1)}, u32[]{:S(2)}, u32[]{:S(2)}) collective-permute-start(bf16[16,8192]{1,0:T(8,128)(2,1)S(1)} %join_cores.1.pa), channel_id=1, source_target_pairs={{0,3},{1,0},{2,1},{3,2},{4,7},{5,4},{6,5},{7,6},{8,11},{9,8},{10,9... | collective-permute-start | bytes 786440 | tf_op jit(solution)/shard_map/ppermute | solution.py:422
  37.5 0.0 collective-permute-start.8
  37.5 1.6 %collective-permute-start.7 = (bf16[16,8192]{1,0:T(8,128)(2,1)S(1)}, bf16[16,8192]{1,0:T(8,128)(2,1)S(1)}, u32[]{:S(2)}, u32[]{:S(2)}) collective-permute-start(bf16[16,8192]{1,0:T(8,128)(2,1)S(1)} %join_cores.1.pa), channel_id=1, source_target_pairs={{0,2},{1,3},{2,0},{3,1},{4,6},{5,7},{6,4},{7,5},{8,10},{9,11},{10,... | collective-permute-start | bytes 786440 | tf_op jit(solution)/shard_map/ppermute | solution.py:422
  39.2 1.7 %collective-permute-done.9.pd = bf16[16,8192]{1,0:T(8,128)(2,1)S(1)} collective-permute-done((bf16[16,8192]{1,0:T(8,128)(2,1)S(1)}, bf16[16,8192]{1,0:T(8,128)(2,1)S(1)}, u32[]{:S(2)}, u32[]{:S(2)}) %collective-permute-start.9) | collective-permute-done | bytes 262176 | tf_op jit(solution)/shard_map/ppermute | solution.py:422
  40.8 1.7 %collective-permute-start.11 = (bf16[5120,128]{1,0:T(8,128)(2,1)}, bf16[5120,128]{1,0:T(8,128)(2,1)}, u32[]{:S(2)}, u32[]{:S(2)}) collective-permute-start(bf16[5120,128]{1,0:T(8,128)(2,1)} %get-tuple-element.50), channel_id=1, source_target_pairs={{0,64},{1,65},{2,66},{3,67},{4,68},{5,69},{6,70},{7,71},{8,72},{9,... | collective-permute-start | bytes 3932168 | tf_op jit(solution)/shard_map/ppermute | solution.py:422
  42.6 4.6 %collective-permute-done.8.pc = bf16[16,8192]{1,0:T(8,128)(2,1)S(1)} collective-permute-done((bf16[16,8192]{1,0:T(8,128)(2,1)S(1)}, bf16[16,8192]{1,0:T(8,128)(2,1)S(1)}, u32[]{:S(2)}, u32[]{:S(2)}) %collective-permute-start.8) | collective-permute-done | bytes 262176 | tf_op jit(solution)/shard_map/ppermute | solution.py:422
  47.2 0.0 collective-permute-done.7.pb
  47.2 0.1 split.1
  47.3 2.5 %collective-permute-start.16 = (bf16[64,3072]{1,0:T(8,128)(2,1)S(1)}, bf16[64,3072]{1,0:T(8,128)(2,1)S(1)}, u32[]{:S(2)}, u32[]{:S(2)}) collective-permute-start(bf16[64,3072]{1,0:T(8,128)(2,1)S(1)} %get-tuple-element.58.refs_5_), channel_id=1, source_target_pairs={{0,24},{1,25},{2,26},{3,27},{4,28},{5,29},{6,30},{7,31},{8,0},{9,1... | collective-permute-start | bytes 1179656 | tf_op jit(solution)/shard_map/ppermute | solution.py:422
  49.8 1.7 %collective-permute-start.14 = (bf16[64,3072]{1,0:T(8,128)(2,1)S(1)}, bf16[64,3072]{1,0:T(8,128)(2,1)S(1)}, u32[]{:S(2)}, u32[]{:S(2)}) collective-permute-start(bf16[64,3072]{1,0:T(8,128)(2,1)S(1)} %get-tuple-element.58.refs_5_), channel_id=1, source_target_pairs={{0,16},{1,17},{2,18},{3,19},{4,20},{5,21},{6,22},{7,23},{8,24},{9,... | collective-permute-start | bytes 1179656 | tf_op jit(solution)/shard_map/ppermute | solution.py:422
  51.6 0.8 collective-permute-done.12.refs_3_
  52.4 2.1 %collective-permute-start.13 = (bf16[3072,128]{1,0:T(8,128)(2,1)}, bf16[3072,128]{1,0:T(8,128)(2,1)}, u32[]{:S(2)}, u32[]{:S(2)}) collective-permute-start(bf16[3072,128]{1,0:T(8,128)(2,1)} %collective-permute-done.12.refs_3_), channel_id=1, source_target_pairs={{0,32},{1,33},{2,34},{3,35},{4,36},{5,37},{6,38},{7,39},{8,40},{9,... | collective-permute-start | bytes 2359304 | tf_op jit(solution)/shard_map/ppermute | solution.py:422
  54.5 4.2 %collective-permute-done.16.refs_8_ = bf16[64,3072]{1,0:T(8,128)(2,1)S(1)} collective-permute-done((bf16[64,3072]{1,0:T(8,128)(2,1)S(1)}, bf16[64,3072]{1,0:T(8,128)(2,1)S(1)}, u32[]{:S(2)}, u32[]{:S(2)}) %collective-permute-start.16) | collective-permute-done | bytes 393248 | tf_op jit(solution)/shard_map/ppermute | solution.py:422
  58.8 3.5 %collective-permute-done.15.refs_7_ = bf16[64,3072]{1,0:T(8,128)(2,1)S(1)} collective-permute-done((bf16[64,3072]{1,0:T(8,128)(2,1)S(1)}, bf16[64,3072]{1,0:T(8,128)(2,1)S(1)}, u32[]{:S(2)}, u32[]{:S(2)}) %collective-permute-start.15) | collective-permute-done | bytes 393248 | tf_op jit(solution)/shard_map/ppermute | solution.py:422
  62.3 0.0 collective-permute-done.14.refs_6_
  62.3 0.1 collective-permute-start.19
  62.4 0.7 copy-done.6
  63.0 0.8 collective-permute-start.18
  63.8 0.4 collective-permute-start.17
  64.3 0.6 fusion.refs_0_
  64.9 0.0 collective-permute-done.13.refs_4_
  64.9 11.4 %correlate_first.1.refs_11_ = f32[64,208,128]{2,1,0:T(8,128)} custom-call(s32[64]{0:T(128)} %fusion.refs_0_, bf16[8192,128]{1,0:T(8,128)(2,1)} %get-tuple-element.42.refs_1_, bf16[8192,128]{1,0:T(8,128)(2,1)} %copy-done.3, bf16[3072,128]{1,0:T(8,128)(2,1)} %collective-permute-done.12.refs_3_, bf16[3072,128]{1,0:T(8,128)(2,1)} %collective-permute-done.13.refs_4_, ...), custom_call_target="tpu_custom_call" | custom-call | flops 1100000 | bytes 1024 | tf_op jit(solution)/shard_map/correlate_first/pallas_call | solution.py:396
  76.3 4.2 %collective-permute-done.11.refs_3_ = bf16[5120,128]{1,0:T(8,128)(2,1)} collective-permute-done((bf16[5120,128]{1,0:T(8,128)(2,1)}, bf16[5120,128]{1,0:T(8,128)(2,1)}, u32[]{:S(2)}, u32[]{:S(2)}) %collective-permute-start.11) | collective-permute-done | bytes 1310752 | tf_op jit(solution)/shard_map/ppermute | solution.py:422
  80.5 0.0 collective-permute-done.19.refs_8_
  80.5 0.6 collective-permute-done.18.refs_7_
  81.1 3.3 %collective-permute-start.20 = (bf16[5120,128]{1,0:T(8,128)(2,1)}, bf16[5120,128]{1,0:T(8,128)(2,1)S(1)}, u32[]{:S(2)}, u32[]{:S(2)}) collective-permute-start(bf16[5120,128]{1,0:T(8,128)(2,1)} %collective-permute-done.11.refs_3_), channel_id=1, source_target_pairs={{0,32},{1,33},{2,34},{3,35},{4,36},{5,37},{6,38},{7,39},{8,40},{9,... | collective-permute-start | bytes 3932168 | tf_op jit(solution)/shard_map/ppermute | solution.py:422
  84.4 2.9 %collective-permute-done.20.refs_4_ = bf16[5120,128]{1,0:T(8,128)(2,1)S(1)} collective-permute-done((bf16[5120,128]{1,0:T(8,128)(2,1)}, bf16[5120,128]{1,0:T(8,128)(2,1)S(1)}, u32[]{:S(2)}, u32[]{:S(2)}) %collective-permute-start.20) | collective-permute-done | bytes 1310752 | tf_op jit(solution)/shard_map/ppermute | solution.py:422
  87.3 1.1 %copy-done.4 = bf16[5120,128]{1,0:T(8,128)(2,1)} copy-done((bf16[5120,128]{1,0:T(8,128)(2,1)}, bf16[5120,128]{1,0:T(8,128)(2,1)S(1)}, u32[]{:S(2)}) %copy-start.4) | copy-done | bytes 1310744
  88.4 17.2 %correlate_last.1 = f32[201,64,128]{2,1,0:T(8,128)} custom-call(s32[64]{0:T(128)} %fusion.refs_0_, bf16[8192,128]{1,0:T(8,128)(2,1)} %get-tuple-element.42.refs_1_, bf16[8192,128]{1,0:T(8,128)(2,1)} %copy-done.3, bf16[5120,128]{1,0:T(8,128)(2,1)} %collective-permute-done.11.refs_3_, bf16[5120,128]{1,0:T(8,128)(2,1)} %copy-done.4, bf16[64,5120]{1,0:T(8,128)(2,1)} %copy-done, ...), custom_call_target="tpu_custom_call" | custom-call | flops 1100000 | bytes 1024 | tf_op jit(solution)/shard_map/correlate_last/pallas_call | solution.py:396
  (24 shorter events, 0.1 us)
Async XLA Ops:
  0.0 6.0 %collective-permute-start.1 = (s32[64]{0:T(128)}, s32[64]{0:T(128)S(1)}, u32[]{:S(2)}, u32[]{:S(2)}) collective-permute-start(s32[64]{0:T(128)} %ia.1), channel_id=1, source_target_pairs={{0,64},{1,65},{2,66},{3,67},{4,68},{5,69},{6,70},{7,71},{8,72},{9,... | collective-permute-start | bytes 776 | tf_op jit(solution)/shard_map/ppermute | solution.py:422
  4.4 1.9 %collective-permute-start = (s32[64]{0:T(128)}, s32[64]{0:T(128)S(1)}, u32[]{:S(2)}, u32[]{:S(2)}) collective-permute-start(s32[64]{0:T(128)} %ia.1), channel_id=1, source_target_pairs={{0,32},{1,33},{2,34},{3,35},{4,36},{5,37},{6,38},{7,39},{8,40},{9,... | collective-permute-start | bytes 776 | tf_op jit(solution)/shard_map/ppermute | solution.py:422
  5.4 4.6 %collective-permute-start.2 = (s32[64]{0:T(128)}, s32[64]{0:T(128)S(1)}, u32[]{:S(2)}, u32[]{:S(2)}) collective-permute-start(s32[64]{0:T(128)} %ia.1), channel_id=1, source_target_pairs={{0,96},{1,97},{2,98},{3,99},{4,100},{5,101},{6,102},{7,103},{8,104... | collective-permute-start | bytes 776 | tf_op jit(solution)/shard_map/ppermute | solution.py:422
  6.0 4.0 %copy-start.8 = (s32[64]{0:T(128)}, s32[64]{0:T(128)S(1)}, u32[]{:S(2)}) copy-start(s32[64]{0:T(128)S(1)} %collective-permute-done.1.ic) | copy-start | bytes 772
  6.3 3.7 %copy-start.9 = (s32[64]{0:T(128)}, s32[64]{0:T(128)S(1)}, u32[]{:S(2)}) copy-start(s32[64]{0:T(128)S(1)} %collective-permute-done.ib) | copy-start | bytes 772
  10.0 0.5 copy-start.10
  22.6 4.0 %collective-permute-start.3 = (bf16[2,2,8192]{2,1,0:T(2,128)(2,1)}, bf16[2,2,8192]{2,1,0:T(2,128)(2,1)S(1)}, u32[]{:S(2)}, u32[]{:S(2)}) collective-permute-start(bf16[2,2,8192]{2,1,0:T(2,128)(2,1)} %get-tuple-element.43.refs_0_), channel_id=1, source_target_pairs={{0,4},{1,5},{2,6},{3,7},{4,0},{5,1},{6,2},{7,3},{8,12},{9,13},{10,... | collective-permute-start | bytes 196616 | tf_op jit(solution)/shard_map/ppermute | solution.py:422
  23.4 6.6 %collective-permute-start.5 = (bf16[2,2,8192]{2,1,0:T(2,128)(2,1)}, bf16[2,2,8192]{2,1,0:T(2,128)(2,1)S(1)}, u32[]{:S(2)}, u32[]{:S(2)}) collective-permute-start(bf16[2,2,8192]{2,1,0:T(2,128)(2,1)} %get-tuple-element.41), channel_id=1, source_target_pairs={{0,68},{1,69},{2,70},{3,71},{4,64},{5,65},{6,66},{7,67},{8,76},{9,... | collective-permute-start | bytes 196616 | tf_op jit(solution)/shard_map/ppermute | solution.py:422
  23.4 6.6 %collective-permute-start.4 = (bf16[2,2,8192]{2,1,0:T(2,128)(2,1)}, bf16[2,2,8192]{2,1,0:T(2,128)(2,1)S(1)}, u32[]{:S(2)}, u32[]{:S(2)}) collective-permute-start(bf16[2,2,8192]{2,1,0:T(2,128)(2,1)} %get-tuple-element.41), channel_id=1, source_target_pairs={{0,64},{1,65},{2,66},{3,67},{4,68},{5,69},{6,70},{7,71},{8,72},{9,... | collective-permute-start | bytes 196616 | tf_op jit(solution)/shard_map/ppermute | solution.py:422
  30.0 17.2 %collective-permute-start.10 = (bf16[8192,128]{1,0:T(8,128)(2,1)}, bf16[8192,128]{1,0:T(8,128)(2,1)S(1)}, u32[]{:S(2)}, u32[]{:S(2)}) collective-permute-start(bf16[8192,128]{1,0:T(8,128)(2,1)} %get-tuple-element.42.refs_1_), channel_id=1, source_target_pairs={{0,32},{1,33},{2,34},{3,35},{4,36},{5,37},{6,38},{7,39},{8,40},{9,... | collective-permute-start | bytes 6291464 | tf_op jit(solution)/shard_map/ppermute | solution.py:422
  30.7 0.8 copy-start.2
  31.7 3.0 %collective-permute-start.6 = (bf16[8,8192]{1,0:T(8,128)(2,1)S(1)}, bf16[8,8192]{1,0:T(8,128)(2,1)S(1)}, u32[]{:S(2)}, u32[]{:S(2)}) collective-permute-start(bf16[8,8192]{1,0:T(8,128)(2,1)S(1)} %get-tuple-element.48), channel_id=1, source_target_pairs={{0,32},{1,33},{2,34},{3,35},{4,36},{5,37},{6,38},{7,39},{8,40},{9,... | collective-permute-start | bytes 393224 | tf_op jit(solution)/shard_map/ppermute | solution.py:422
  31.8 20.6 %collective-permute-start.12 = (bf16[3072,128]{1,0:T(8,128)(2,1)}, bf16[3072,128]{1,0:T(8,128)(2,1)}, u32[]{:S(2)}, u32[]{:S(2)}) collective-permute-start(bf16[3072,128]{1,0:T(8,128)(2,1)} %get-tuple-element.51), channel_id=1, source_target_pairs={{0,64},{1,65},{2,66},{3,67},{4,68},{5,69},{6,70},{7,71},{8,72},{9,... | collective-permute-start | bytes 2359304 | tf_op jit(solution)/shard_map/ppermute | solution.py:422
  34.7 6.1 %collective-permute-start.9 = (bf16[16,8192]{1,0:T(8,128)(2,1)S(1)}, bf16[16,8192]{1,0:T(8,128)(2,1)S(1)}, u32[]{:S(2)}, u32[]{:S(2)}) collective-permute-start(bf16[16,8192]{1,0:T(8,128)(2,1)S(1)} %join_cores.1.pa), channel_id=1, source_target_pairs={{0,3},{1,0},{2,1},{3,2},{4,7},{5,4},{6,5},{7,6},{8,11},{9,8},{10,9... | collective-permute-start | bytes 786440 | tf_op jit(solution)/shard_map/ppermute | solution.py:422
  37.5 9.6 %collective-permute-start.8 = (bf16[16,8192]{1,0:T(8,128)(2,1)S(1)}, bf16[16,8192]{1,0:T(8,128)(2,1)S(1)}, u32[]{:S(2)}, u32[]{:S(2)}) collective-permute-start(bf16[16,8192]{1,0:T(8,128)(2,1)S(1)} %join_cores.1.pa), channel_id=1, source_target_pairs={{0,1},{1,2},{2,3},{3,0},{4,5},{5,6},{6,7},{7,4},{8,9},{9,10},{10,1... | collective-permute-start | bytes 786440 | tf_op jit(solution)/shard_map/ppermute | solution.py:422
  37.5 9.6 %collective-permute-start.7 = (bf16[16,8192]{1,0:T(8,128)(2,1)S(1)}, bf16[16,8192]{1,0:T(8,128)(2,1)S(1)}, u32[]{:S(2)}, u32[]{:S(2)}) collective-permute-start(bf16[16,8192]{1,0:T(8,128)(2,1)S(1)} %join_cores.1.pa), channel_id=1, source_target_pairs={{0,2},{1,3},{2,0},{3,1},{4,6},{5,7},{6,4},{7,5},{8,10},{9,11},{10,... | collective-permute-start | bytes 786440 | tf_op jit(solution)/shard_map/ppermute | solution.py:422
  40.8 39.7 %collective-permute-start.11 = (bf16[5120,128]{1,0:T(8,128)(2,1)}, bf16[5120,128]{1,0:T(8,128)(2,1)}, u32[]{:S(2)}, u32[]{:S(2)}) collective-permute-start(bf16[5120,128]{1,0:T(8,128)(2,1)} %get-tuple-element.50), channel_id=1, source_target_pairs={{0,64},{1,65},{2,66},{3,67},{4,68},{5,69},{6,70},{7,71},{8,72},{9,... | collective-permute-start | bytes 3932168 | tf_op jit(solution)/shard_map/ppermute | solution.py:422
  47.2 17.7 %copy-start.3 = (bf16[8192,128]{1,0:T(8,128)(2,1)}, bf16[8192,128]{1,0:T(8,128)(2,1)S(1)}, u32[]{:S(2)}) copy-start(bf16[8192,128]{1,0:T(8,128)(2,1)S(1)} %collective-permute-done.10.refs_2_) | copy-start | bytes 6291460
  47.3 17.6 %copy-start.1 = (bf16[64,3072]{1,0:T(8,128)(2,1)}, bf16[64,3072]{1,0:T(8,128)(2,1)S(1)}, u32[]{:S(2)}) copy-start(bf16[64,3072]{1,0:T(8,128)(2,1)S(1)} %get-tuple-element.58.refs_5_) | copy-start | bytes 1179652
  47.3 29.0 %copy-start = (bf16[64,5120]{1,0:T(8,128)(2,1)}, bf16[64,5120]{1,0:T(8,128)(2,1)S(1)}, u32[]{:S(2)}) copy-start(bf16[64,5120]{1,0:T(8,128)(2,1)S(1)} %get-tuple-element.64.refs_5_) | copy-start | bytes 1966084
  47.3 11.5 %collective-permute-start.16 = (bf16[64,3072]{1,0:T(8,128)(2,1)S(1)}, bf16[64,3072]{1,0:T(8,128)(2,1)S(1)}, u32[]{:S(2)}, u32[]{:S(2)}) collective-permute-start(bf16[64,3072]{1,0:T(8,128)(2,1)S(1)} %get-tuple-element.58.refs_5_), channel_id=1, source_target_pairs={{0,24},{1,25},{2,26},{3,27},{4,28},{5,29},{6,30},{7,31},{8,0},{9,1... | collective-permute-start | bytes 1179656 | tf_op jit(solution)/shard_map/ppermute | solution.py:422
  49.8 12.5 %collective-permute-start.15 = (bf16[64,3072]{1,0:T(8,128)(2,1)S(1)}, bf16[64,3072]{1,0:T(8,128)(2,1)S(1)}, u32[]{:S(2)}, u32[]{:S(2)}) collective-permute-start(bf16[64,3072]{1,0:T(8,128)(2,1)S(1)} %get-tuple-element.58.refs_5_), channel_id=1, source_target_pairs={{0,8},{1,9},{2,10},{3,11},{4,12},{5,13},{6,14},{7,15},{8,16},{9,17... | collective-permute-start | bytes 1179656 | tf_op jit(solution)/shard_map/ppermute | solution.py:422
  49.8 12.5 %collective-permute-start.14 = (bf16[64,3072]{1,0:T(8,128)(2,1)S(1)}, bf16[64,3072]{1,0:T(8,128)(2,1)S(1)}, u32[]{:S(2)}, u32[]{:S(2)}) collective-permute-start(bf16[64,3072]{1,0:T(8,128)(2,1)S(1)} %get-tuple-element.58.refs_5_), channel_id=1, source_target_pairs={{0,16},{1,17},{2,18},{3,19},{4,20},{5,21},{6,22},{7,23},{8,24},{9,... | collective-permute-start | bytes 1179656 | tf_op jit(solution)/shard_map/ppermute | solution.py:422
  52.4 12.5 %collective-permute-start.13 = (bf16[3072,128]{1,0:T(8,128)(2,1)}, bf16[3072,128]{1,0:T(8,128)(2,1)}, u32[]{:S(2)}, u32[]{:S(2)}) collective-permute-start(bf16[3072,128]{1,0:T(8,128)(2,1)} %collective-permute-done.12.refs_3_), channel_id=1, source_target_pairs={{0,32},{1,33},{2,34},{3,35},{4,36},{5,37},{6,38},{7,39},{8,40},{9,... | collective-permute-start | bytes 2359304 | tf_op jit(solution)/shard_map/ppermute | solution.py:422
  58.8 6.1 %copy-start.5 = (bf16[64,3072]{1,0:T(8,128)(2,1)}, bf16[64,3072]{1,0:T(8,128)(2,1)S(1)}, u32[]{:S(2)}) copy-start(bf16[64,3072]{1,0:T(8,128)(2,1)S(1)} %collective-permute-done.16.refs_8_) | copy-start | bytes 1179652
  62.3 0.8 copy-start.6
  62.3 1.5 %copy-start.7 = (bf16[64,3072]{1,0:T(8,128)(2,1)}, bf16[64,3072]{1,0:T(8,128)(2,1)S(1)}, u32[]{:S(2)}) copy-start(bf16[64,3072]{1,0:T(8,128)(2,1)S(1)} %collective-permute-done.14.refs_6_) | copy-start | bytes 1179652
  62.3 18.2 %collective-permute-start.19 = (bf16[64,5120]{1,0:T(8,128)(2,1)S(1)}, bf16[64,5120]{1,0:T(8,128)(2,1)}, u32[]{:S(2)}, u32[]{:S(2)}) collective-permute-start(bf16[64,5120]{1,0:T(8,128)(2,1)S(1)} %get-tuple-element.64.refs_5_), channel_id=1, source_target_pairs={{0,24},{1,25},{2,26},{3,27},{4,28},{5,29},{6,30},{7,31},{8,0},{9,1... | collective-permute-start | bytes 1966088 | tf_op jit(solution)/shard_map/ppermute | solution.py:422
  63.0 18.1 %collective-permute-start.18 = (bf16[64,5120]{1,0:T(8,128)(2,1)S(1)}, bf16[64,5120]{1,0:T(8,128)(2,1)}, u32[]{:S(2)}, u32[]{:S(2)}) collective-permute-start(bf16[64,5120]{1,0:T(8,128)(2,1)S(1)} %get-tuple-element.64.refs_5_), channel_id=1, source_target_pairs={{0,8},{1,9},{2,10},{3,11},{4,12},{5,13},{6,14},{7,15},{8,16},{9,17... | collective-permute-start | bytes 1966088 | tf_op jit(solution)/shard_map/ppermute | solution.py:422
  63.8 17.3 %collective-permute-start.17 = (bf16[64,5120]{1,0:T(8,128)(2,1)S(1)}, bf16[64,5120]{1,0:T(8,128)(2,1)}, u32[]{:S(2)}, u32[]{:S(2)}) collective-permute-start(bf16[64,5120]{1,0:T(8,128)(2,1)S(1)} %get-tuple-element.64.refs_5_), channel_id=1, source_target_pairs={{0,16},{1,17},{2,18},{3,19},{4,20},{5,21},{6,22},{7,23},{8,24},{9,... | collective-permute-start | bytes 1966088 | tf_op jit(solution)/shard_map/ppermute | solution.py:422
  81.1 6.2 %collective-permute-start.20 = (bf16[5120,128]{1,0:T(8,128)(2,1)}, bf16[5120,128]{1,0:T(8,128)(2,1)S(1)}, u32[]{:S(2)}, u32[]{:S(2)}) collective-permute-start(bf16[5120,128]{1,0:T(8,128)(2,1)} %collective-permute-done.11.refs_3_), channel_id=1, source_target_pairs={{0,32},{1,33},{2,34},{3,35},{4,36},{5,37},{6,38},{7,39},{8,40},{9,... | collective-permute-start | bytes 3932168 | tf_op jit(solution)/shard_map/ppermute | solution.py:422
  87.3 1.1 %copy-start.4 = (bf16[5120,128]{1,0:T(8,128)(2,1)}, bf16[5120,128]{1,0:T(8,128)(2,1)S(1)}, u32[]{:S(2)}) copy-start(bf16[5120,128]{1,0:T(8,128)(2,1)S(1)} %collective-permute-done.20.refs_4_) | copy-start | bytes 3932164
